TPU v7x, 32 devices: a whole 2x2x4 slice. The times are simulated.
32 devices in a mesh: dp: 8 (over z, core), member: 4 (over y, x).
Axes of the slice: x: 2, y: 2, z: 4, core: 2. Of those that a mesh axis runs over, the one named last changes fastest.
Arguments:
- tokens: bfloat16 [1024, 4096], P('dp', 'member'), may hold values from -6 to 6
- routes: int32 [1024, 2], P('dp'), may hold values from 0 to 7, all different within a row; in each aligned block of 128 rows (0 to 127, 128 to 255, ...) at most 34 rows name the same one
- route_weights: float32 [1024, 2], P('dp'), may hold values from 0.2 to 1
- up_stacked: bfloat16 [8, 4096, 7168], P(None, ('member', 'dp')), may hold values from -0.09375 to 0.09375
- down_stacked: bfloat16 [8, 4096, 7168], P(None, ('member', 'dp')), may hold values from -0.0625 to 0.0625
- cotangent: bfloat16 [1024, 4096], P('dp', 'member'), may hold values from -6 to 6
Outputs:
- mixed: bfloat16 [1024, 4096], P('dp', 'member')
- grad_tokens: bfloat16 [1024, 4096], P('dp', 'member')
- grad_up: bfloat16 [8, 4096, 7168], P('dp', 'member')
- grad_down: bfloat16 [8, 4096, 7168], P('dp', 'member')
Inputs may be any that keep to these rules, and one draw needn't show every extreme that they name: `routes`: each row names two different experts. In each aligned block of 128 rows no expert is named by more than 34 rows, and in some block some expert is named by exactly 34 rows.
All inputs are finite; a program needn't handle non-finite values.
Results may differ from a plain program's by a relative error of at most 0.018.
Values may be sent and summed in bfloat16 or wider, within the bound.
No kernel may reach another device: no remote copies, remote signals or barrier semaphores. Data moves between devices by JAX's collectives and lax.ppermute only.
A program may use at most 192 MiB of HBM per device.

v0:
```python
import jax
import jax.numpy as jnp
from jax import lax
from jax.sharding import PartitionSpec as P

FF_W = 7168
E = 8
CAP = 34


def contract(left, right, left_dim, right_dim):
    return lax.dot_general(
        left, right, (((left_dim,), (right_dim,)), ((), ())), preferred_element_type=jnp.float32
    )


def body(tokens, routes, route_weights, up_stacked, down_stacked, cotangent):
    dp_count = lax.axis_size("dp")
    member_count = lax.axis_size("member")
    quarters = dp_count // E
    share_rows = up_stacked.shape[1]
    features = tokens.shape[1]
    hidden_own = FF_W // quarters
    per_member = hidden_own // member_count
    slots_all = E * CAP
    up_parts = (
        up_stacked.reshape(E, share_rows, quarters, hidden_own)
        .transpose(0, 2, 1, 3)
        .reshape(dp_count, share_rows, hidden_own)
    )
    down_parts = (
        down_stacked.reshape(E, share_rows, quarters, hidden_own)
        .transpose(0, 2, 1, 3)
        .reshape(dp_count, share_rows, hidden_own)
    )
    up_own, down_own = (
        lax.all_to_all(up_parts, "dp", split_axis=0, concat_axis=1, tiled=True),
        lax.all_to_all(down_parts, "dp", split_axis=0, concat_axis=1, tiled=True),
    )
    up_own = up_own.reshape(dp_count * share_rows, hidden_own)
    down_own = down_own.reshape(dp_count * share_rows, hidden_own)
    chosen = (routes[:, :, None] == jnp.arange(E, dtype=jnp.int32)[None, None, :]).astype(jnp.int32)
    flat_hits = chosen.reshape(-1, E)
    before = jnp.cumsum(flat_hits, axis=0) - flat_hits
    slot_pos = jnp.sum(before * flat_hits, axis=1).reshape(-1, 2)
    target = routes * CAP + slot_pos
    slot_hits = jnp.arange(slots_all, dtype=jnp.int32)[:, None, None] == target[None, :, :]
    pick_table = jnp.sum(slot_hits.astype(jnp.float32), axis=2)
    weighted = jnp.sum(jnp.where(slot_hits, route_weights[None, :, :], 0.0), axis=2)
    x_local = jnp.dot(
        pick_table.astype(jnp.bfloat16), tokens, preferred_element_type=jnp.float32
    ).astype(jnp.bfloat16)
    d_local = jnp.dot(
        weighted, cotangent.astype(jnp.float32), precision=lax.Precision.HIGHEST
    ).astype(jnp.bfloat16)

    def spread(local):
        return jnp.broadcast_to(
            local.reshape(E, 1, CAP, features), (E, quarters, CAP, features)
        ).reshape(dp_count, CAP, features)

    def collect(returned):
        return jnp.sum(returned.reshape(E, quarters, CAP, features), axis=1).reshape(
            slots_all, features
        )

    x_in = lax.all_to_all(spread(x_local), "dp", split_axis=0, concat_axis=0, tiled=True).reshape(
        dp_count * CAP, features
    )
    partial_value = jnp.dot(x_in, up_own, preferred_element_type=jnp.float32).astype(jnp.bfloat16)
    pre_full = lax.psum(partial_value, "member").astype(jnp.float32)
    act_full = jax.nn.silu(pre_full).astype(jnp.bfloat16)
    y_part = contract(act_full, down_own, 1, 1)
    y_part, pre_full, act_full = (y_part, pre_full, act_full)
    y_back = lax.all_to_all(
        y_part.reshape(dp_count, CAP, features).astype(jnp.bfloat16),
        "dp",
        split_axis=0,
        concat_axis=0,
        tiled=True,
    ).astype(jnp.float32)
    d_in = lax.all_to_all(spread(d_local), "dp", split_axis=0, concat_axis=0, tiled=True).reshape(
        dp_count * CAP, features
    )
    d_act = lax.psum_scatter(
        contract(down_own, d_in, 0, 1).astype(jnp.bfloat16),
        "member",
        scatter_dimension=0,
        tiled=True,
    ).astype(jnp.float32)
    own_start = lax.axis_index("member") * per_member
    pre_share = lax.dynamic_slice_in_dim(pre_full, own_start, per_member, 1).T
    sigma = jax.nn.sigmoid(pre_share)
    d_share = (d_act * sigma * (1.0 + pre_share * (1.0 - sigma))).astype(jnp.bfloat16)
    d_pre = lax.all_gather(d_share, "member", axis=0, tiled=True)
    g_down = contract(d_in, act_full, 0, 0)
    g_up = contract(x_in, d_pre, 0, 1)
    dx_part = contract(d_pre, up_own, 0, 1)
    dx_part, g_up, g_down = (dx_part, g_up, g_down)
    dx_back = lax.all_to_all(
        dx_part.reshape(dp_count, CAP, features).astype(jnp.bfloat16),
        "dp",
        split_axis=0,
        concat_axis=0,
        tiled=True,
    ).astype(jnp.float32)
    y_slots = collect(y_back)
    dx_slots = collect(dx_back)
    mixed = jnp.dot(weighted.T, y_slots, precision=lax.Precision.HIGHEST).astype(jnp.bfloat16)
    grad_tokens = jnp.dot(pick_table.T, dx_slots, precision=lax.Precision.HIGHEST).astype(
        jnp.bfloat16
    )
    grad_up = g_up.astype(jnp.bfloat16).reshape(1, features, hidden_own)
    grad_down = g_down.astype(jnp.bfloat16).reshape(1, features, hidden_own)
    return (mixed, grad_tokens, grad_up, grad_down)


def solution(mesh):
    placed = (
        P("dp", "member"),
        P("dp", None),
        P("dp", None),
        P(None, ("member", "dp"), None),
        P(None, ("member", "dp"), None),
        P("dp", "member"),
    )
    return jax.shard_map(
        body,
        mesh=mesh,
        in_specs=placed,
        out_specs=(
            P("dp", "member"),
            P("dp", "member"),
            P("dp", "member", None),
            P("dp", "member", None),
        ),
        check_vma=False,
    )
```

profile of v0, /device:TPU:0, one launch (start us, length us, event | category | flops | bytes accessed | tf_op | source)
XLA Modules:
  0.0 869.8 jit_solution(2469178723526900404)
XLA Ops:
  12.2 6.4 all-to-all-start
  18.6 1.5 convolution_convert_fusion.4
  20.3 16.4 %all-to-all-done = bf16[8,34,1024]{2,1,0:T(8,128)(2,1)S(1)} async-done(((bf16[8,34,1024]{2,1,0:T(8,128)(2,1)}), bf16[8,34,1024]{2,1,0:T(8,128)(2,1)S(1)}, u32[]{:S(2)}, u32[]{:S(2)}) %all-to-all-start) | async-done | bytes 557088 | tf_op jit(solution)/shard_map/all_to_all | solution.py:67
  36.7 20.5 %all_to_all.38 = bf16[8,34,1024]{2,1,0:T(8,128)(2,1)S(1)} all-to-all(bf16[8,34,1024]{2,1,0:T(8,128)(2,1)S(1)} %reshape_reshape.7), channel_id=1, replica_groups=mesh['dp'=8,'member'=4] {'dp'}, dimensions={0} | all-to-all | bytes 1114112 | tf_op jit(solution)/shard_map/all_to_all | solution.py:82
  57.2 326.0 %all_to_all.39 = bf16[8,128,7168]{2,1,0:T(8,128)(2,1)} all-to-all(bf16[8,128,7168]{2,1,0:T(8,128)(2,1)} %param.9), channel_id=1, replica_groups=mesh['dp'=8,'member'=4] {'dp'}, dimensions={0} | all-to-all | bytes 29360128 | tf_op jit(solution)/shard_map/all_to_all | solution.py:37
  383.2 5.5 all-to-all-start.2
  389.0 10.9 %convolution_convert_fusion.1 = bf16[272,7168]{1,0:T(8,128)(2,1)} fusion(bf16[272,1024]{1,0:T(8,128)(2,1)S(1)} %reshape.77, bf16[1024,7168]{1,0:T(8,128)(2,1)} %bitcast.56), kind=kOutput, calls=%fused_computation.3 | convolution fusion | flops 3994927104 | bytes 19136512 | tf_op jit(solution)/shard_map/dot_general | solution.py:70
  400.1 307.4 %all-to-all-done.2 = bf16[8,128,7168]{2,1,0:T(8,128)(2,1)} async-done(((bf16[8,128,7168]{2,1,0:T(8,128)(2,1)}), bf16[8,128,7168]{2,1,0:T(8,128)(2,1)}, u32[]{:S(2)}, u32[]{:S(2)}) %all-to-all-start.2) | async-done | bytes 14680096 | tf_op jit(solution)/shard_map/all_to_all | solution.py:38
  707.4 10.9 %fusion = bf16[7168,272]{0,1:T(8,128)(2,1)} fusion(bf16[272,1024]{1,0:T(8,128)(2,1)S(1)} %reshape.81, bf16[1024,7168]{1,0:T(8,128)(2,1)} %bitcast.3), kind=kOutput, calls=%fused_computation.4 | convolution fusion | flops 3994927104 | bytes 19136512 | tf_op jit(solution)/shard_map/dot_general | solution.py:12
  718.6 6.3 convert_element_type.68
  724.8 43.7 %reduce-scatter.2.cloned.1.call-done = bf16[1792,272]{0,1:T(8,128)(2,1)} async-done(((bf16[7168,272]{0,1:T(8,128)(2,1)}), bf16[1792,272]{0,1:T(8,128)(2,1)}) %reduce-scatter.2.cloned.1.call-update) | async-done | bytes 974864 | tf_op jit(solution)/shard_map/reduce_scatter | solution.py:85
  768.6 3.5 fusion.6
  772.1 4.9 multiply_convert_fusion
  777.1 4.3 dot_general.38
  781.4 12.3 %convolution_convert_fusion.3 = bf16[8,34,1024]{2,1,0:T(8,128)(2,1)} fusion(bf16[8,34,7168]{2,1,0:T(8,128)(2,1)} %dot_general.38, bf16[1024,7168,1]{1,0,2:T(8,128)(2,1)} %bitcast.4), kind=kOutput, calls=%fused_computation.15 | convolution fusion | flops 3993255936 | bytes 19136512 | tf_op jit(solution)/shard_map/dot_general | solution.py:12
  793.7 4.7 all-to-all-start.3
  798.5 14.2 %convert_bitcast_fusion = bf16[1,1024,7168]{2,1,0:T(8,128)(2,1)} fusion(bf16[272,1024]{1,0:T(8,128)(2,1)S(1)} %reshape.81, bf16[272,7168]{1,0:T(8,128)(2,1)} %all-reduce.2.cloned.1.call-done), kind=kOutput, calls=%fused_computation | convolution fusion | flops 4012015616 | bytes 19136512 | tf_op jit(solution)/shard_map/dot_general | solution.py:12
  812.7 3.9 all-to-all-done.3
  816.8 5.6 all-gather.2.cloned.1.call-done
  822.4 4.3 dot_general.44
  826.7 12.4 %convolution_convert_fusion.2 = bf16[8,34,1024]{2,1,0:T(8,128)(2,1)} fusion(bf16[8,34,7168]{2,1,0:T(8,128)(2,1)} %dot_general.44, bf16[1024,7168,1]{1,0,2:T(8,128)(2,1)} %bitcast.57), kind=kOutput, calls=%fused_computation.14 | convolution fusion | flops 3993255936 | bytes 19136512 | tf_op jit(solution)/shard_map/dot_general | solution.py:12
  839.1 4.6 all-to-all-start.5
  845.0 13.2 %convert_bitcast_fusion.1 = bf16[1,1024,7168]{2,1,0:T(8,128)(2,1)} fusion(bf16[272,1024]{1,0:T(8,128)(2,1)S(1)} %reshape.77, bf16[7168,272]{0,1:T(8,128)(2,1)} %all-gather.2.cloned.1.call-done), kind=kOutput, calls=%fused_computation.1 | convolution fusion | flops 4000317440 | bytes 19136512 | tf_op jit(solution)/shard_map/dot_general | solution.py:12
  858.3 3.6 all-to-all-done.5
  (33 shorter events, 8.8 us)
Async XLA Ops:
  7.2 3.8 copy-start
  12.2 24.5 %all-to-all-start = ((bf16[8,34,1024]{2,1,0:T(8,128)(2,1)}), bf16[8,34,1024]{2,1,0:T(8,128)(2,1)S(1)}, u32[]{:S(2)}, u32[]{:S(2)}) async-start(bf16[8,34,1024]{2,1,0:T(8,128)(2,1)} %reshape_reshape.6), calls=%async_computation | async-start | bytes 1310720 | tf_op jit(solution)/shard_map/all_to_all | solution.py:67
  383.2 324.2 %all-to-all-start.2 = ((bf16[8,128,7168]{2,1,0:T(8,128)(2,1)}), bf16[8,128,7168]{2,1,0:T(8,128)(2,1)}, u32[]{:S(2)}, u32[]{:S(2)}) async-start(bf16[8,128,7168]{2,1,0:T(8,128)(2,1)} %param.10), calls=%async_computation.2 | async-start | bytes 29360128 | tf_op jit(solution)/shard_map/all_to_all | solution.py:38
  388.7 329.8 %all-reduce.2.cloned.1.call-start = ((), (), s32[]{:S(2)}) async-start(), calls=%async_computation.7 | async-start | bytes 7798784 | tf_op jit(solution)/shard_map/psum | solution.py:71
  399.9 368.7 %reduce-scatter.2.cloned.1.call-start = ((), (), s32[]{:S(2)}) async-start(), calls=%async_computation.8 | async-start | bytes 4874240 | tf_op jit(solution)/shard_map/reduce_scatter | solution.py:85
  718.3 104.1 %all-gather.2.cloned.1.call-start = ((), (), s32[]{:S(2)}) async-start(), calls=%async_computation.9 | async-start | bytes 4874240 | tf_op jit(solution)/shard_map/all_gather | solution.py:95
  793.7 22.9 %all-to-all-start.3 = ((bf16[8,34,1024]{2,1,0:T(8,128)(2,1)}), bf16[8,34,1024]{2,1,0:T(8,128)(2,1)S(1)}, u32[]{:S(2)}, u32[]{:S(2)}) async-start(bf16[8,34,1024]{2,1,0:T(8,128)(2,1)} %convolution_convert_fusion.3), calls=%async_computation.3 | async-start | bytes 1310720 | tf_op jit(solution)/shard_map/all_to_all | solution.py:75
  839.1 22.7 %all-to-all-start.5 = ((bf16[8,34,1024]{2,1,0:T(8,128)(2,1)}), bf16[8,34,1024]{2,1,0:T(8,128)(2,1)S(1)}, u32[]{:S(2)}, u32[]{:S(2)}) async-start(bf16[8,34,1024]{2,1,0:T(8,128)(2,1)} %convolution_convert_fusion.2), calls=%async_computation.6 | async-start | bytes 1310720 | tf_op jit(solution)/shard_map/all_to_all | solution.py:100
  845.0 18.3 %copy-start.1 = (bf16[128,1024]{1,0:T(8,128)(2,1)S(1)}, bf16[128,1024]{1,0:T(8,128)(2,1)}, u32[]{:S(2)}) copy-start(bf16[128,1024]{1,0:T(8,128)(2,1)} %param.6) | copy-start | bytes 786436
Sparse Core Ops, SparseCore 0:
  400.0 100.9 all-reduce.1
  718.4 50.0 reduce-scatter.1
  772.3 50.1 all-gather.1
where the time goes:
time: 871 us; the launch traced here: 870 us
  waiting for transfers between devices  381 us (44%)
  blocking collectives  346 us (40%)
  matrix products  78.4 us (9%)
  starting transfers between devices  21.5 us (2%)
  other arithmetic  16.9 us (2%)
  between operations  13.9 us (2%)
  local copies, waits for them, and re-layouts  11.9 us (1%)
    all_to_all x1, blocking collectives, body(): lax.all_to_all(up_parts, 'dp', split_axis=0, concat_axis=1, tiled=True)  326 us
    all_to_all x1, waiting for transfers between devices, body(): lax.all_to_all(down_parts, 'dp', split_axis=0, concat_axis=1, tiled=True)  307 us
    dot_general x5, matrix products, contract(): lax.dot_general(left, right, (((left_dim,), (right_dim,)), ((), ())), pre...  63 us
    reduce_scatter x1, waiting for transfers between devices, body(): lax.psum_scatter(contract(down_own, d_in, 0, 1).astype(jnp.bfloat16), 'me...  43.7 us
    all_to_all x1, blocking collectives, body(): lax.all_to_all(spread(d_local), 'dp', split_axis=0, concat_axis=0, tiled=...  20.5 us
  transfers between devices with their start and end apart: 7, of which 6 were waited for; matrix products, arithmetic and copies ran while one was open for 9% of the time, Pallas kernels for 0%

commit v1 on v0

--- a/solution.py
+++ b/solution.py
@@ -1,11 +1,20 @@
+import functools
+
 import jax
 import jax.numpy as jnp
 from jax import lax
+from jax.experimental import pallas as pl
+from jax.experimental.pallas import tpu as pltpu
 from jax.sharding import PartitionSpec as P
+
 
 FF_W = 7168
 E = 8
 CAP = 34
+HALVES = 2
+LANES = 128
+BF = jnp.bfloat16
+F32 = jnp.float32
 
 
 def contract(left, right, left_dim, right_dim):
@@ -14,7 +23,7 @@
     )
 
 
-def body(tokens, routes, route_weights, up_stacked, down_stacked, cotangent):
+def plain_body(tokens, routes, route_weights, up_stacked, down_stacked, cotangent):
     dp_count = lax.axis_size("dp")
     member_count = lax.axis_size("member")
     quarters = dp_count // E
@@ -71,7 +80,6 @@
     pre_full = lax.psum(partial_value, "member").astype(jnp.float32)
     act_full = jax.nn.silu(pre_full).astype(jnp.bfloat16)
     y_part = contract(act_full, down_own, 1, 1)
-    y_part, pre_full, act_full = (y_part, pre_full, act_full)
     y_back = lax.all_to_all(
         y_part.reshape(dp_count, CAP, features).astype(jnp.bfloat16),
         "dp",
@@ -96,7 +104,6 @@
     g_down = contract(d_in, act_full, 0, 0)
     g_up = contract(x_in, d_pre, 0, 1)
     dx_part = contract(d_pre, up_own, 0, 1)
-    dx_part, g_up, g_down = (dx_part, g_up, g_down)
     dx_back = lax.all_to_all(
         dx_part.reshape(dp_count, CAP, features).astype(jnp.bfloat16),
         "dp",
@@ -115,6 +122,470 @@
     return (mixed, grad_tokens, grad_up, grad_down)
 
 
+def slot_rows(routes_ref):
+    tok = routes_ref.shape[1]
+    expert = lax.broadcasted_iota(jnp.int32, (E, tok), 0)
+    hits = [(routes_ref[k : k + 1, :] == expert) for k in range(2)]
+    either = jnp.where(hits[0] | hits[1], 1.0, 0.0).astype(BF)
+    earlier = lax.broadcasted_iota(jnp.int32, (tok, tok), 0) < lax.broadcasted_iota(
+        jnp.int32, (tok, tok), 1
+    )
+    before = jnp.dot(either, jnp.where(earlier, 1.0, 0.0).astype(BF), preferred_element_type=F32)
+    return [jnp.where(hit, before, -1.0) for hit in hits]
+
+
+def slot_hits(rows, e):
+    slot = lax.broadcasted_iota(jnp.int32, (CAP, rows[0].shape[1]), 0).astype(F32)
+    return [jnp.where(slot == rows[k][e : e + 1, :], 1.0, 0.0) for k in range(2)]
+
+
+def route_kernel(routes_ref, weights_ref, tokens_ref, cot_ref, out_ref):
+    features = tokens_ref.shape[1]
+    size = out_ref.shape[0] // HALVES
+    half = features // HALVES
+    rows = slot_rows(routes_ref)
+    for e in range(E):
+        at = slot_hits(rows, e)
+        pick = (at[0] + at[1]).astype(BF)
+        scale = jnp.sum(at[0] * weights_ref[0:1, :] + at[1] * weights_ref[1:2, :], 1, keepdims=True)
+        x_rows = jnp.dot(pick, tokens_ref[...], preferred_element_type=F32).astype(BF)
+        d_rows = (scale * jnp.dot(pick, cot_ref[...], preferred_element_type=F32)).astype(BF)
+        other = e ^ size
+        cut = (other // size) * half
+        for i, value in enumerate((x_rows, d_rows)):
+            out_ref[e, :, i * features : (i + 1) * features] = value
+            out_ref[other, :, 2 * features + i * half : 2 * features + (i + 1) * half] = value[
+                :, cut : cut + half
+            ]
+
+
+def route(routes_t, weights_t, tokens, cotangent, dp_count):
+    features = tokens.shape[1]
+    return pl.pallas_call(
+        route_kernel,
+        out_shape=jax.ShapeDtypeStruct((dp_count, CAP, 3 * features), BF),
+        cost_estimate=pl.CostEstimate(
+            flops=4 * E * CAP * tokens.size, bytes_accessed=2 * 10 * tokens.size, transcendentals=0
+        ),
+        name="route",
+    )(routes_t, weights_t, tokens, cotangent)
+
+
+def returned_rows(ref, e, half, kind):
+    size, width = ref.shape[0] // HALVES, ref.shape[2] // 4
+    if e // size == half:
+        return ref[e, :, kind * width : (kind + 1) * width]
+    return ref[e ^ size, :, (2 + kind) * width : (3 + kind) * width]
+
+
+def mix_kernel(routes_ref, weights_ref, back_ref, mixed_ref, grad_ref):
+    tok = routes_ref.shape[1]
+    rows = slot_rows(routes_ref)
+    width = back_ref.shape[2] // 4
+    for half in range(HALVES):
+        first, second, grad = [jnp.zeros((tok, width), F32) for _ in range(3)]
+        for e in range(E):
+            at = [hit.astype(BF) for hit in slot_hits(rows, e)]
+            y_rows = returned_rows(back_ref, e, half, 0)
+            first += contract(at[0], y_rows, 0, 0)
+            second += contract(at[1], y_rows, 0, 0)
+            grad += contract(at[0] + at[1], returned_rows(back_ref, e, half, 1), 0, 0)
+        lanes = slice(half * width, (half + 1) * width)
+        mixed_ref[:, lanes] = (weights_ref[:, 0:1] * first + weights_ref[:, 1:2] * second).astype(BF)
+        grad_ref[:, lanes] = grad.astype(BF)
+
+
+def full_spec(shape):
+    return pl.BlockSpec(shape, lambda q, where: (0,) * len(shape))
+
+
+class Plan:
+    def __init__(self, dp_count, members, share, hidden):
+        self.dp_count, self.members, self.share, self.hidden = dp_count, members, share, hidden
+        self.size = dp_count // HALVES
+        self.peers = self.size - 1
+        self.group_features = self.size * share
+        self.slots = dp_count * CAP
+        self.where = jnp.stack([lax.axis_index("dp"), lax.axis_index("member")]).astype(jnp.int32)
+        self.last = None
+
+    def part(self, where, p, k=0):
+        return (where[0] ^ (p * self.size)) ^ k
+
+    def swap(self, value, k):
+        return lax.ppermute(value, "dp", [(i, i ^ k) for i in range(self.dp_count)])
+
+    def pass_on(self, value, k):
+        return lax.ppermute(value, "member", [(i, i ^ k) for i in range(self.members)])
+
+    def call(self, kernel, grid, in_specs, args, out_specs, out_shape, cost, aliases=None, scratch=()):
+        args, in_specs = list(args), list(in_specs)
+        if self.last is not None and not any(arg is self.last for arg in args):
+            args.append(self.last)
+            in_specs.append(pl.BlockSpec(memory_space=pl.ANY))
+
+            def placed(where, *refs, count=len(args) - 1):
+                kernel(where, *refs[:count], *refs[count + 1 :])
+        else:
+            placed = kernel
+        outs = pl.pallas_call(
+            placed,
+            grid_spec=pltpu.PrefetchScalarGridSpec(
+                num_scalar_prefetch=1,
+                grid=grid,
+                in_specs=in_specs,
+                out_specs=out_specs,
+                scratch_shapes=scratch,
+            ),
+            out_shape=out_shape,
+            input_output_aliases={i + 1: o for i, o in (aliases or {}).items()},
+            cost_estimate=pl.CostEstimate(flops=cost[0], bytes_accessed=cost[1], transcendentals=0),
+        )(self.where, *args)
+        self.last = outs[-1]
+        return outs
+
+
+def prepare(plan, got):
+    features = got.shape[2] // 3
+    half, share, slots = plan.group_features, plan.share, plan.slots
+
+    def kernel(where, got_ref, own_ref, rows_ref, wide_ref):
+        place, group = where[0] % plan.size, where[0] // plan.size
+        for b in range(plan.dp_count):
+            wide_ref[b * CAP : (b + 1) * CAP, :] = got_ref[b].astype(F32)
+        for i in range(2):
+            own_ref[i] = wide_ref[:, i * features : (i + 1) * features].astype(BF)
+            for k in range(plan.size):
+                into = slice(k * share, (k + 1) * share)
+                shift = (place ^ k) * share
+                for p, base in ((0, i * features + group * half), (1, 2 * features + i * half)):
+                    at = pl.multiple_of(base + shift, LANES)
+                    rows_ref[2 * p + i, :, into] = wide_ref[:, pl.ds(at, share)].astype(BF)
+
+    return plan.call(
+        kernel,
+        (1,),
+        [full_spec(got.shape)],
+        [got],
+        [full_spec((2, slots, features)), full_spec((4, slots, half))],
+        [
+            jax.ShapeDtypeStruct((2, slots, features), BF),
+            jax.ShapeDtypeStruct((4, slots, half), BF),
+        ],
+        (0, 6 * got.size),
+        scratch=[pltpu.VMEM((slots, got.shape[2]), F32)],
+    )
+
+
+def pack(plan, up, down, start, width):
+    step = plan.members * LANES
+    first = start // step
+
+    def kernel(where, *refs):
+        del where
+        sources, outs = refs[: plan.peers * 4], refs[-plan.peers :]
+        for k in range(plan.peers):
+            for i in range(4):
+                outs[k][i] = sources[k * 4 + i][0]
+
+    in_specs = [
+        pl.BlockSpec(
+            (1, plan.share, step),
+            functools.partial(lambda i, where, p, k: (plan.part(where, p, k), 0, first + i), p=p, k=k),
+        )
+        for k in range(1, plan.size)
+        for p in range(HALVES)
+        for _ in range(2)
+    ]
+    return plan.call(
+        kernel,
+        (width // step,),
+        in_specs,
+        [up, down] * (plan.peers * HALVES),
+        [
+            pl.BlockSpec((4, plan.share, step), lambda i, where: (0, 0, i))
+            for _ in range(plan.peers)
+        ],
+        [jax.ShapeDtypeStruct((4, plan.share, width), BF) for _ in range(plan.peers)],
+        (0, plan.peers * 4 * plan.share * width * 4),
+    )
+
+
+def weight_specs(plan, start, width):
+    own = pl.BlockSpec(
+        (1, plan.share, width), lambda p, where: (plan.part(where, p), 0, start // width)
+    )
+    return [own, own] + [
+        pl.BlockSpec((2, plan.share, width), lambda p, where: (p, 0, 0)) for _ in range(plan.peers)
+    ]
+
+
+def member_lanes(where, m, sub):
+    return pl.ds(pl.multiple_of((where[1] ^ m) * sub, LANES), sub)
+
+
+def stacked_rows(refs, i, lanes):
+    return jnp.concatenate([refs[i][0, :, lanes]] + [ref[i, :, lanes] for ref in refs[2:]], axis=0)
+
+
+def hidden_partials(plan, rows, up, down, came, start, width):
+    sub = width // plan.members
+    half, slots = plan.group_features, plan.slots
+
+    def kernel(where, rows_ref, *refs):
+        w_refs, outs = refs[: 2 + plan.peers], refs[-plan.members :]
+        for m in range(plan.members):
+            lanes = member_lanes(where, m, sub)
+            for i in range(2):
+                outs[m][i] = jnp.dot(
+                    rows_ref[i], stacked_rows(w_refs, i, lanes), preferred_element_type=F32
+                ).astype(BF)
+
+    return plan.call(
+        kernel,
+        (HALVES,),
+        [pl.BlockSpec((2, slots, half), lambda p, where: (p, 0, 0))]
+        + weight_specs(plan, start, width),
+        [rows, up, down, *came],
+        [pl.BlockSpec((2, slots, sub), lambda p, where: (p, 0, 0)) for _ in range(plan.members)],
+        [jax.ShapeDtypeStruct((4, slots, sub), BF) for _ in range(plan.members)],
+        (8 * slots * half * width, 8 * width * (slots + half)),
+    )
+
+
+def sum_away(plan, parts):
+    _, slots, sub = parts[0].shape
+
+    def kernel(where, *refs):
+        del where
+        total = refs[0][0].astype(F32)
+        for ref in refs[1 : plan.members]:
+            total += ref[0].astype(F32)
+        refs[-1][0] = total.astype(BF)
+
+    return plan.call(
+        kernel,
+        (2,),
+        [pl.BlockSpec((1, slots, sub), lambda q, where: (2 + q, 0, 0))] * plan.members,
+        parts,
+        [pl.BlockSpec((1, slots, sub), lambda q, where: (q, 0, 0))],
+        [jax.ShapeDtypeStruct((2, slots, sub), BF)],
+        (0, 4 * slots * sub * (plan.members + 1)),
+    )[0]
+
+
+def activate(plan, parts, back):
+    _, slots, sub = parts[0].shape
+    lanes = min(sub, 2 * LANES)
+
+    def kernel(where, *refs):
+        del where
+        sums = []
+        for i in range(2):
+            total = refs[plan.members][i].astype(F32)
+            for ref in refs[: plan.members]:
+                total += ref[i].astype(F32)
+            sums.append(total)
+        pre, d_act = sums
+        sigma = 1.0 / (1.0 + jnp.exp(-pre))
+        refs[-1][0] = (pre * sigma).astype(BF)
+        refs[-1][1] = (d_act * sigma * (1.0 + pre * (1.0 - sigma))).astype(BF)
+
+    spec = pl.BlockSpec((2, slots, lanes), lambda q, where: (0, 0, q))
+    return plan.call(
+        kernel,
+        (sub // lanes,),
+        [spec] * (plan.members + 1),
+        [*parts, back],
+        [spec],
+        [jax.ShapeDtypeStruct((2, slots, sub), BF)],
+        (0, 4 * slots * sub * (plan.members + 2)),
+    )[0]
+
+
+def feature_sums(plan, total, pieces, up, down, came, start, width, final):
+    sub = width // plan.members
+    half, share, slots = plan.group_features, plan.share, plan.slots
+
+    def kernel(where, *refs):
+        place = where[0] % plan.size
+        p_refs = refs[: plan.members]
+        w_refs = refs[plan.members : plan.members + 2 + plan.peers]
+        before = refs[plan.members + 2 + plan.peers]
+        out = refs[-2] if final else refs[-1]
+        for i in range(2):
+            value = None
+            for m in range(plan.members):
+                weights = stacked_rows(w_refs, 1 - i, member_lanes(where, m, sub))
+                term = contract(p_refs[m][i], weights, 1, 1)
+                value = term if value is None else value + term
+            for k in range(plan.size):
+                at = pl.ds(pl.multiple_of((place ^ k) * share, LANES), share)
+                piece = value[:, k * share : (k + 1) * share]
+                if total is not None:
+                    piece += before[i, :, at]
+                if final:
+                    refs[-1][:, at] = piece
+                else:
+                    out[i, :, at] = piece
+            if final:
+                for b in range(plan.dp_count):
+                    out[b, :, i * half : (i + 1) * half] = refs[-1][
+                        b * CAP : (b + 1) * CAP, :
+                    ].astype(BF)
+
+    stack = pl.BlockSpec((2, slots, half), lambda p, where: (p, 0, 0))
+    in_specs = [
+        pl.BlockSpec((2, slots, sub), lambda p, where: (p, 0, 0)) for _ in range(plan.members)
+    ] + weight_specs(plan, start, width)
+    args = [*pieces, up, down, *came]
+    if total is not None:
+        in_specs.append(stack)
+        args.append(total)
+    if final:
+        out_spec = pl.BlockSpec((plan.dp_count, CAP, 2 * half), lambda p, where: (0, 0, p))
+        out = jax.ShapeDtypeStruct((plan.dp_count, CAP, 4 * half), BF)
+    else:
+        out_spec, out = stack, jax.ShapeDtypeStruct((4, slots, half), F32)
+    return plan.call(
+        kernel,
+        (HALVES,),
+        in_specs,
+        args,
+        [out_spec],
+        [out],
+        (8 * slots * half * width, 8 * width * (slots + half) + 32 * slots * half),
+        scratch=[pltpu.VMEM((slots, half), F32)] if final else (),
+    )[0]
+
+
+def weight_grads(plan, buffers, x_t, d_t, pieces, start, width):
+    sub = width // plan.members
+    features, slots = x_t.shape
+    block = features // 2
+
+    def kernel(where, x_ref, d_ref, *refs):
+        up_out, down_out = refs[-2:]
+        for m in range(plan.members):
+            lanes = member_lanes(where, m, sub)
+            down_out[0, :, lanes] = jnp.dot(
+                d_ref[...], refs[m][0], preferred_element_type=F32
+            ).astype(BF)
+            up_out[0, :, lanes] = jnp.dot(
+                x_ref[...], refs[m][1], preferred_element_type=F32
+            ).astype(BF)
+
+    in_specs = [pl.BlockSpec((block, slots), lambda q, where: (q, 0))] * 2
+    in_specs += [full_spec((2, slots, sub))] * plan.members
+    args = [x_t, d_t, *pieces]
+    aliases = {}
+    if buffers is not None:
+        aliases = {len(args): 0, len(args) + 1: 1}
+        in_specs += [pl.BlockSpec(memory_space=pl.ANY)] * 2
+        args += buffers
+    return plan.call(
+        kernel,
+        (2,),
+        in_specs,
+        args,
+        [pl.BlockSpec((1, block, width), lambda q, where: (0, q, start // width))] * 2,
+        [jax.ShapeDtypeStruct((1, features, plan.hidden), BF) for _ in range(2)],
+        (4 * features * slots * width, 4 * width * (slots + features)),
+        aliases=aliases,
+    )
+
+
+def chunk_list(hidden, unit):
+    units = hidden // unit
+    wide = max(0, (units - 1) // 2)
+    narrow = [(2 * wide + i, 1) for i in range(units - 2 * wide)]
+    chunks = narrow[:-1] + [(2 * i, 2) for i in range(wide)] + narrow[-1:]
+    return [(unit * start, unit * width) for start, width in chunks]
+
+
+LAGS = (
+    ("hidden", 0),
+    ("spread", 2),
+    ("activate", 1),
+    ("features", 3),
+    ("away", 0),
+    ("fetch", -2),
+    ("grads", 5),
+)
+
+
+def order_of(count):
+    steps = [("fetch", 0), ("route", 0), ("fetch", 1), ("prepare", 0)]
+    for i in range(count + max(lag for _, lag in LAGS)):
+        for kind, lag in LAGS:
+            first = 2 if kind == "fetch" else 0
+            if first <= i - lag < count:
+                steps.append((kind, i - lag))
+                if (kind, i - lag) == ("features", count - 1):
+                    steps.append(("return", 0))
+    return steps
+
+
+def halves_body(tokens, routes, route_weights, up, down, cotangent):
+    dp_count, members = lax.axis_size("dp"), lax.axis_size("member")
+    share, hidden = up.shape[1:]
+    plan = Plan(dp_count, members, share, hidden)
+
+    chunks = chunk_list(hidden, members * LANES)
+    count = len(chunks)
+    routes_t, weights_t = routes.T, route_weights.T
+
+    came, reduced, backs, owns, others, pieces = {}, {}, {}, {}, {}, {}
+    got = own = rows = total = grads = back = None
+    for kind, i in order_of(count):
+        if kind == "fetch":
+            packed = pack(plan, up, down, *chunks[i])
+        elif kind == "route":
+            send = route(routes_t, weights_t, tokens, cotangent, dp_count)
+        elif kind == "prepare":
+            own, rows = prepare(plan, got)
+        elif kind == "hidden":
+            outs = hidden_partials(plan, rows, up, down, came[i], *chunks[i])
+        elif kind == "away":
+            away = sum_away(plan, reduced[i])
+        elif kind == "activate":
+            owns[i] = activate(plan, reduced[i], backs[i])
+        elif kind == "spread":
+            both = jnp.concatenate([owns[i], others[i]], axis=0)
+        elif kind == "features":
+            total = feature_sums(
+                plan, total, pieces[i], up, down, came[i], *chunks[i], i == count - 1
+            )
+        elif kind == "grads":
+            grads = weight_grads(plan, grads, x_t, d_t, pieces[i], *chunks[i])
+        if kind == "fetch":
+            came[i] = [plan.swap(packed[k], k + 1) for k in range(plan.peers)]
+        elif kind == "route":
+            got = lax.all_to_all(send, "dp", split_axis=0, concat_axis=0, tiled=True)
+        elif kind == "prepare":
+            x_t, d_t = own[0].T, own[1].T
+        elif kind == "hidden":
+            reduced[i] = [outs[0]] + [plan.pass_on(outs[k], k) for k in range(1, members)]
+        elif kind == "away":
+            backs[i] = plan.swap(away, plan.size)
+        elif kind == "activate":
+            others[i] = plan.swap(owns[i], plan.size)
+        elif kind == "spread":
+            pieces[i] = [both] + [plan.pass_on(both, k) for k in range(1, members)]
+        elif kind == "return":
+            back = lax.all_to_all(total, "dp", split_axis=0, concat_axis=0, tiled=True)
+
+    out = jax.ShapeDtypeStruct(tokens.shape, BF)
+    mixed, grad_tokens = pl.pallas_call(mix_kernel, out_shape=(out, out), name="mix")(
+        routes_t, route_weights, back
+    )
+    return (mixed, grad_tokens, *grads)
+
+
+def power_of_two(value):
+    return value & (value - 1) == 0
+
+
 def solution(mesh):
     placed = (
         P("dp", "member"),
@@ -124,6 +595,19 @@
         P(None, ("member", "dp"), None),
         P("dp", "member"),
     )
+
+    dp_count, members = mesh.shape["dp"], mesh.shape["member"]
+    fits = (
+        dp_count == E
+        and power_of_two(members)
+        and FF_W % (members * LANES) == 0
+    )
+
+    def body(*args):
+        if not fits or args[3].shape[1] % LANES:
+            return plain_body(*args)
+        return halves_body(*args)
+
     return jax.shard_map(
         body,
         mesh=mesh,

time: 871 us -> 758 us (0.87); the launches traced: 870 us -> 747 us
  blocking collectives: 346 us -> 0 us
  Pallas kernels: 0 us -> 220 us
  starting transfers between devices: 21.5 us -> 112 us
  matrix products: 78.4 us -> 0 us
  between operations: 13.9 us -> 1.56 us
  other arithmetic: 16.9 us -> 5.43 us
  waiting for transfers between devices: 381 us -> 392 us
    all_to_all x2 -> x0, blocking collectives: 346 us -> none  [the longest x1 326 us: body(): lax.all_to_all(up_parts, 'dp', split_axis=0, concat_axis=1, tiled=True)]
    ppermute x0 -> x88, waiting for transfers between devices: none -> 343 us  [the longest x40 193 us: swap(): return lax.ppermute(value, 'dp', [(i, i ^ k) for i in range(self.dp_count)])]
    all_to_all x4 -> x2, waiting for transfers between devices: 331 us -> 48.6 us  [the longest x1 34 us: halves_body(): got = lax.all_to_all(send, 'dp', split_axis=0, concat_axis=0, tiled=True)]
    pallas_call x0 -> x51, Pallas kernels: none -> 220 us  [the longest x49 212 us: call(): pl.pallas_call(placed, grid_spec=pltpu.PrefetchScalarGridSpec(num_scalar_...]
    ppermute x0 -> x88, starting transfers between devices: none -> 97.4 us  [the longest x48 64.2 us: pass_on(): lax.ppermute(value, 'member', [(i, i ^ k) for i in range(self.members)])]
    dot_general x10 -> x0, matrix products: 78.4 us -> none  [the longest x5 63 us: contract(): lax.dot_general(left, right, (((left_dim,), (right_dim,)), ((), ())), pre...]
    reduce_scatter x1 -> x0, waiting for transfers between devices: 43.7 us -> none  [body(): lax.psum_scatter(contract(down_own, d_in, 0, 1).astype(jnp.bfloat16), 'me...]
    convert_element_type x4 -> x0, other arithmetic: 14.7 us -> none  [the longest x1 6.27 us: body(): pre_full = lax.psum(partial_value, 'member').astype(jnp.float32)]
  transfers between devices with their start and end apart: 7 -> 90, of which waited for: 6 -> 29; matrix products, arithmetic and copies ran while one was open for 9% -> 1% of each run, Pallas kernels for 0% -> 26%
where the time goes in v1:
time: 758 us; the launch traced here: 747 us
  waiting for transfers between devices  392 us (52%)
  Pallas kernels  220 us (29%)
  starting transfers between devices  112 us (15%)
  local copies, waits for them, and re-layouts  15.9 us (2%)
    pallas_call x49, Pallas kernels, call(): pl.pallas_call(placed, grid_spec=pltpu.PrefetchScalarGridSpec(num_scalar_...  212 us
    ppermute x40, waiting for transfers between devices, swap(): return lax.ppermute(value, 'dp', [(i, i ^ k) for i in range(self.dp_count)])  193 us
    ppermute x48, waiting for transfers between devices, pass_on(): lax.ppermute(value, 'member', [(i, i ^ k) for i in range(self.members)])  150 us
    ppermute x48, starting transfers between devices, pass_on(): lax.ppermute(value, 'member', [(i, i ^ k) for i in range(self.members)])  64.2 us
    all_to_all x1, waiting for transfers between devices, halves_body(): got = lax.all_to_all(send, 'dp', split_axis=0, concat_axis=0, tiled=True)  34 us
    ppermute x40, starting transfers between devices, swap(): return lax.ppermute(value, 'dp', [(i, i ^ k) for i in range(self.dp_count)])  33.2 us
  transfers between devices with their start and end apart: 90, of which 29 were waited for; matrix products, arithmetic and copies ran while one was open for 1% of the time, Pallas kernels for 26%

profile of v1, /device:TPU:0, one launch (start us, length us, event | category | flops | bytes accessed | tf_op | source)
XLA Modules:
  0.0 746.8 jit_solution(12679086836735801871)
XLA Ops:
  3.8 6.4 all-to-all-start
  22.5 34.0 %all-to-all-done.refs_0_ = bf16[8,34,3072]{2,1,0:T(8,128)(2,1)S(1)} async-done(((bf16[8,34,3072]{2,1,0:T(8,128)(2,1)}), bf16[8,34,3072]{2,1,0:T(8,128)(2,1)S(1)}, u32[]{:S(2)}, u32[]{:S(2)}) %all-to-all-start) | async-done | bytes 1671200 | tf_op jit(solution)/shard_map/all_to_all | solution.py:564
  74.3 6.7 collective-permute-done.6.refs_1_
  83.5 7.4 collective-permute-done.8.refs_3_
  98.2 13.7 %collective-permute-done.2.refs_5_.refs_8_ = bf16[4,128,1024]{2,1,0:T(8,128)(2,1)} collective-permute-done((bf16[4,128,1024]{2,1,0:T(8,128)(2,1)}, bf16[4,128,1024]{2,1,0:T(8,128)(2,1)}, u32[]{:S(2)}, u32[]{:S(2)}) %collective-permute-start.2) | collective-permute-done | bytes 1048608 | tf_op jit(solution)/shard_map/ppermute | solution.py:216
  122.7 45.3 %collective-permute-done.12.refs_4_ = bf16[2,272,128]{2,1,0:T(8,128)(2,1)S(1)} collective-permute-done((bf16[2,272,128]{2,1,0:T(8,128)(2,1)S(1)}, bf16[2,272,128]{2,1,0:T(8,128)(2,1)S(1)}, u32[]{:S(2)}, u32[]{:S(2)}) %collective-permute-start.12) | collective-permute-done | bytes 139296 | tf_op jit(solution)/shard_map/ppermute | solution.py:216
  172.6 21.8 %collective-permute-done.10.refs_2_ = bf16[4,272,256]{2,1,0:T(8,128)(2,1)} collective-permute-done((bf16[4,272,256]{2,1,0:T(8,128)(2,1)}, bf16[4,272,256]{2,1,0:T(8,128)(2,1)}, u32[]{:S(2)}, u32[]{:S(2)}) %collective-permute-start.10) | collective-permute-done | bytes 557088 | tf_op jit(solution)/shard_map/ppermute | solution.py:219
  213.7 47.5 %collective-permute-done.26 = bf16[2,272,128]{2,1,0:T(8,128)(2,1)S(1)} collective-permute-done((bf16[2,272,128]{2,1,0:T(8,128)(2,1)S(1)}, bf16[2,272,128]{2,1,0:T(8,128)(2,1)S(1)}, u32[]{:S(2)}, u32[]{:S(2)}) %collective-permute-start.26) | collective-permute-done | bytes 139296 | tf_op jit(solution)/shard_map/ppermute | solution.py:216
  264.6 12.8 %collective-permute-done.22.refs_4_ = bf16[2,272,256]{2,1,0:T(8,128)(2,1)} collective-permute-done((bf16[2,272,256]{2,1,0:T(8,128)(2,1)}, bf16[2,272,256]{2,1,0:T(8,128)(2,1)}, u32[]{:S(2)}, u32[]{:S(2)}) %collective-permute-start.22) | collective-permute-done | bytes 278560 | tf_op jit(solution)/shard_map/ppermute | solution.py:216
  281.0 22.5 %collective-permute-done.20.refs_2_ = bf16[4,272,256]{2,1,0:T(8,128)(2,1)} collective-permute-done((bf16[4,272,256]{2,1,0:T(8,128)(2,1)}, bf16[4,272,256]{2,1,0:T(8,128)(2,1)}, u32[]{:S(2)}, u32[]{:S(2)}) %collective-permute-start.20) | collective-permute-done | bytes 557088 | tf_op jit(solution)/shard_map/ppermute | solution.py:219
  327.7 13.9 %collective-permute-done.40 = bf16[2,272,256]{2,1,0:T(8,128)(2,1)S(1)} collective-permute-done((bf16[2,272,256]{2,1,0:T(8,128)(2,1)S(1)}, bf16[2,272,256]{2,1,0:T(8,128)(2,1)S(1)}, u32[]{:S(2)}, u32[]{:S(2)}) %collective-permute-start.40) | collective-permute-done | bytes 278560 | tf_op jit(solution)/shard_map/ppermute | solution.py:216
  350.7 23.5 %collective-permute-done.24.refs_2_ = bf16[4,272,256]{2,1,0:T(8,128)(2,1)S(1)} collective-permute-done((bf16[4,272,256]{2,1,0:T(8,128)(2,1)}, bf16[4,272,256]{2,1,0:T(8,128)(2,1)S(1)}, u32[]{:S(2)}, u32[]{:S(2)}) %collective-permute-start.24) | collective-permute-done | bytes 557088 | tf_op jit(solution)/shard_map/ppermute | solution.py:219
  408.6 11.8 %collective-permute-done.48 = bf16[2,272,256]{2,1,0:T(8,128)(2,1)S(1)} collective-permute-done((bf16[2,272,256]{2,1,0:T(8,128)(2,1)S(1)}, bf16[2,272,256]{2,1,0:T(8,128)(2,1)S(1)}, u32[]{:S(2)}, u32[]{:S(2)}) %collective-permute-start.48) | collective-permute-done | bytes 278560 | tf_op jit(solution)/shard_map/ppermute | solution.py:216
  429.1 22.4 %collective-permute-done.38.refs_2_ = bf16[4,272,256]{2,1,0:T(8,128)(2,1)S(1)} collective-permute-done((bf16[4,272,256]{2,1,0:T(8,128)(2,1)}, bf16[4,272,256]{2,1,0:T(8,128)(2,1)S(1)}, u32[]{:S(2)}, u32[]{:S(2)}) %collective-permute-start.38) | collective-permute-done | bytes 557088 | tf_op jit(solution)/shard_map/ppermute | solution.py:219
  480.3 12.7 %collective-permute-done.52.refs_4_ = bf16[2,272,256]{2,1,0:T(8,128)(2,1)S(1)} collective-permute-done((bf16[2,272,256]{2,1,0:T(8,128)(2,1)S(1)}, bf16[2,272,256]{2,1,0:T(8,128)(2,1)S(1)}, u32[]{:S(2)}, u32[]{:S(2)}) %collective-permute-start.52) | collective-permute-done | bytes 278560 | tf_op jit(solution)/shard_map/ppermute | solution.py:216
  493.9 6.4 collective-permute-done.45.refs_1_
  503.4 10.6 %collective-permute-done.47.refs_3_ = bf16[4,272,256]{2,1,0:T(8,128)(2,1)S(1)} collective-permute-done((bf16[4,272,256]{2,1,0:T(8,128)(2,1)}, bf16[4,272,256]{2,1,0:T(8,128)(2,1)S(1)}, u32[]{:S(2)}, u32[]{:S(2)}) %collective-permute-start.47) | collective-permute-done | bytes 557088 | tf_op jit(solution)/shard_map/ppermute | solution.py:219
  567.0 7.0 collective-permute-done.54.refs_4_.refs_7_
  576.1 11.1 %collective-permute-done.60.refs_2_ = bf16[4,272,256]{2,1,0:T(8,128)(2,1)S(1)} collective-permute-done((bf16[4,272,256]{2,1,0:T(8,128)(2,1)}, bf16[4,272,256]{2,1,0:T(8,128)(2,1)S(1)}, u32[]{:S(2)}, u32[]{:S(2)}) %collective-permute-start.60) | collective-permute-done | bytes 557088 | tf_op jit(solution)/shard_map/ppermute | solution.py:219
  591.1 6.3 shard_map.125.refs_4_.refs_9_
  627.1 6.2 shard_map.130.refs_4_.refs_9_
  633.3 9.8 %collective-permute-done.69.refs_3_ = bf16[4,272,128]{2,1,0:T(8,128)(2,1)} collective-permute-done((bf16[4,272,128]{2,1,0:T(8,128)(2,1)}, bf16[4,272,128]{2,1,0:T(8,128)(2,1)}, u32[]{:S(2)}, u32[]{:S(2)}) %collective-permute-start.69) | collective-permute-done | bytes 278560 | tf_op jit(solution)/shard_map/ppermute | solution.py:219
  700.5 8.7 %all-to-all-start.1 = ((bf16[8,34,2048]{2,1,0:T(8,128)(2,1)}), bf16[8,34,2048]{2,1,0:T(8,128)(2,1)S(1)}, u32[]{:S(2)}, u32[]{:S(2)}) async-start(bf16[8,34,2048]{2,1,0:T(8,128)(2,1)} %shard_map.138.refs_8_), calls=%async_computation.1 | async-start | bytes 2621440 | tf_op jit(solution)/shard_map/all_to_all | solution.py:576
  726.7 14.6 %all-to-all-done.1.back_ref = bf16[8,34,2048]{2,1,0:T(8,128)(2,1)S(1)} async-done(((bf16[8,34,2048]{2,1,0:T(8,128)(2,1)}), bf16[8,34,2048]{2,1,0:T(8,128)(2,1)S(1)}, u32[]{:S(2)}, u32[]{:S(2)}) %all-to-all-start.1) | async-done | bytes 1114144 | tf_op jit(solution)/shard_map/all_to_all | solution.py:576
  (351 shorter events, 362.2 us)
Async XLA Ops:
  3.8 52.7 %all-to-all-start = ((bf16[8,34,3072]{2,1,0:T(8,128)(2,1)}), bf16[8,34,3072]{2,1,0:T(8,128)(2,1)S(1)}, u32[]{:S(2)}, u32[]{:S(2)}) async-start(bf16[8,34,3072]{2,1,0:T(8,128)(2,1)} %route.1), calls=%async_computation | async-start | bytes 3932160 | tf_op jit(solution)/shard_map/all_to_all | solution.py:564
  14.6 47.5 %collective-permute-start.4 = (bf16[4,128,512]{2,1,0:T(8,128)(2,1)}, bf16[4,128,512]{2,1,0:T(8,128)(2,1)}, u32[]{:S(2)}, u32[]{:S(2)}) collective-permute-start(bf16[4,128,512]{2,1,0:T(8,128)(2,1)} %get-tuple-element.86), channel_id=1, source_target_pairs={{0,8},{4,12},{8,0},{12,4},{16,24},{20,28},{24,16},{28,20},{1,9},{5... | collective-permute-start | bytes 1572872 | tf_op jit(solution)/shard_map/ppermute | solution.py:216
  16.3 50.7 %collective-permute-start.5 = (bf16[4,128,512]{2,1,0:T(8,128)(2,1)}, bf16[4,128,512]{2,1,0:T(8,128)(2,1)}, u32[]{:S(2)}, u32[]{:S(2)}) collective-permute-start(bf16[4,128,512]{2,1,0:T(8,128)(2,1)} %get-tuple-element.80.refs_12_), channel_id=1, source_target_pairs={{0,12},{4,8},{8,4},{12,0},{16,28},{20,24},{24,20},{28,16},{1,13},{... | collective-permute-start | bytes 1572872 | tf_op jit(solution)/shard_map/ppermute | solution.py:216
  20.3 77.9 %collective-permute-start = (bf16[4,128,1024]{2,1,0:T(8,128)(2,1)}, bf16[4,128,1024]{2,1,0:T(8,128)(2,1)S(1)}, u32[]{:S(2)}, u32[]{:S(2)}) collective-permute-start(bf16[4,128,1024]{2,1,0:T(8,128)(2,1)} %get-tuple-element.83), channel_id=1, source_target_pairs={{0,4},{4,0},{8,12},{12,8},{16,20},{20,16},{24,28},{28,24},{1,5},{5... | collective-permute-start | bytes 3145736 | tf_op jit(solution)/shard_map/ppermute | solution.py:216
  20.9 77.3 %collective-permute-start.1 = (bf16[4,128,1024]{2,1,0:T(8,128)(2,1)}, bf16[4,128,1024]{2,1,0:T(8,128)(2,1)}, u32[]{:S(2)}, u32[]{:S(2)}) collective-permute-start(bf16[4,128,1024]{2,1,0:T(8,128)(2,1)} %get-tuple-element.84), channel_id=1, source_target_pairs={{0,8},{4,12},{8,0},{12,4},{16,24},{20,28},{24,16},{28,20},{1,9},{5... | collective-permute-start | bytes 3145736 | tf_op jit(solution)/shard_map/ppermute | solution.py:216
  22.5 89.4 %collective-permute-start.2 = (bf16[4,128,1024]{2,1,0:T(8,128)(2,1)}, bf16[4,128,1024]{2,1,0:T(8,128)(2,1)}, u32[]{:S(2)}, u32[]{:S(2)}) collective-permute-start(bf16[4,128,1024]{2,1,0:T(8,128)(2,1)} %get-tuple-element.81.refs_1_), channel_id=1, source_target_pairs={{0,12},{4,8},{8,4},{12,0},{16,28},{20,24},{24,20},{28,16},{1,13},{... | collective-permute-start | bytes 3145736 | tf_op jit(solution)/shard_map/ppermute | solution.py:216
  116.9 52.6 %collective-permute-start.9 = (bf16[4,272,256]{2,1,0:T(8,128)(2,1)}, bf16[4,272,256]{2,1,0:T(8,128)(2,1)}, u32[]{:S(2)}, u32[]{:S(2)}) collective-permute-start(bf16[4,272,256]{2,1,0:T(8,128)(2,1)} %get-tuple-element.93), channel_id=1, source_target_pairs={{0,1},{1,0},{2,3},{3,2},{4,5},{5,4},{6,7},{7,6},{8,9},{9,8},{10,11... | collective-permute-start | bytes 1671176 | tf_op jit(solution)/shard_map/ppermute | solution.py:219
  118.4 82.8 %collective-permute-start.16 = (bf16[4,128,1024]{2,1,0:T(8,128)(2,1)}, bf16[4,128,1024]{2,1,0:T(8,128)(2,1)S(1)}, u32[]{:S(2)}, u32[]{:S(2)}) collective-permute-start(bf16[4,128,1024]{2,1,0:T(8,128)(2,1)} %get-tuple-element.99), channel_id=1, source_target_pairs={{0,4},{4,0},{8,12},{12,8},{16,20},{20,16},{24,28},{28,24},{1,5},{5... | collective-permute-start | bytes 3145736 | tf_op jit(solution)/shard_map/ppermute | solution.py:216
  118.5 82.7 %collective-permute-start.17 = (bf16[4,128,1024]{2,1,0:T(8,128)(2,1)}, bf16[4,128,1024]{2,1,0:T(8,128)(2,1)S(1)}, u32[]{:S(2)}, u32[]{:S(2)}) collective-permute-start(bf16[4,128,1024]{2,1,0:T(8,128)(2,1)} %get-tuple-element.100), channel_id=1, source_target_pairs={{0,8},{4,12},{8,0},{12,4},{16,24},{20,28},{24,16},{28,20},{1,9},{5... | collective-permute-start | bytes 3145736 | tf_op jit(solution)/shard_map/ppermute | solution.py:216
  119.2 82.0 %collective-permute-start.18 = (bf16[4,128,1024]{2,1,0:T(8,128)(2,1)}, bf16[4,128,1024]{2,1,0:T(8,128)(2,1)S(1)}, u32[]{:S(2)}, u32[]{:S(2)}) collective-permute-start(bf16[4,128,1024]{2,1,0:T(8,128)(2,1)} %get-tuple-element.91.refs_6_), channel_id=1, source_target_pairs={{0,12},{4,8},{8,4},{12,0},{16,28},{20,24},{24,20},{28,16},{1,13},{... | collective-permute-start | bytes 3145736 | tf_op jit(solution)/shard_map/ppermute | solution.py:216
  120.2 47.7 %collective-permute-start.12 = (bf16[2,272,128]{2,1,0:T(8,128)(2,1)S(1)}, bf16[2,272,128]{2,1,0:T(8,128)(2,1)S(1)}, u32[]{:S(2)}, u32[]{:S(2)}) collective-permute-start(bf16[2,272,128]{2,1,0:T(8,128)(2,1)S(1)} %copy-done.58), channel_id=1, source_target_pairs={{0,16},{4,20},{8,24},{12,28},{16,0},{20,4},{24,8},{28,12},{1,17},{... | collective-permute-start | bytes 417800 | tf_op jit(solution)/shard_map/ppermute | solution.py:216
  207.8 71.0 %collective-permute-start.19 = (bf16[4,272,256]{2,1,0:T(8,128)(2,1)}, bf16[4,272,256]{2,1,0:T(8,128)(2,1)}, u32[]{:S(2)}, u32[]{:S(2)}) collective-permute-start(bf16[4,272,256]{2,1,0:T(8,128)(2,1)} %get-tuple-element.102), channel_id=1, source_target_pairs={{0,1},{1,0},{2,3},{3,2},{4,5},{5,4},{6,7},{7,6},{8,9},{9,8},{10,11... | collective-permute-start | bytes 1671176 | tf_op jit(solution)/shard_map/ppermute | solution.py:219
  208.4 107.9 %collective-permute-start.13 = (bf16[4,128,1024]{2,1,0:T(8,128)(2,1)}, bf16[4,128,1024]{2,1,0:T(8,128)(2,1)S(1)}, u32[]{:S(2)}, u32[]{:S(2)}) collective-permute-start(bf16[4,128,1024]{2,1,0:T(8,128)(2,1)} %get-tuple-element.96), channel_id=1, source_target_pairs={{0,4},{4,0},{8,12},{12,8},{16,20},{20,16},{24,28},{28,24},{1,5},{5... | collective-permute-start | bytes 3145736 | tf_op jit(solution)/shard_map/ppermute | solution.py:216
  208.4 108.4 %collective-permute-start.14 = (bf16[4,128,1024]{2,1,0:T(8,128)(2,1)}, bf16[4,128,1024]{2,1,0:T(8,128)(2,1)S(1)}, u32[]{:S(2)}, u32[]{:S(2)}) collective-permute-start(bf16[4,128,1024]{2,1,0:T(8,128)(2,1)} %get-tuple-element.97), channel_id=1, source_target_pairs={{0,8},{4,12},{8,0},{12,4},{16,24},{20,28},{24,16},{28,20},{1,9},{5... | collective-permute-start | bytes 3145736 | tf_op jit(solution)/shard_map/ppermute | solution.py:216
  212.4 104.4 %collective-permute-start.15 = (bf16[4,128,1024]{2,1,0:T(8,128)(2,1)}, bf16[4,128,1024]{2,1,0:T(8,128)(2,1)S(1)}, u32[]{:S(2)}, u32[]{:S(2)}) collective-permute-start(bf16[4,128,1024]{2,1,0:T(8,128)(2,1)} %get-tuple-element.98.refs_6_), channel_id=1, source_target_pairs={{0,12},{4,8},{8,4},{12,0},{16,28},{20,24},{24,20},{28,16},{1,13},{... | collective-permute-start | bytes 3145736 | tf_op jit(solution)/shard_map/ppermute | solution.py:216
  212.5 48.6 %collective-permute-start.26 = (bf16[2,272,128]{2,1,0:T(8,128)(2,1)S(1)}, bf16[2,272,128]{2,1,0:T(8,128)(2,1)S(1)}, u32[]{:S(2)}, u32[]{:S(2)}) collective-permute-start(bf16[2,272,128]{2,1,0:T(8,128)(2,1)S(1)} %copy-done.48), channel_id=1, source_target_pairs={{0,16},{4,20},{8,24},{12,28},{16,0},{20,4},{24,8},{28,12},{1,17},{... | collective-permute-start | bytes 417800 | tf_op jit(solution)/shard_map/ppermute | solution.py:216
  327.6 52.9 %collective-permute-start.34 = (bf16[4,128,1024]{2,1,0:T(8,128)(2,1)}, bf16[4,128,1024]{2,1,0:T(8,128)(2,1)S(1)}, u32[]{:S(2)}, u32[]{:S(2)}) collective-permute-start(bf16[4,128,1024]{2,1,0:T(8,128)(2,1)} %get-tuple-element.113), channel_id=1, source_target_pairs={{0,4},{4,0},{8,12},{12,8},{16,20},{20,16},{24,28},{28,24},{1,5},{5... | collective-permute-start | bytes 3145736 | tf_op jit(solution)/shard_map/ppermute | solution.py:216
  327.6 61.4 %collective-permute-start.35 = (bf16[4,128,1024]{2,1,0:T(8,128)(2,1)}, bf16[4,128,1024]{2,1,0:T(8,128)(2,1)S(1)}, u32[]{:S(2)}, u32[]{:S(2)}) collective-permute-start(bf16[4,128,1024]{2,1,0:T(8,128)(2,1)} %get-tuple-element.114), channel_id=1, source_target_pairs={{0,8},{4,12},{8,0},{12,4},{16,24},{20,28},{24,16},{28,20},{1,9},{5... | collective-permute-start | bytes 3145736 | tf_op jit(solution)/shard_map/ppermute | solution.py:216
  341.6 51.5 %collective-permute-start.36 = (bf16[4,128,1024]{2,1,0:T(8,128)(2,1)}, bf16[4,128,1024]{2,1,0:T(8,128)(2,1)}, u32[]{:S(2)}, u32[]{:S(2)}) collective-permute-start(bf16[4,128,1024]{2,1,0:T(8,128)(2,1)} %get-tuple-element.105.refs_6_), channel_id=1, source_target_pairs={{0,12},{4,8},{8,4},{12,0},{16,28},{20,24},{24,20},{28,16},{1,13},{... | collective-permute-start | bytes 3145736 | tf_op jit(solution)/shard_map/ppermute | solution.py:216
  402.5 52.1 %collective-permute-start.31 = (bf16[4,128,1024]{2,1,0:T(8,128)(2,1)}, bf16[4,128,1024]{2,1,0:T(8,128)(2,1)S(1)}, u32[]{:S(2)}, u32[]{:S(2)}) collective-permute-start(bf16[4,128,1024]{2,1,0:T(8,128)(2,1)} %get-tuple-element.110), channel_id=1, source_target_pairs={{0,4},{4,0},{8,12},{12,8},{16,20},{20,16},{24,28},{28,24},{1,5},{5... | collective-permute-start | bytes 3145736 | tf_op jit(solution)/shard_map/ppermute | solution.py:216
  406.3 62.4 %collective-permute-start.32 = (bf16[4,128,1024]{2,1,0:T(8,128)(2,1)}, bf16[4,128,1024]{2,1,0:T(8,128)(2,1)}, u32[]{:S(2)}, u32[]{:S(2)}) collective-permute-start(bf16[4,128,1024]{2,1,0:T(8,128)(2,1)} %get-tuple-element.111), channel_id=1, source_target_pairs={{0,8},{4,12},{8,0},{12,4},{16,24},{20,28},{24,16},{28,20},{1,9},{5... | collective-permute-start | bytes 3145736 | tf_op jit(solution)/shard_map/ppermute | solution.py:216
  420.4 49.6 %collective-permute-start.33 = (bf16[4,128,1024]{2,1,0:T(8,128)(2,1)}, bf16[4,128,1024]{2,1,0:T(8,128)(2,1)}, u32[]{:S(2)}, u32[]{:S(2)}) collective-permute-start(bf16[4,128,1024]{2,1,0:T(8,128)(2,1)} %get-tuple-element.112.refs_6_), channel_id=1, source_target_pairs={{0,12},{4,8},{8,4},{12,0},{16,28},{20,24},{24,20},{28,16},{1,13},{... | collective-permute-start | bytes 3145736 | tf_op jit(solution)/shard_map/ppermute | solution.py:216
  477.0 60.9 %collective-permute-start.56 = (bf16[4,128,1024]{2,1,0:T(8,128)(2,1)}, bf16[4,128,1024]{2,1,0:T(8,128)(2,1)}, u32[]{:S(2)}, u32[]{:S(2)}) collective-permute-start(bf16[4,128,1024]{2,1,0:T(8,128)(2,1)} %get-tuple-element.130), channel_id=1, source_target_pairs={{0,4},{4,0},{8,12},{12,8},{16,20},{20,16},{24,28},{28,24},{1,5},{5... | collective-permute-start | bytes 3145736 | tf_op jit(solution)/shard_map/ppermute | solution.py:216
  492.9 54.0 %collective-permute-start.58 = (bf16[4,128,1024]{2,1,0:T(8,128)(2,1)}, bf16[4,128,1024]{2,1,0:T(8,128)(2,1)}, u32[]{:S(2)}, u32[]{:S(2)}) collective-permute-start(bf16[4,128,1024]{2,1,0:T(8,128)(2,1)} %get-tuple-element.119.refs_6_), channel_id=1, source_target_pairs={{0,12},{4,8},{8,4},{12,0},{16,28},{20,24},{24,20},{28,16},{1,13},{... | collective-permute-start | bytes 3145736 | tf_op jit(solution)/shard_map/ppermute | solution.py:216
  (132 other events, 2249.6 us)

commit v2 on v1

--- a/solution.py
+++ b/solution.py
@@ -12,7 +12,10 @@
 E = 8
 CAP = 34
 HALVES = 2
+GRAD_STEPS = 4
 LANES = 128
+SUBLANES = 8
+NOWHERE = -1e6
 BF = jnp.bfloat16
 F32 = jnp.float32
 
@@ -131,15 +134,19 @@
         jnp.int32, (tok, tok), 1
     )
     before = jnp.dot(either, jnp.where(earlier, 1.0, 0.0).astype(BF), preferred_element_type=F32)
-    return [jnp.where(hit, before, -1.0) for hit in hits]
-
-
-def slot_hits(rows, e):
-    slot = lax.broadcasted_iota(jnp.int32, (CAP, rows[0].shape[1]), 0).astype(F32)
-    return [jnp.where(slot == rows[k][e : e + 1, :], 1.0, 0.0) for k in range(2)]
-
-
-def route_kernel(routes_ref, weights_ref, tokens_ref, cot_ref, out_ref):
+    return [jnp.where(hit, before, NOWHERE) for hit in hits]
+
+
+def padded(rows):
+    return -(-rows // SUBLANES) * SUBLANES
+
+
+def slot_hits(rows, e, count=CAP, base=0):
+    slot = lax.broadcasted_iota(jnp.int32, (count, rows[0].shape[1]), 0).astype(F32)
+    return [jnp.where(slot == rows[k][e : e + 1, :] + base, 1.0, 0.0) for k in range(2)]
+
+
+def route_kernel(routes_ref, weights_ref, tokens_ref, cot_ref, out_ref, wide_ref):
     features = tokens_ref.shape[1]
     size = out_ref.shape[0] // HALVES
     half = features // HALVES
@@ -148,22 +155,26 @@
         at = slot_hits(rows, e)
         pick = (at[0] + at[1]).astype(BF)
         scale = jnp.sum(at[0] * weights_ref[0:1, :] + at[1] * weights_ref[1:2, :], 1, keepdims=True)
-        x_rows = jnp.dot(pick, tokens_ref[...], preferred_element_type=F32).astype(BF)
-        d_rows = (scale * jnp.dot(pick, cot_ref[...], preferred_element_type=F32)).astype(BF)
+        x_rows = jnp.dot(pick, tokens_ref[...], preferred_element_type=F32)
+        d_rows = scale * jnp.dot(pick, cot_ref[...], preferred_element_type=F32)
         other = e ^ size
         cut = (other // size) * half
         for i, value in enumerate((x_rows, d_rows)):
-            out_ref[e, :, i * features : (i + 1) * features] = value
-            out_ref[other, :, 2 * features + i * half : 2 * features + (i + 1) * half] = value[
-                :, cut : cut + half
-            ]
+            wide_ref[e, i * CAP : (i + 1) * CAP, :] = value
+            wide_ref[other, 2 * CAP : 3 * CAP, i * half : (i + 1) * half] = value[:, cut : cut + half]
+    extra = out_ref.shape[1] - 3 * CAP
+    for e in range(E):
+        if extra:
+            wide_ref[e, 3 * CAP :, :] = jnp.zeros((extra, features), F32)
+        out_ref[e] = wide_ref[e].astype(BF)
 
 
 def route(routes_t, weights_t, tokens, cotangent, dp_count):
     features = tokens.shape[1]
     return pl.pallas_call(
         route_kernel,
-        out_shape=jax.ShapeDtypeStruct((dp_count, CAP, 3 * features), BF),
+        out_shape=jax.ShapeDtypeStruct((dp_count, padded(3 * CAP), features), BF),
+        scratch_shapes=[pltpu.VMEM((dp_count, padded(3 * CAP), features), F32)],
         cost_estimate=pl.CostEstimate(
             flops=4 * E * CAP * tokens.size, bytes_accessed=2 * 10 * tokens.size, transcendentals=0
         ),
@@ -171,25 +182,25 @@
     )(routes_t, weights_t, tokens, cotangent)
 
 
-def returned_rows(ref, e, half, kind):
-    size, width = ref.shape[0] // HALVES, ref.shape[2] // 4
-    if e // size == half:
-        return ref[e, :, kind * width : (kind + 1) * width]
-    return ref[e ^ size, :, (2 + kind) * width : (3 + kind) * width]
+def returned(size, e, half, kind):
+    near = e // size == half
+    return (e if near else e ^ size), (kind if near else 2 + kind) * CAP
 
 
 def mix_kernel(routes_ref, weights_ref, back_ref, mixed_ref, grad_ref):
     tok = routes_ref.shape[1]
     rows = slot_rows(routes_ref)
-    width = back_ref.shape[2] // 4
+    owners, count, width = back_ref.shape
     for half in range(HALVES):
         first, second, grad = [jnp.zeros((tok, width), F32) for _ in range(3)]
         for e in range(E):
-            at = [hit.astype(BF) for hit in slot_hits(rows, e)]
-            y_rows = returned_rows(back_ref, e, half, 0)
-            first += contract(at[0], y_rows, 0, 0)
-            second += contract(at[1], y_rows, 0, 0)
-            grad += contract(at[0] + at[1], returned_rows(back_ref, e, half, 1), 0, 0)
+            owner, base = returned(owners // HALVES, e, half, 0)
+            at = slot_hits(rows, e, count, base)
+            first += contract(at[0].astype(BF), back_ref[owner], 0, 0)
+            second += contract(at[1].astype(BF), back_ref[owner], 0, 0)
+            owner, base = returned(owners // HALVES, e, half, 1)
+            at = slot_hits(rows, e, count, base)
+            grad += contract((at[0] + at[1]).astype(BF), back_ref[owner], 0, 0)
         lanes = slice(half * width, (half + 1) * width)
         mixed_ref[:, lanes] = (weights_ref[:, 0:1] * first + weights_ref[:, 1:2] * second).astype(BF)
         grad_ref[:, lanes] = grad.astype(BF)
@@ -246,13 +257,17 @@
 
 
 def prepare(plan, got):
-    features = got.shape[2] // 3
+    features = got.shape[2]
     half, share, slots = plan.group_features, plan.share, plan.slots
 
     def kernel(where, got_ref, own_ref, rows_ref, wide_ref):
         place, group = where[0] % plan.size, where[0] // plan.size
         for b in range(plan.dp_count):
-            wide_ref[b * CAP : (b + 1) * CAP, :] = got_ref[b].astype(F32)
+            value = got_ref[b].astype(F32)
+            for i in range(3):
+                wide_ref[b * CAP : (b + 1) * CAP, i * features : (i + 1) * features] = value[
+                    i * CAP : (i + 1) * CAP
+                ]
         for i in range(2):
             own_ref[i] = wide_ref[:, i * features : (i + 1) * features].astype(BF)
             for k in range(plan.size):
@@ -272,8 +287,8 @@
             jax.ShapeDtypeStruct((2, slots, features), BF),
             jax.ShapeDtypeStruct((4, slots, half), BF),
         ],
-        (0, 6 * got.size),
-        scratch=[pltpu.VMEM((slots, got.shape[2]), F32)],
+        (0, 4 * got.size),
+        scratch=[pltpu.VMEM((slots, 3 * features), F32)],
     )
 
 
@@ -353,66 +368,61 @@
     )
 
 
-def sum_away(plan, parts):
+def sum_members(plan, parts):
     _, slots, sub = parts[0].shape
 
     def kernel(where, *refs):
         del where
-        total = refs[0][0].astype(F32)
+        total = refs[0][...].astype(F32)
         for ref in refs[1 : plan.members]:
-            total += ref[0].astype(F32)
-        refs[-1][0] = total.astype(BF)
-
+            total += ref[...].astype(F32)
+        refs[-1][...] = total.astype(BF)
+
+    spec = pl.BlockSpec((2, slots, sub), lambda p, where: (p, 0, 0))
     return plan.call(
         kernel,
-        (2,),
-        [pl.BlockSpec((1, slots, sub), lambda q, where: (2 + q, 0, 0))] * plan.members,
+        (HALVES,),
+        [spec] * plan.members,
         parts,
-        [pl.BlockSpec((1, slots, sub), lambda q, where: (q, 0, 0))],
-        [jax.ShapeDtypeStruct((2, slots, sub), BF)],
-        (0, 4 * slots * sub * (plan.members + 1)),
+        [spec],
+        [jax.ShapeDtypeStruct((4, slots, sub), BF)],
+        (0, 8 * slots * sub * (plan.members + 1)),
     )[0]
 
 
-def activate(plan, parts, back):
-    _, slots, sub = parts[0].shape
-    lanes = min(sub, 2 * LANES)
-
-    def kernel(where, *refs):
+def activate(plan, sums, back):
+    _, slots, sub = sums.shape
+
+    def kernel(where, sums_ref, back_ref, *refs):
         del where
-        sums = []
-        for i in range(2):
-            total = refs[plan.members][i].astype(F32)
-            for ref in refs[: plan.members]:
-                total += ref[i].astype(F32)
-            sums.append(total)
-        pre, d_act = sums
+        pre, d_act = [sums_ref[i].astype(F32) + back_ref[i].astype(F32) for i in range(2)]
         sigma = 1.0 / (1.0 + jnp.exp(-pre))
         refs[-1][0] = (pre * sigma).astype(BF)
         refs[-1][1] = (d_act * sigma * (1.0 + pre * (1.0 - sigma))).astype(BF)
 
-    spec = pl.BlockSpec((2, slots, lanes), lambda q, where: (0, 0, q))
+    spec = pl.BlockSpec((2, slots, sub), lambda p, where: (p, 0, 0))
     return plan.call(
         kernel,
-        (sub // lanes,),
-        [spec] * (plan.members + 1),
-        [*parts, back],
+        (HALVES,),
+        [spec, pl.BlockSpec((2, slots, sub), lambda p, where: (1 - p, 0, 0))],
+        [sums, back],
         [spec],
-        [jax.ShapeDtypeStruct((2, slots, sub), BF)],
-        (0, 4 * slots * sub * (plan.members + 2)),
+        [jax.ShapeDtypeStruct((4, slots, sub), BF)],
+        (0, 24 * slots * sub),
     )[0]
 
 
 def feature_sums(plan, total, pieces, up, down, came, start, width, final):
     sub = width // plan.members
     half, share, slots = plan.group_features, plan.share, plan.slots
+    count = padded(4 * CAP)
 
     def kernel(where, *refs):
         place = where[0] % plan.size
         p_refs = refs[: plan.members]
         w_refs = refs[plan.members : plan.members + 2 + plan.peers]
         before = refs[plan.members + 2 + plan.peers]
-        out = refs[-2] if final else refs[-1]
+        out, acc, wide = refs[-3:] if final else (refs[-1], None, None)
         for i in range(2):
             value = None
             for m in range(plan.members):
@@ -425,14 +435,25 @@
                 if total is not None:
                     piece += before[i, :, at]
                 if final:
-                    refs[-1][:, at] = piece
+                    acc[:, at] = piece
                 else:
                     out[i, :, at] = piece
             if final:
+                for p in range(HALVES):
+
+                    @pl.when(pl.program_id(0) == p)
+                    def _(first=(2 * p + i) * CAP):
+                        for b in range(plan.dp_count):
+                            wide[b, first : first + CAP, :] = acc[b * CAP : (b + 1) * CAP, :]
+
+        if final:
+
+            @pl.when(pl.program_id(0) == HALVES - 1)
+            def _():
                 for b in range(plan.dp_count):
-                    out[b, :, i * half : (i + 1) * half] = refs[-1][
-                        b * CAP : (b + 1) * CAP, :
-                    ].astype(BF)
+                    if count > 4 * CAP:
+                        wide[b, 4 * CAP :, :] = jnp.zeros((count - 4 * CAP, half), F32)
+                    out[b] = wide[b].astype(BF)
 
     stack = pl.BlockSpec((2, slots, half), lambda p, where: (p, 0, 0))
     in_specs = [
@@ -443,10 +464,11 @@
         in_specs.append(stack)
         args.append(total)
     if final:
-        out_spec = pl.BlockSpec((plan.dp_count, CAP, 2 * half), lambda p, where: (0, 0, p))
-        out = jax.ShapeDtypeStruct((plan.dp_count, CAP, 4 * half), BF)
+        shape = (plan.dp_count, count, half)
+        out_spec, out = full_spec(shape), jax.ShapeDtypeStruct(shape, BF)
+        scratch = [pltpu.VMEM((slots, half), F32), pltpu.VMEM(shape, F32)]
     else:
-        out_spec, out = stack, jax.ShapeDtypeStruct((4, slots, half), F32)
+        out_spec, out, scratch = stack, jax.ShapeDtypeStruct((4, slots, half), F32), ()
     return plan.call(
         kernel,
         (HALVES,),
@@ -455,14 +477,14 @@
         [out_spec],
         [out],
         (8 * slots * half * width, 8 * width * (slots + half) + 32 * slots * half),
-        scratch=[pltpu.VMEM((slots, half), F32)] if final else (),
+        scratch=scratch,
     )[0]
 
 
 def weight_grads(plan, buffers, x_t, d_t, pieces, start, width):
     sub = width // plan.members
     features, slots = x_t.shape
-    block = features // 2
+    block = features // GRAD_STEPS
 
     def kernel(where, x_ref, d_ref, *refs):
         up_out, down_out = refs[-2:]
@@ -485,7 +507,7 @@
         args += buffers
     return plan.call(
         kernel,
-        (2,),
+        (GRAD_STEPS,),
         in_specs,
         args,
         [pl.BlockSpec((1, block, width), lambda q, where: (0, q, start // width))] * 2,
@@ -505,12 +527,11 @@
 
 LAGS = (
     ("hidden", 0),
-    ("spread", 2),
+    ("features", 3),
+    ("grads", 5),
     ("activate", 1),
-    ("features", 3),
-    ("away", 0),
+    ("sums", 0),
     ("fetch", -2),
-    ("grads", 5),
 )
 
 
@@ -535,7 +556,7 @@
     count = len(chunks)
     routes_t, weights_t = routes.T, route_weights.T
 
-    came, reduced, backs, owns, others, pieces = {}, {}, {}, {}, {}, {}
+    came, reduced, summed, backs, pieces = {}, {}, {}, {}, {}
     got = own = rows = total = grads = back = None
     for kind, i in order_of(count):
         if kind == "fetch":
@@ -546,12 +567,10 @@
             own, rows = prepare(plan, got)
         elif kind == "hidden":
             outs = hidden_partials(plan, rows, up, down, came[i], *chunks[i])
-        elif kind == "away":
-            away = sum_away(plan, reduced[i])
+        elif kind == "sums":
+            summed[i] = sum_members(plan, reduced[i])
         elif kind == "activate":
-            owns[i] = activate(plan, reduced[i], backs[i])
-        elif kind == "spread":
-            both = jnp.concatenate([owns[i], others[i]], axis=0)
+            acts = activate(plan, summed[i], backs[i])
         elif kind == "features":
             total = feature_sums(
                 plan, total, pieces[i], up, down, came[i], *chunks[i], i == count - 1
@@ -566,12 +585,10 @@
             x_t, d_t = own[0].T, own[1].T
         elif kind == "hidden":
             reduced[i] = [outs[0]] + [plan.pass_on(outs[k], k) for k in range(1, members)]
-        elif kind == "away":
-            backs[i] = plan.swap(away, plan.size)
+        elif kind == "sums":
+            backs[i] = plan.swap(summed[i], plan.size)
         elif kind == "activate":
-            others[i] = plan.swap(owns[i], plan.size)
-        elif kind == "spread":
-            pieces[i] = [both] + [plan.pass_on(both, k) for k in range(1, members)]
+            pieces[i] = [acts] + [plan.pass_on(acts, k) for k in range(1, members)]
         elif kind == "return":
             back = lax.all_to_all(total, "dp", split_axis=0, concat_axis=0, tiled=True)
 

time: 758 us -> 660 us (0.87); the launches traced: 747 us -> 658 us
  waiting for transfers between devices: 392 us -> 306 us
    all_to_all x1, waiting for transfers between devices: 34 us -> 0.01 us  [halves_body(): got = lax.all_to_all(send, 'dp', split_axis=0, concat_axis=0, tiled=True)]
    ppermute x40 -> x32, waiting for transfers between devices: 193 us -> 164 us  [swap(): return lax.ppermute(value, 'dp', [(i, i ^ k) for i in range(self.dp_count)])]
    ppermute x48, waiting for transfers between devices: 150 us -> 134 us  [pass_on(): lax.ppermute(value, 'member', [(i, i ^ k) for i in range(self.members)])]
    ppermute x40 -> x32, starting transfers between devices: 33.2 us -> 35.4 us  [swap(): return lax.ppermute(value, 'dp', [(i, i ^ k) for i in range(self.dp_count)])]
  transfers between devices with their start and end apart: 90 -> 82, of which waited for: 29 -> 29; matrix products, arithmetic and copies ran while one was open for 1% -> 1% of each run, Pallas kernels for 26% -> 32%
where the time goes in v2:
time: 660 us; the launch traced here: 658 us
  waiting for transfers between devices  306 us (46%)
  Pallas kernels  227 us (34%)
  starting transfers between devices  108 us (16%)
  local copies, waits for them, and re-layouts  14.9 us (2%)
    pallas_call x49, Pallas kernels, call(): pl.pallas_call(placed, grid_spec=pltpu.PrefetchScalarGridSpec(num_scalar_...  220 us
    ppermute x32, waiting for transfers between devices, swap(): return lax.ppermute(value, 'dp', [(i, i ^ k) for i in range(self.dp_count)])  164 us
    ppermute x48, waiting for transfers between devices, pass_on(): lax.ppermute(value, 'member', [(i, i ^ k) for i in range(self.members)])  134 us
    ppermute x48, starting transfers between devices, pass_on(): lax.ppermute(value, 'member', [(i, i ^ k) for i in range(self.members)])  61.2 us
    ppermute x32, starting transfers between devices, swap(): return lax.ppermute(value, 'dp', [(i, i ^ k) for i in range(self.dp_count)])  35.4 us
  transfers between devices with their start and end apart: 82, of which 29 were waited for; matrix products, arithmetic and copies ran while one was open for 1% of the time, Pallas kernels for 32%

profile of v2, /device:TPU:0, one launch (start us, length us, event | category | flops | bytes accessed | tf_op | source)
XLA Modules:
  0.0 657.8 jit_solution(7736547061597126272)
XLA Ops:
  3.8 6.4 all-to-all-start
  22.5 28.9 %collective-permute-done.5.refs_4_.refs_8_ = bf16[4,128,512]{2,1,0:T(8,128)(2,1)S(1)} collective-permute-done((bf16[4,128,512]{2,1,0:T(8,128)(2,1)}, bf16[4,128,512]{2,1,0:T(8,128)(2,1)S(1)}, u32[]{:S(2)}, u32[]{:S(2)}) %collective-permute-start.5) | collective-permute-done | bytes 524320 | tf_op jit(solution)/shard_map/ppermute | solution.py:227
  91.3 17.0 %collective-permute-done.1.refs_4_.refs_7_ = bf16[4,128,1024]{2,1,0:T(8,128)(2,1)} collective-permute-done((bf16[4,128,1024]{2,1,0:T(8,128)(2,1)}, bf16[4,128,1024]{2,1,0:T(8,128)(2,1)}, u32[]{:S(2)}, u32[]{:S(2)}) %collective-permute-start.1) | collective-permute-done | bytes 1048608 | tf_op jit(solution)/shard_map/ppermute | solution.py:227
  119.1 47.9 %collective-permute-done.12.refs_1_ = bf16[4,272,128]{2,1,0:T(8,128)(2,1)S(1)} collective-permute-done((bf16[4,272,128]{2,1,0:T(8,128)(2,1)S(1)}, bf16[4,272,128]{2,1,0:T(8,128)(2,1)S(1)}, u32[]{:S(2)}, u32[]{:S(2)}) %collective-permute-start.12) | collective-permute-done | bytes 278560 | tf_op jit(solution)/shard_map/ppermute | solution.py:227
  172.2 12.1 %collective-permute-done.11.refs_3_ = bf16[4,272,256]{2,1,0:T(8,128)(2,1)S(1)} collective-permute-done((bf16[4,272,256]{2,1,0:T(8,128)(2,1)}, bf16[4,272,256]{2,1,0:T(8,128)(2,1)S(1)}, u32[]{:S(2)}, u32[]{:S(2)}) %collective-permute-start.11) | collective-permute-done | bytes 557088 | tf_op jit(solution)/shard_map/ppermute | solution.py:230
  184.3 9.8 %collective-permute-done.9.refs_1_ = bf16[4,272,256]{2,1,0:T(8,128)(2,1)} collective-permute-done((bf16[4,272,256]{2,1,0:T(8,128)(2,1)}, bf16[4,272,256]{2,1,0:T(8,128)(2,1)}, u32[]{:S(2)}, u32[]{:S(2)}) %collective-permute-start.9) | collective-permute-done | bytes 557088 | tf_op jit(solution)/shard_map/ppermute | solution.py:230
  214.5 14.1 %collective-permute-done.22.refs_1_ = bf16[4,272,256]{2,1,0:T(8,128)(2,1)} collective-permute-done((bf16[4,272,256]{2,1,0:T(8,128)(2,1)S(1)}, bf16[4,272,256]{2,1,0:T(8,128)(2,1)}, u32[]{:S(2)}, u32[]{:S(2)}) %collective-permute-start.22) | collective-permute-done | bytes 557088 | tf_op jit(solution)/shard_map/ppermute | solution.py:227
  234.3 19.1 %collective-permute-done.20.refs_2_ = bf16[4,272,256]{2,1,0:T(8,128)(2,1)S(1)} collective-permute-done((bf16[4,272,256]{2,1,0:T(8,128)(2,1)}, bf16[4,272,256]{2,1,0:T(8,128)(2,1)S(1)}, u32[]{:S(2)}, u32[]{:S(2)}) %collective-permute-start.20) | collective-permute-done | bytes 557088 | tf_op jit(solution)/shard_map/ppermute | solution.py:230
  264.9 9.9 %collective-permute-done.15.refs_5_.refs_8_ = bf16[4,128,1024]{2,1,0:T(8,128)(2,1)} collective-permute-done((bf16[4,128,1024]{2,1,0:T(8,128)(2,1)}, bf16[4,128,1024]{2,1,0:T(8,128)(2,1)}, u32[]{:S(2)}, u32[]{:S(2)}) %collective-permute-start.15) | collective-permute-done | bytes 1048608 | tf_op jit(solution)/shard_map/ppermute | solution.py:227
  285.6 9.6 %collective-permute-done.23.refs_1_ = bf16[4,272,256]{2,1,0:T(8,128)(2,1)S(1)} collective-permute-done((bf16[4,272,256]{2,1,0:T(8,128)(2,1)}, bf16[4,272,256]{2,1,0:T(8,128)(2,1)S(1)}, u32[]{:S(2)}, u32[]{:S(2)}) %collective-permute-start.23) | collective-permute-done | bytes 557088 | tf_op jit(solution)/shard_map/ppermute | solution.py:230
  299.1 12.7 %collective-permute-done.25.refs_3_ = bf16[4,272,256]{2,1,0:T(8,128)(2,1)S(1)} collective-permute-done((bf16[4,272,256]{2,1,0:T(8,128)(2,1)}, bf16[4,272,256]{2,1,0:T(8,128)(2,1)S(1)}, u32[]{:S(2)}, u32[]{:S(2)}) %collective-permute-start.25) | collective-permute-done | bytes 557088 | tf_op jit(solution)/shard_map/ppermute | solution.py:230
  340.9 8.7 %collective-permute-done.39.refs_1_ = bf16[4,272,256]{2,1,0:T(8,128)(2,1)} collective-permute-done((bf16[4,272,256]{2,1,0:T(8,128)(2,1)}, bf16[4,272,256]{2,1,0:T(8,128)(2,1)}, u32[]{:S(2)}, u32[]{:S(2)}) %collective-permute-start.39) | collective-permute-done | bytes 557088 | tf_op jit(solution)/shard_map/ppermute | solution.py:227
  354.7 18.0 %collective-permute-done.37.refs_2_ = bf16[4,272,256]{2,1,0:T(8,128)(2,1)S(1)} collective-permute-done((bf16[4,272,256]{2,1,0:T(8,128)(2,1)}, bf16[4,272,256]{2,1,0:T(8,128)(2,1)S(1)}, u32[]{:S(2)}, u32[]{:S(2)}) %collective-permute-start.37) | collective-permute-done | bytes 557088 | tf_op jit(solution)/shard_map/ppermute | solution.py:230
  414.4 8.3 %collective-permute-done.46.refs_1_ = bf16[4,272,256]{2,1,0:T(8,128)(2,1)} collective-permute-done((bf16[4,272,256]{2,1,0:T(8,128)(2,1)S(1)}, bf16[4,272,256]{2,1,0:T(8,128)(2,1)}, u32[]{:S(2)}, u32[]{:S(2)}) %collective-permute-start.46) | collective-permute-done | bytes 557088 | tf_op jit(solution)/shard_map/ppermute | solution.py:227
  428.5 19.6 %collective-permute-done.44.refs_2_ = bf16[4,272,256]{2,1,0:T(8,128)(2,1)} collective-permute-done((bf16[4,272,256]{2,1,0:T(8,128)(2,1)}, bf16[4,272,256]{2,1,0:T(8,128)(2,1)}, u32[]{:S(2)}, u32[]{:S(2)}) %collective-permute-start.44) | collective-permute-done | bytes 557088 | tf_op jit(solution)/shard_map/ppermute | solution.py:230
  486.1 12.5 %collective-permute-done.51.refs_4_.refs_7_ = bf16[4,128,512]{2,1,0:T(8,128)(2,1)} collective-permute-done((bf16[4,128,512]{2,1,0:T(8,128)(2,1)}, bf16[4,128,512]{2,1,0:T(8,128)(2,1)}, u32[]{:S(2)}, u32[]{:S(2)}) %collective-permute-start.51) | collective-permute-done | bytes 524320 | tf_op jit(solution)/shard_map/ppermute | solution.py:227
  510.4 6.7 %shard_map.125 = (bf16[1,1024,7168]{2,1,0:T(8,128)(2,1)}, bf16[1,1024,7168]{2,1,0:T(8,128)(2,1)}) custom-call(s32[2]{0:T(128)} %pad_add_fusion.where, bf16[1024,272]{1,0:T(8,128)(2,1)} %get-tuple-element.157.refs_0_.x_ref, bf16[1024,272]{1,0:T(8,128)(2,1)} %get-tuple-element.156.refs_1_.d_ref, ...), custom_call_target="tpu_custom_call", output_to_operand_aliasing={{0}: (7, {}), {1}: (8, {})} | custom-call | flops 1140850688 | bytes 5308416 | tf_op jit(solution)/shard_map/pallas_call | solution.py:242
  538.4 9.9 %collective-permute-done.71.refs_1_.refs_3_ = bf16[4,272,256]{2,1,0:T(8,128)(2,1)S(1)} collective-permute-done((bf16[4,272,256]{2,1,0:T(8,128)(2,1)}, bf16[4,272,256]{2,1,0:T(8,128)(2,1)S(1)}, u32[]{:S(2)}, u32[]{:S(2)}) %collective-permute-start.71) | collective-permute-done | bytes 557088 | tf_op jit(solution)/shard_map/ppermute | solution.py:230
  559.3 6.9 %shard_map.130 = (bf16[1,1024,7168]{2,1,0:T(8,128)(2,1)}, bf16[1,1024,7168]{2,1,0:T(8,128)(2,1)}) custom-call(s32[2]{0:T(128)} %pad_add_fusion.where, bf16[1024,272]{1,0:T(8,128)(2,1)} %get-tuple-element.157.refs_0_.x_ref, bf16[1024,272]{1,0:T(8,128)(2,1)} %get-tuple-element.156.refs_1_.d_ref, ...), custom_call_target="tpu_custom_call", output_to_operand_aliasing={{0}: (7, {}), {1}: (8, {})} | custom-call | flops 1140850688 | bytes 5308416 | tf_op jit(solution)/shard_map/pallas_call | solution.py:242
  584.5 6.7 %shard_map.134 = (bf16[1,1024,7168]{2,1,0:T(8,128)(2,1)}, bf16[1,1024,7168]{2,1,0:T(8,128)(2,1)}) custom-call(s32[2]{0:T(128)} %pad_add_fusion.where, bf16[1024,272]{1,0:T(8,128)(2,1)} %get-tuple-element.157.refs_0_.x_ref, bf16[1024,272]{1,0:T(8,128)(2,1)} %get-tuple-element.156.refs_1_.d_ref, ...), custom_call_target="tpu_custom_call", output_to_operand_aliasing={{0}: (7, {}), {1}: (8, {})} | custom-call | flops 1140850688 | bytes 5308416 | tf_op jit(solution)/shard_map/pallas_call | solution.py:242
  605.8 6.6 %shard_map.137 = (bf16[1,1024,7168]{2,1,0:T(8,128)(2,1)}, bf16[1,1024,7168]{2,1,0:T(8,128)(2,1)}) custom-call(s32[2]{0:T(128)} %pad_add_fusion.where, bf16[1024,272]{1,0:T(8,128)(2,1)} %get-tuple-element.157.refs_0_.x_ref, bf16[1024,272]{1,0:T(8,128)(2,1)} %get-tuple-element.156.refs_1_.d_ref, ...), custom_call_target="tpu_custom_call", output_to_operand_aliasing={{0}: (7, {}), {1}: (8, {})} | custom-call | flops 1140850688 | bytes 5308416 | tf_op jit(solution)/shard_map/pallas_call | solution.py:242
  625.5 6.7 %shard_map.139 = (bf16[1,1024,7168]{2,1,0:T(8,128)(2,1)}, bf16[1,1024,7168]{2,1,0:T(8,128)(2,1)}) custom-call(s32[2]{0:T(128)} %pad_add_fusion.where, bf16[1024,272]{1,0:T(8,128)(2,1)} %get-tuple-element.157.refs_0_.x_ref, bf16[1024,272]{1,0:T(8,128)(2,1)} %get-tuple-element.156.refs_1_.d_ref, ...), custom_call_target="tpu_custom_call", output_to_operand_aliasing={{0}: (7, {}), {1}: (8, {})} | custom-call | flops 1140850688 | bytes 5308416 | tf_op jit(solution)/shard_map/pallas_call | solution.py:242
  632.2 6.6 %shard_map.140 = (bf16[1,1024,7168]{2,1,0:T(8,128)(2,1)}, bf16[1,1024,7168]{2,1,0:T(8,128)(2,1)}) custom-call(s32[2]{0:T(128)} %pad_add_fusion.where, bf16[1024,272]{1,0:T(8,128)(2,1)} %get-tuple-element.157.refs_0_.x_ref, bf16[1024,272]{1,0:T(8,128)(2,1)} %get-tuple-element.156.refs_1_.d_ref, ...), custom_call_target="tpu_custom_call", output_to_operand_aliasing={{0}: (7, {}), {1}: (8, {})} | custom-call | flops 1140850688 | bytes 5308416 | tf_op jit(solution)/shard_map/pallas_call | solution.py:242
  644.4 8.3 %all-to-all-done.1.back_ref = bf16[8,136,512]{2,1,0:T(8,128)(2,1)S(1)} async-done(((bf16[8,136,512]{2,1,0:T(8,128)(2,1)}), bf16[8,136,512]{2,1,0:T(8,128)(2,1)S(1)}, u32[]{:S(2)}, u32[]{:S(2)}) %all-to-all-start.1) | async-done | bytes 1114144 | tf_op jit(solution)/shard_map/all_to_all | solution.py:593
  (303 shorter events, 344.0 us)
Async XLA Ops:
  3.8 48.4 %all-to-all-start = ((bf16[8,104,1024]{2,1,0:T(8,128)(2,1)}), bf16[8,104,1024]{2,1,0:T(8,128)(2,1)S(1)}, u32[]{:S(2)}, u32[]{:S(2)}) async-start(bf16[8,104,1024]{2,1,0:T(8,128)(2,1)} %route.1), calls=%async_computation | async-start | bytes 3407872 | tf_op jit(solution)/shard_map/all_to_all | solution.py:583
  15.9 41.7 %collective-permute-start.3 = (bf16[4,128,512]{2,1,0:T(8,128)(2,1)}, bf16[4,128,512]{2,1,0:T(8,128)(2,1)}, u32[]{:S(2)}, u32[]{:S(2)}) collective-permute-start(bf16[4,128,512]{2,1,0:T(8,128)(2,1)} %get-tuple-element.85), channel_id=1, source_target_pairs={{0,4},{4,0},{8,12},{12,8},{16,20},{20,16},{24,28},{28,24},{1,5},{5... | collective-permute-start | bytes 1572872 | tf_op jit(solution)/shard_map/ppermute | solution.py:227
  16.3 47.6 %collective-permute-start.4 = (bf16[4,128,512]{2,1,0:T(8,128)(2,1)}, bf16[4,128,512]{2,1,0:T(8,128)(2,1)}, u32[]{:S(2)}, u32[]{:S(2)}) collective-permute-start(bf16[4,128,512]{2,1,0:T(8,128)(2,1)} %get-tuple-element.86), channel_id=1, source_target_pairs={{0,8},{4,12},{8,0},{12,4},{16,24},{20,28},{24,16},{28,20},{1,9},{5... | collective-permute-start | bytes 1572872 | tf_op jit(solution)/shard_map/ppermute | solution.py:227
  20.3 71.0 %collective-permute-start.2 = (bf16[4,128,1024]{2,1,0:T(8,128)(2,1)}, bf16[4,128,1024]{2,1,0:T(8,128)(2,1)S(1)}, u32[]{:S(2)}, u32[]{:S(2)}) collective-permute-start(bf16[4,128,1024]{2,1,0:T(8,128)(2,1)} %get-tuple-element.81.refs_1_), channel_id=1, source_target_pairs={{0,12},{4,8},{8,4},{12,0},{16,28},{20,24},{24,20},{28,16},{1,13},{... | collective-permute-start | bytes 3145736 | tf_op jit(solution)/shard_map/ppermute | solution.py:227
  21.8 69.5 %collective-permute-start = (bf16[4,128,1024]{2,1,0:T(8,128)(2,1)}, bf16[4,128,1024]{2,1,0:T(8,128)(2,1)}, u32[]{:S(2)}, u32[]{:S(2)}) collective-permute-start(bf16[4,128,1024]{2,1,0:T(8,128)(2,1)} %get-tuple-element.83), channel_id=1, source_target_pairs={{0,4},{4,0},{8,12},{12,8},{16,20},{20,16},{24,28},{28,24},{1,5},{5... | collective-permute-start | bytes 3145736 | tf_op jit(solution)/shard_map/ppermute | solution.py:227
  51.4 56.9 %collective-permute-start.1 = (bf16[4,128,1024]{2,1,0:T(8,128)(2,1)}, bf16[4,128,1024]{2,1,0:T(8,128)(2,1)}, u32[]{:S(2)}, u32[]{:S(2)}) collective-permute-start(bf16[4,128,1024]{2,1,0:T(8,128)(2,1)} %get-tuple-element.84), channel_id=1, source_target_pairs={{0,8},{4,12},{8,0},{12,4},{16,24},{20,28},{24,16},{28,20},{1,9},{5... | collective-permute-start | bytes 3145736 | tf_op jit(solution)/shard_map/ppermute | solution.py:227
  113.3 55.8 %collective-permute-start.10 = (bf16[4,272,256]{2,1,0:T(8,128)(2,1)}, bf16[4,272,256]{2,1,0:T(8,128)(2,1)S(1)}, u32[]{:S(2)}, u32[]{:S(2)}) collective-permute-start(bf16[4,272,256]{2,1,0:T(8,128)(2,1)} %get-tuple-element.94), channel_id=1, source_target_pairs={{0,2},{1,3},{2,0},{3,1},{4,6},{5,7},{6,4},{7,5},{8,10},{9,11},{10,... | collective-permute-start | bytes 1671176 | tf_op jit(solution)/shard_map/ppermute | solution.py:230
  114.8 90.0 %collective-permute-start.16 = (bf16[4,128,1024]{2,1,0:T(8,128)(2,1)}, bf16[4,128,1024]{2,1,0:T(8,128)(2,1)S(1)}, u32[]{:S(2)}, u32[]{:S(2)}) collective-permute-start(bf16[4,128,1024]{2,1,0:T(8,128)(2,1)} %get-tuple-element.99), channel_id=1, source_target_pairs={{0,4},{4,0},{8,12},{12,8},{16,20},{20,16},{24,28},{28,24},{1,5},{5... | collective-permute-start | bytes 3145736 | tf_op jit(solution)/shard_map/ppermute | solution.py:227
  114.8 90.0 %collective-permute-start.17 = (bf16[4,128,1024]{2,1,0:T(8,128)(2,1)}, bf16[4,128,1024]{2,1,0:T(8,128)(2,1)S(1)}, u32[]{:S(2)}, u32[]{:S(2)}) collective-permute-start(bf16[4,128,1024]{2,1,0:T(8,128)(2,1)} %get-tuple-element.100), channel_id=1, source_target_pairs={{0,8},{4,12},{8,0},{12,4},{16,24},{20,28},{24,16},{28,20},{1,9},{5... | collective-permute-start | bytes 3145736 | tf_op jit(solution)/shard_map/ppermute | solution.py:227
  115.2 89.6 %collective-permute-start.18 = (bf16[4,128,1024]{2,1,0:T(8,128)(2,1)}, bf16[4,128,1024]{2,1,0:T(8,128)(2,1)}, u32[]{:S(2)}, u32[]{:S(2)}) collective-permute-start(bf16[4,128,1024]{2,1,0:T(8,128)(2,1)} %get-tuple-element.91.refs_6_), channel_id=1, source_target_pairs={{0,12},{4,8},{8,4},{12,0},{16,28},{20,24},{24,20},{28,16},{1,13},{... | collective-permute-start | bytes 3145736 | tf_op jit(solution)/shard_map/ppermute | solution.py:227
  116.7 50.3 %collective-permute-start.12 = (bf16[4,272,128]{2,1,0:T(8,128)(2,1)S(1)}, bf16[4,272,128]{2,1,0:T(8,128)(2,1)S(1)}, u32[]{:S(2)}, u32[]{:S(2)}) collective-permute-start(bf16[4,272,128]{2,1,0:T(8,128)(2,1)S(1)} %copy-done.20), channel_id=1, source_target_pairs={{0,16},{4,20},{8,24},{12,28},{16,0},{20,4},{24,8},{28,12},{1,17},{... | collective-permute-start | bytes 835592 | tf_op jit(solution)/shard_map/ppermute | solution.py:227
  212.6 46.2 %collective-permute-start.13 = (bf16[4,128,1024]{2,1,0:T(8,128)(2,1)}, bf16[4,128,1024]{2,1,0:T(8,128)(2,1)S(1)}, u32[]{:S(2)}, u32[]{:S(2)}) collective-permute-start(bf16[4,128,1024]{2,1,0:T(8,128)(2,1)} %get-tuple-element.96), channel_id=1, source_target_pairs={{0,4},{4,0},{8,12},{12,8},{16,20},{20,16},{24,28},{28,24},{1,5},{5... | collective-permute-start | bytes 3145736 | tf_op jit(solution)/shard_map/ppermute | solution.py:227
  212.6 47.7 %collective-permute-start.14 = (bf16[4,128,1024]{2,1,0:T(8,128)(2,1)}, bf16[4,128,1024]{2,1,0:T(8,128)(2,1)S(1)}, u32[]{:S(2)}, u32[]{:S(2)}) collective-permute-start(bf16[4,128,1024]{2,1,0:T(8,128)(2,1)} %get-tuple-element.97), channel_id=1, source_target_pairs={{0,8},{4,12},{8,0},{12,4},{16,24},{20,28},{24,16},{28,20},{1,9},{5... | collective-permute-start | bytes 3145736 | tf_op jit(solution)/shard_map/ppermute | solution.py:227
  213.8 61.0 %collective-permute-start.15 = (bf16[4,128,1024]{2,1,0:T(8,128)(2,1)}, bf16[4,128,1024]{2,1,0:T(8,128)(2,1)}, u32[]{:S(2)}, u32[]{:S(2)}) collective-permute-start(bf16[4,128,1024]{2,1,0:T(8,128)(2,1)} %get-tuple-element.98.refs_6_), channel_id=1, source_target_pairs={{0,12},{4,8},{8,4},{12,0},{16,28},{20,24},{24,20},{28,16},{1,13},{... | collective-permute-start | bytes 3145736 | tf_op jit(solution)/shard_map/ppermute | solution.py:227
  280.7 43.9 %collective-permute-start.34 = (bf16[4,128,1024]{2,1,0:T(8,128)(2,1)}, bf16[4,128,1024]{2,1,0:T(8,128)(2,1)S(1)}, u32[]{:S(2)}, u32[]{:S(2)}) collective-permute-start(bf16[4,128,1024]{2,1,0:T(8,128)(2,1)} %get-tuple-element.114), channel_id=1, source_target_pairs={{0,8},{4,12},{8,0},{12,4},{16,24},{20,28},{24,16},{28,20},{1,9},{5... | collective-permute-start | bytes 3145736 | tf_op jit(solution)/shard_map/ppermute | solution.py:227
  280.7 50.9 %collective-permute-start.35 = (bf16[4,128,1024]{2,1,0:T(8,128)(2,1)}, bf16[4,128,1024]{2,1,0:T(8,128)(2,1)}, u32[]{:S(2)}, u32[]{:S(2)}) collective-permute-start(bf16[4,128,1024]{2,1,0:T(8,128)(2,1)} %get-tuple-element.105.refs_6_), channel_id=1, source_target_pairs={{0,12},{4,8},{8,4},{12,0},{16,28},{20,24},{24,20},{28,16},{1,13},{... | collective-permute-start | bytes 3145736 | tf_op jit(solution)/shard_map/ppermute | solution.py:227
  297.6 39.9 %collective-permute-start.40 = (bf16[4,272,256]{2,1,0:T(8,128)(2,1)S(1)}, bf16[4,272,256]{2,1,0:T(8,128)(2,1)S(1)}, u32[]{:S(2)}, u32[]{:S(2)}) collective-permute-start(bf16[4,272,256]{2,1,0:T(8,128)(2,1)S(1)} %copy-done.2), channel_id=1, source_target_pairs={{0,1},{1,0},{2,3},{3,2},{4,5},{5,4},{6,7},{7,6},{8,9},{9,8},{10,11... | collective-permute-start | bytes 1671176 | tf_op jit(solution)/shard_map/ppermute | solution.py:230
  338.9 47.5 %collective-permute-start.31 = (bf16[4,128,1024]{2,1,0:T(8,128)(2,1)}, bf16[4,128,1024]{2,1,0:T(8,128)(2,1)}, u32[]{:S(2)}, u32[]{:S(2)}) collective-permute-start(bf16[4,128,1024]{2,1,0:T(8,128)(2,1)} %get-tuple-element.111), channel_id=1, source_target_pairs={{0,8},{4,12},{8,0},{12,4},{16,24},{20,28},{24,16},{28,20},{1,9},{5... | collective-permute-start | bytes 3145736 | tf_op jit(solution)/shard_map/ppermute | solution.py:227
  340.7 55.0 %collective-permute-start.32 = (bf16[4,128,1024]{2,1,0:T(8,128)(2,1)}, bf16[4,128,1024]{2,1,0:T(8,128)(2,1)}, u32[]{:S(2)}, u32[]{:S(2)}) collective-permute-start(bf16[4,128,1024]{2,1,0:T(8,128)(2,1)} %get-tuple-element.112.refs_6_), channel_id=1, source_target_pairs={{0,12},{4,8},{8,4},{12,0},{16,28},{20,24},{24,20},{28,16},{1,13},{... | collective-permute-start | bytes 3145736 | tf_op jit(solution)/shard_map/ppermute | solution.py:227
  404.0 68.7 %collective-permute-start.53 = (bf16[4,128,1024]{2,1,0:T(8,128)(2,1)}, bf16[4,128,1024]{2,1,0:T(8,128)(2,1)S(1)}, u32[]{:S(2)}, u32[]{:S(2)}) collective-permute-start(bf16[4,128,1024]{2,1,0:T(8,128)(2,1)} %get-tuple-element.129), channel_id=1, source_target_pairs={{0,4},{4,0},{8,12},{12,8},{16,20},{20,16},{24,28},{28,24},{1,5},{5... | collective-permute-start | bytes 3145736 | tf_op jit(solution)/shard_map/ppermute | solution.py:227
  404.0 68.8 %collective-permute-start.54 = (bf16[4,128,1024]{2,1,0:T(8,128)(2,1)}, bf16[4,128,1024]{2,1,0:T(8,128)(2,1)}, u32[]{:S(2)}, u32[]{:S(2)}) collective-permute-start(bf16[4,128,1024]{2,1,0:T(8,128)(2,1)} %get-tuple-element.130), channel_id=1, source_target_pairs={{0,8},{4,12},{8,0},{12,4},{16,24},{20,28},{24,16},{28,20},{1,9},{5... | collective-permute-start | bytes 3145736 | tf_op jit(solution)/shard_map/ppermute | solution.py:227
  410.4 63.6 %collective-permute-start.55 = (bf16[4,128,1024]{2,1,0:T(8,128)(2,1)}, bf16[4,128,1024]{2,1,0:T(8,128)(2,1)}, u32[]{:S(2)}, u32[]{:S(2)}) collective-permute-start(bf16[4,128,1024]{2,1,0:T(8,128)(2,1)} %get-tuple-element.119.refs_6_), channel_id=1, source_target_pairs={{0,12},{4,8},{8,4},{12,0},{16,28},{20,24},{24,20},{28,16},{1,13},{... | collective-permute-start | bytes 3145736 | tf_op jit(solution)/shard_map/ppermute | solution.py:227
  526.1 51.3 %collective-permute-start.72 = (bf16[4,272,256]{2,1,0:T(8,128)(2,1)}, bf16[4,272,256]{2,1,0:T(8,128)(2,1)}, u32[]{:S(2)}, u32[]{:S(2)}) collective-permute-start(bf16[4,272,256]{2,1,0:T(8,128)(2,1)} %shard_map.126.refs_4_.refs_0_.refs_2_), channel_id=1, source_target_pairs={{0,2},{1,3},{2,0},{3,1},{4,6},{5,7},{6,4},{7,5},{8,10},{9,11},{10,... | collective-permute-start | bytes 1671176 | tf_op jit(solution)/shard_map/ppermute | solution.py:230
  537.6 39.9 %collective-permute-start.73 = (bf16[4,272,256]{2,1,0:T(8,128)(2,1)S(1)}, bf16[4,272,256]{2,1,0:T(8,128)(2,1)S(1)}, u32[]{:S(2)}, u32[]{:S(2)}) collective-permute-start(bf16[4,272,256]{2,1,0:T(8,128)(2,1)S(1)} %copy-done.1), channel_id=1, source_target_pairs={{0,3},{1,2},{2,1},{3,0},{4,7},{5,6},{6,5},{7,4},{8,11},{9,10},{10,... | collective-permute-start | bytes 1671176 | tf_op jit(solution)/shard_map/ppermute | solution.py:230
  (112 other events, 1901.9 us)

commit v3 on v2

--- a/solution.py
+++ b/solution.py
@@ -528,10 +528,10 @@
 LAGS = (
     ("hidden", 0),
     ("features", 3),
-    ("grads", 5),
     ("activate", 1),
     ("sums", 0),
     ("fetch", -2),
+    ("grads", 3),
 )
 
 
@@ -540,11 +540,10 @@
     for i in range(count + max(lag for _, lag in LAGS)):
         for kind, lag in LAGS:
             first = 2 if kind == "fetch" else 0
-            if first <= i - lag < count:
+            if first <= i - lag < count and (kind != "grads" or i < count):
                 steps.append((kind, i - lag))
-                if (kind, i - lag) == ("features", count - 1):
-                    steps.append(("return", 0))
-    return steps
+    steps.append(("return", 0))
+    return steps + [("grads", i) for i in range(count) if ("grads", i) not in steps]
 
 
 def halves_body(tokens, routes, route_weights, up, down, cotangent):

time: 660 us -> 673 us (1.020)
  waiting for transfers between devices: 306 us -> 330 us
  starting transfers between devices: 108 us -> 97.4 us
    ppermute x48, waiting for transfers between devices: 134 us -> 170 us  [pass_on(): lax.ppermute(value, 'member', [(i, i ^ k) for i in range(self.members)])]
    ppermute x32, waiting for transfers between devices: 164 us -> 152 us  [swap(): return lax.ppermute(value, 'dp', [(i, i ^ k) for i in range(self.dp_count)])]
  transfers between devices with their start and end apart: 82 -> 82, of which waited for: 29 -> 25; matrix products, arithmetic and copies ran while one was open for 1% -> 1% of each run, Pallas kernels for 32% -> 31%
where the time goes in v3:
time: 673 us; the launch traced here: 671 us
  waiting for transfers between devices  330 us (49%)
  Pallas kernels  227 us (34%)
  starting transfers between devices  97.4 us (14%)
  local copies, waits for them, and re-layouts  13.7 us (2%)
    pallas_call x49, Pallas kernels, call(): pl.pallas_call(placed, grid_spec=pltpu.PrefetchScalarGridSpec(num_scalar_...  220 us
    ppermute x48, waiting for transfers between devices, pass_on(): lax.ppermute(value, 'member', [(i, i ^ k) for i in range(self.members)])  170 us
    ppermute x32, waiting for transfers between devices, swap(): return lax.ppermute(value, 'dp', [(i, i ^ k) for i in range(self.dp_count)])  152 us
    ppermute x48, starting transfers between devices, pass_on(): lax.ppermute(value, 'member', [(i, i ^ k) for i in range(self.members)])  57.7 us
    ppermute x32, starting transfers between devices, swap(): return lax.ppermute(value, 'dp', [(i, i ^ k) for i in range(self.dp_count)])  29.9 us
  transfers between devices with their start and end apart: 82, of which 25 were waited for; matrix products, arithmetic and copies ran while one was open for 1% of the time, Pallas kernels for 31%

profile of v3, /device:TPU:0, one launch (start us, length us, event | category | flops | bytes accessed | tf_op | source)
XLA Modules:
  0.0 670.8 jit_solution(347475444741400001)
XLA Ops:
  3.8 6.4 all-to-all-start
  22.6 28.8 %collective-permute-done.5.refs_4_.refs_8_ = bf16[4,128,512]{2,1,0:T(8,128)(2,1)S(1)} collective-permute-done((bf16[4,128,512]{2,1,0:T(8,128)(2,1)}, bf16[4,128,512]{2,1,0:T(8,128)(2,1)S(1)}, u32[]{:S(2)}, u32[]{:S(2)}) %collective-permute-start.5) | collective-permute-done | bytes 524320 | tf_op jit(solution)/shard_map/ppermute | solution.py:227
  91.3 17.0 %collective-permute-done.1.refs_4_.refs_7_ = bf16[4,128,1024]{2,1,0:T(8,128)(2,1)} collective-permute-done((bf16[4,128,1024]{2,1,0:T(8,128)(2,1)}, bf16[4,128,1024]{2,1,0:T(8,128)(2,1)}, u32[]{:S(2)}, u32[]{:S(2)}) %collective-permute-start.1) | collective-permute-done | bytes 1048608 | tf_op jit(solution)/shard_map/ppermute | solution.py:227
  119.2 47.9 %collective-permute-done.12.refs_1_ = bf16[4,272,128]{2,1,0:T(8,128)(2,1)S(1)} collective-permute-done((bf16[4,272,128]{2,1,0:T(8,128)(2,1)S(1)}, bf16[4,272,128]{2,1,0:T(8,128)(2,1)S(1)}, u32[]{:S(2)}, u32[]{:S(2)}) %collective-permute-start.12) | collective-permute-done | bytes 278560 | tf_op jit(solution)/shard_map/ppermute | solution.py:227
  171.5 12.1 %collective-permute-done.11.refs_3_ = bf16[4,272,256]{2,1,0:T(8,128)(2,1)S(1)} collective-permute-done((bf16[4,272,256]{2,1,0:T(8,128)(2,1)}, bf16[4,272,256]{2,1,0:T(8,128)(2,1)S(1)}, u32[]{:S(2)}, u32[]{:S(2)}) %collective-permute-start.11) | collective-permute-done | bytes 557088 | tf_op jit(solution)/shard_map/ppermute | solution.py:230
  183.6 9.8 %collective-permute-done.9.refs_1_ = bf16[4,272,256]{2,1,0:T(8,128)(2,1)} collective-permute-done((bf16[4,272,256]{2,1,0:T(8,128)(2,1)}, bf16[4,272,256]{2,1,0:T(8,128)(2,1)}, u32[]{:S(2)}, u32[]{:S(2)}) %collective-permute-start.9) | collective-permute-done | bytes 557088 | tf_op jit(solution)/shard_map/ppermute | solution.py:230
  213.8 14.0 %collective-permute-done.22.refs_1_ = bf16[4,272,256]{2,1,0:T(8,128)(2,1)S(1)} collective-permute-done((bf16[4,272,256]{2,1,0:T(8,128)(2,1)S(1)}, bf16[4,272,256]{2,1,0:T(8,128)(2,1)S(1)}, u32[]{:S(2)}, u32[]{:S(2)}) %collective-permute-start.22) | collective-permute-done | bytes 557088 | tf_op jit(solution)/shard_map/ppermute | solution.py:227
  230.7 21.9 %collective-permute-done.20.refs_2_ = bf16[4,272,256]{2,1,0:T(8,128)(2,1)S(1)} collective-permute-done((bf16[4,272,256]{2,1,0:T(8,128)(2,1)}, bf16[4,272,256]{2,1,0:T(8,128)(2,1)S(1)}, u32[]{:S(2)}, u32[]{:S(2)}) %collective-permute-start.20) | collective-permute-done | bytes 557088 | tf_op jit(solution)/shard_map/ppermute | solution.py:230
  280.4 18.4 %collective-permute-done.29.refs_3_.refs_5_ = bf16[4,272,128]{2,1,0:T(8,128)(2,1)S(1)} collective-permute-done((bf16[4,272,128]{2,1,0:T(8,128)(2,1)S(1)}, bf16[4,272,128]{2,1,0:T(8,128)(2,1)S(1)}, u32[]{:S(2)}, u32[]{:S(2)}) %collective-permute-start.29) | collective-permute-done | bytes 278560 | tf_op jit(solution)/shard_map/ppermute | solution.py:230
  302.7 22.7 %collective-permute-done.24.refs_2_ = bf16[4,272,256]{2,1,0:T(8,128)(2,1)} collective-permute-done((bf16[4,272,256]{2,1,0:T(8,128)(2,1)}, bf16[4,272,256]{2,1,0:T(8,128)(2,1)}, u32[]{:S(2)}, u32[]{:S(2)}) %collective-permute-start.24) | collective-permute-done | bytes 557088 | tf_op jit(solution)/shard_map/ppermute | solution.py:230
  374.0 19.6 %collective-permute-done.40.refs_2_ = bf16[4,272,256]{2,1,0:T(8,128)(2,1)S(1)} collective-permute-done((bf16[4,272,256]{2,1,0:T(8,128)(2,1)}, bf16[4,272,256]{2,1,0:T(8,128)(2,1)S(1)}, u32[]{:S(2)}, u32[]{:S(2)}) %collective-permute-start.40) | collective-permute-done | bytes 557088 | tf_op jit(solution)/shard_map/ppermute | solution.py:230
  414.1 6.8 %shard_map.118 = (bf16[1,1024,7168]{2,1,0:T(8,128)(2,1)}, bf16[1,1024,7168]{2,1,0:T(8,128)(2,1)}) custom-call(s32[2]{0:T(128)} %pad_add_fusion.where, bf16[1024,272]{1,0:T(8,128)(2,1)} %get-tuple-element.157.refs_0_.x_ref, bf16[1024,272]{1,0:T(8,128)(2,1)} %get-tuple-element.156.refs_1_.d_ref, ...), custom_call_target="tpu_custom_call", output_to_operand_aliasing={{0}: (7, {}), {1}: (8, {})} | custom-call | flops 1140850688 | bytes 5308416 | tf_op jit(solution)/shard_map/pallas_call | solution.py:242
  433.1 10.7 %collective-permute-done.46.refs_1_ = bf16[4,272,256]{2,1,0:T(8,128)(2,1)} collective-permute-done((bf16[4,272,256]{2,1,0:T(8,128)(2,1)S(1)}, bf16[4,272,256]{2,1,0:T(8,128)(2,1)}, u32[]{:S(2)}, u32[]{:S(2)}) %collective-permute-start.46) | collective-permute-done | bytes 557088 | tf_op jit(solution)/shard_map/ppermute | solution.py:227
  445.6 24.8 %collective-permute-done.44.refs_2_ = bf16[4,272,256]{2,1,0:T(8,128)(2,1)S(1)} collective-permute-done((bf16[4,272,256]{2,1,0:T(8,128)(2,1)}, bf16[4,272,256]{2,1,0:T(8,128)(2,1)S(1)}, u32[]{:S(2)}, u32[]{:S(2)}) %collective-permute-start.44) | collective-permute-done | bytes 557088 | tf_op jit(solution)/shard_map/ppermute | solution.py:230
  487.9 6.8 %shard_map.124 = (bf16[1,1024,7168]{2,1,0:T(8,128)(2,1)}, bf16[1,1024,7168]{2,1,0:T(8,128)(2,1)}) custom-call(s32[2]{0:T(128)} %pad_add_fusion.where, bf16[1024,272]{1,0:T(8,128)(2,1)} %get-tuple-element.157.refs_0_.x_ref, bf16[1024,272]{1,0:T(8,128)(2,1)} %get-tuple-element.156.refs_1_.d_ref, ...), custom_call_target="tpu_custom_call", output_to_operand_aliasing={{0}: (7, {}), {1}: (8, {})} | custom-call | flops 1140850688 | bytes 5308416 | tf_op jit(solution)/shard_map/pallas_call | solution.py:242
  505.0 17.7 %collective-permute-done.62.refs_1_ = bf16[4,272,256]{2,1,0:T(8,128)(2,1)S(1)} collective-permute-done((bf16[4,272,256]{2,1,0:T(8,128)(2,1)S(1)}, bf16[4,272,256]{2,1,0:T(8,128)(2,1)S(1)}, u32[]{:S(2)}, u32[]{:S(2)}) %collective-permute-start.62) | collective-permute-done | bytes 557088 | tf_op jit(solution)/shard_map/ppermute | solution.py:227
  540.8 6.8 %shard_map.129 = (bf16[1,1024,7168]{2,1,0:T(8,128)(2,1)}, bf16[1,1024,7168]{2,1,0:T(8,128)(2,1)}) custom-call(s32[2]{0:T(128)} %pad_add_fusion.where, bf16[1024,272]{1,0:T(8,128)(2,1)} %get-tuple-element.157.refs_0_.x_ref, bf16[1024,272]{1,0:T(8,128)(2,1)} %get-tuple-element.156.refs_1_.d_ref, ...), custom_call_target="tpu_custom_call", output_to_operand_aliasing={{0}: (7, {}), {1}: (8, {})} | custom-call | flops 1140850688 | bytes 5308416 | tf_op jit(solution)/shard_map/pallas_call | solution.py:242
  555.6 7.8 %collective-permute-done.71.refs_1_.refs_3_ = bf16[4,272,256]{2,1,0:T(8,128)(2,1)S(1)} collective-permute-done((bf16[4,272,256]{2,1,0:T(8,128)(2,1)}, bf16[4,272,256]{2,1,0:T(8,128)(2,1)S(1)}, u32[]{:S(2)}, u32[]{:S(2)}) %collective-permute-start.71) | collective-permute-done | bytes 557088 | tf_op jit(solution)/shard_map/ppermute | solution.py:230
  566.6 6.4 shard_map.131.refs_2_.refs_9_
  576.8 12.4 %collective-permute-done.64.refs_2_ = bf16[4,272,128]{2,1,0:T(8,128)(2,1)S(1)} collective-permute-done((bf16[4,272,128]{2,1,0:T(8,128)(2,1)}, bf16[4,272,128]{2,1,0:T(8,128)(2,1)S(1)}, u32[]{:S(2)}, u32[]{:S(2)}) %collective-permute-start.64) | collective-permute-done | bytes 278560 | tf_op jit(solution)/shard_map/ppermute | solution.py:230
  599.0 6.7 shard_map.134
  638.6 6.7 shard_map.139
  645.2 6.7 shard_map.140
  657.5 8.2 %all-to-all-done.1.back_ref = bf16[8,136,512]{2,1,0:T(8,128)(2,1)S(1)} async-done(((bf16[8,136,512]{2,1,0:T(8,128)(2,1)}), bf16[8,136,512]{2,1,0:T(8,128)(2,1)S(1)}, u32[]{:S(2)}, u32[]{:S(2)}) %all-to-all-start.1) | async-done | bytes 1114144 | tf_op jit(solution)/shard_map/all_to_all | solution.py:592
  (311 shorter events, 322.8 us)
Async XLA Ops:
  3.8 48.4 %all-to-all-start = ((bf16[8,104,1024]{2,1,0:T(8,128)(2,1)}), bf16[8,104,1024]{2,1,0:T(8,128)(2,1)S(1)}, u32[]{:S(2)}, u32[]{:S(2)}) async-start(bf16[8,104,1024]{2,1,0:T(8,128)(2,1)} %route.1), calls=%async_computation | async-start | bytes 3407872 | tf_op jit(solution)/shard_map/all_to_all | solution.py:582
  15.9 41.8 %collective-permute-start.3 = (bf16[4,128,512]{2,1,0:T(8,128)(2,1)}, bf16[4,128,512]{2,1,0:T(8,128)(2,1)}, u32[]{:S(2)}, u32[]{:S(2)}) collective-permute-start(bf16[4,128,512]{2,1,0:T(8,128)(2,1)} %get-tuple-element.85), channel_id=1, source_target_pairs={{0,4},{4,0},{8,12},{12,8},{16,20},{20,16},{24,28},{28,24},{1,5},{5... | collective-permute-start | bytes 1572872 | tf_op jit(solution)/shard_map/ppermute | solution.py:227
  16.3 47.6 %collective-permute-start.4 = (bf16[4,128,512]{2,1,0:T(8,128)(2,1)}, bf16[4,128,512]{2,1,0:T(8,128)(2,1)}, u32[]{:S(2)}, u32[]{:S(2)}) collective-permute-start(bf16[4,128,512]{2,1,0:T(8,128)(2,1)} %get-tuple-element.86), channel_id=1, source_target_pairs={{0,8},{4,12},{8,0},{12,4},{16,24},{20,28},{24,16},{28,20},{1,9},{5... | collective-permute-start | bytes 1572872 | tf_op jit(solution)/shard_map/ppermute | solution.py:227
  20.4 70.8 %collective-permute-start.2 = (bf16[4,128,1024]{2,1,0:T(8,128)(2,1)}, bf16[4,128,1024]{2,1,0:T(8,128)(2,1)S(1)}, u32[]{:S(2)}, u32[]{:S(2)}) collective-permute-start(bf16[4,128,1024]{2,1,0:T(8,128)(2,1)} %get-tuple-element.81.refs_1_), channel_id=1, source_target_pairs={{0,12},{4,8},{8,4},{12,0},{16,28},{20,24},{24,20},{28,16},{1,13},{... | collective-permute-start | bytes 3145736 | tf_op jit(solution)/shard_map/ppermute | solution.py:227
  21.9 69.3 %collective-permute-start = (bf16[4,128,1024]{2,1,0:T(8,128)(2,1)}, bf16[4,128,1024]{2,1,0:T(8,128)(2,1)}, u32[]{:S(2)}, u32[]{:S(2)}) collective-permute-start(bf16[4,128,1024]{2,1,0:T(8,128)(2,1)} %get-tuple-element.83), channel_id=1, source_target_pairs={{0,4},{4,0},{8,12},{12,8},{16,20},{20,16},{24,28},{28,24},{1,5},{5... | collective-permute-start | bytes 3145736 | tf_op jit(solution)/shard_map/ppermute | solution.py:227
  51.4 56.9 %collective-permute-start.1 = (bf16[4,128,1024]{2,1,0:T(8,128)(2,1)}, bf16[4,128,1024]{2,1,0:T(8,128)(2,1)}, u32[]{:S(2)}, u32[]{:S(2)}) collective-permute-start(bf16[4,128,1024]{2,1,0:T(8,128)(2,1)} %get-tuple-element.84), channel_id=1, source_target_pairs={{0,8},{4,12},{8,0},{12,4},{16,24},{20,28},{24,16},{28,20},{1,9},{5... | collective-permute-start | bytes 3145736 | tf_op jit(solution)/shard_map/ppermute | solution.py:227
  113.3 55.1 %collective-permute-start.10 = (bf16[4,272,256]{2,1,0:T(8,128)(2,1)}, bf16[4,272,256]{2,1,0:T(8,128)(2,1)S(1)}, u32[]{:S(2)}, u32[]{:S(2)}) collective-permute-start(bf16[4,272,256]{2,1,0:T(8,128)(2,1)} %get-tuple-element.94), channel_id=1, source_target_pairs={{0,2},{1,3},{2,0},{3,1},{4,6},{5,7},{6,4},{7,5},{8,10},{9,11},{10,... | collective-permute-start | bytes 1671176 | tf_op jit(solution)/shard_map/ppermute | solution.py:230
  114.8 89.3 %collective-permute-start.16 = (bf16[4,128,1024]{2,1,0:T(8,128)(2,1)}, bf16[4,128,1024]{2,1,0:T(8,128)(2,1)S(1)}, u32[]{:S(2)}, u32[]{:S(2)}) collective-permute-start(bf16[4,128,1024]{2,1,0:T(8,128)(2,1)} %get-tuple-element.99), channel_id=1, source_target_pairs={{0,4},{4,0},{8,12},{12,8},{16,20},{20,16},{24,28},{28,24},{1,5},{5... | collective-permute-start | bytes 3145736 | tf_op jit(solution)/shard_map/ppermute | solution.py:227
  114.8 89.3 %collective-permute-start.17 = (bf16[4,128,1024]{2,1,0:T(8,128)(2,1)}, bf16[4,128,1024]{2,1,0:T(8,128)(2,1)S(1)}, u32[]{:S(2)}, u32[]{:S(2)}) collective-permute-start(bf16[4,128,1024]{2,1,0:T(8,128)(2,1)} %get-tuple-element.100), channel_id=1, source_target_pairs={{0,8},{4,12},{8,0},{12,4},{16,24},{20,28},{24,16},{28,20},{1,9},{5... | collective-permute-start | bytes 3145736 | tf_op jit(solution)/shard_map/ppermute | solution.py:227
  115.3 88.9 %collective-permute-start.18 = (bf16[4,128,1024]{2,1,0:T(8,128)(2,1)}, bf16[4,128,1024]{2,1,0:T(8,128)(2,1)}, u32[]{:S(2)}, u32[]{:S(2)}) collective-permute-start(bf16[4,128,1024]{2,1,0:T(8,128)(2,1)} %get-tuple-element.91.refs_6_), channel_id=1, source_target_pairs={{0,12},{4,8},{8,4},{12,0},{16,28},{20,24},{24,20},{28,16},{1,13},{... | collective-permute-start | bytes 3145736 | tf_op jit(solution)/shard_map/ppermute | solution.py:227
  116.7 50.3 %collective-permute-start.12 = (bf16[4,272,128]{2,1,0:T(8,128)(2,1)S(1)}, bf16[4,272,128]{2,1,0:T(8,128)(2,1)S(1)}, u32[]{:S(2)}, u32[]{:S(2)}) collective-permute-start(bf16[4,272,128]{2,1,0:T(8,128)(2,1)S(1)} %copy-done.20), channel_id=1, source_target_pairs={{0,16},{4,20},{8,24},{12,28},{16,0},{20,4},{24,8},{28,12},{1,17},{... | collective-permute-start | bytes 835592 | tf_op jit(solution)/shard_map/ppermute | solution.py:227
  211.9 54.5 %collective-permute-start.13 = (bf16[4,128,1024]{2,1,0:T(8,128)(2,1)}, bf16[4,128,1024]{2,1,0:T(8,128)(2,1)S(1)}, u32[]{:S(2)}, u32[]{:S(2)}) collective-permute-start(bf16[4,128,1024]{2,1,0:T(8,128)(2,1)} %get-tuple-element.96), channel_id=1, source_target_pairs={{0,4},{4,0},{8,12},{12,8},{16,20},{20,16},{24,28},{28,24},{1,5},{5... | collective-permute-start | bytes 3145736 | tf_op jit(solution)/shard_map/ppermute | solution.py:227
  211.9 54.6 %collective-permute-start.14 = (bf16[4,128,1024]{2,1,0:T(8,128)(2,1)}, bf16[4,128,1024]{2,1,0:T(8,128)(2,1)S(1)}, u32[]{:S(2)}, u32[]{:S(2)}) collective-permute-start(bf16[4,128,1024]{2,1,0:T(8,128)(2,1)} %get-tuple-element.97), channel_id=1, source_target_pairs={{0,8},{4,12},{8,0},{12,4},{16,24},{20,28},{24,16},{28,20},{1,9},{5... | collective-permute-start | bytes 3145736 | tf_op jit(solution)/shard_map/ppermute | solution.py:227
  213.1 55.4 %collective-permute-start.15 = (bf16[4,128,1024]{2,1,0:T(8,128)(2,1)}, bf16[4,128,1024]{2,1,0:T(8,128)(2,1)}, u32[]{:S(2)}, u32[]{:S(2)}) collective-permute-start(bf16[4,128,1024]{2,1,0:T(8,128)(2,1)} %get-tuple-element.98.refs_6_), channel_id=1, source_target_pairs={{0,12},{4,8},{8,4},{12,0},{16,28},{20,24},{24,20},{28,16},{1,13},{... | collective-permute-start | bytes 3145736 | tf_op jit(solution)/shard_map/ppermute | solution.py:227
  274.1 63.0 %collective-permute-start.36 = (bf16[4,128,1024]{2,1,0:T(8,128)(2,1)}, bf16[4,128,1024]{2,1,0:T(8,128)(2,1)S(1)}, u32[]{:S(2)}, u32[]{:S(2)}) collective-permute-start(bf16[4,128,1024]{2,1,0:T(8,128)(2,1)} %get-tuple-element.116), channel_id=1, source_target_pairs={{0,4},{4,0},{8,12},{12,8},{16,20},{20,16},{24,28},{28,24},{1,5},{5... | collective-permute-start | bytes 3145736 | tf_op jit(solution)/shard_map/ppermute | solution.py:227
  277.2 62.5 %collective-permute-start.37 = (bf16[4,128,1024]{2,1,0:T(8,128)(2,1)}, bf16[4,128,1024]{2,1,0:T(8,128)(2,1)}, u32[]{:S(2)}, u32[]{:S(2)}) collective-permute-start(bf16[4,128,1024]{2,1,0:T(8,128)(2,1)} %get-tuple-element.117), channel_id=1, source_target_pairs={{0,8},{4,12},{8,0},{12,4},{16,24},{20,28},{24,16},{28,20},{1,9},{5... | collective-permute-start | bytes 3145736 | tf_op jit(solution)/shard_map/ppermute | solution.py:227
  298.8 55.5 %collective-permute-start.38 = (bf16[4,128,1024]{2,1,0:T(8,128)(2,1)}, bf16[4,128,1024]{2,1,0:T(8,128)(2,1)}, u32[]{:S(2)}, u32[]{:S(2)}) collective-permute-start(bf16[4,128,1024]{2,1,0:T(8,128)(2,1)} %get-tuple-element.105.refs_6_), channel_id=1, source_target_pairs={{0,12},{4,8},{8,4},{12,0},{16,28},{20,24},{24,20},{28,16},{1,13},{... | collective-permute-start | bytes 3145736 | tf_op jit(solution)/shard_map/ppermute | solution.py:227
  360.0 53.4 %collective-permute-start.31 = (bf16[4,128,1024]{2,1,0:T(8,128)(2,1)}, bf16[4,128,1024]{2,1,0:T(8,128)(2,1)}, u32[]{:S(2)}, u32[]{:S(2)}) collective-permute-start(bf16[4,128,1024]{2,1,0:T(8,128)(2,1)} %get-tuple-element.111), channel_id=1, source_target_pairs={{0,8},{4,12},{8,0},{12,4},{16,24},{20,28},{24,16},{28,20},{1,9},{5... | collective-permute-start | bytes 3145736 | tf_op jit(solution)/shard_map/ppermute | solution.py:227
  362.1 58.8 %collective-permute-start.32 = (bf16[4,128,1024]{2,1,0:T(8,128)(2,1)}, bf16[4,128,1024]{2,1,0:T(8,128)(2,1)}, u32[]{:S(2)}, u32[]{:S(2)}) collective-permute-start(bf16[4,128,1024]{2,1,0:T(8,128)(2,1)} %get-tuple-element.112.refs_6_), channel_id=1, source_target_pairs={{0,12},{4,8},{8,4},{12,0},{16,28},{20,24},{24,20},{28,16},{1,13},{... | collective-permute-start | bytes 3145736 | tf_op jit(solution)/shard_map/ppermute | solution.py:227
  427.5 60.3 %collective-permute-start.56 = (bf16[4,128,1024]{2,1,0:T(8,128)(2,1)}, bf16[4,128,1024]{2,1,0:T(8,128)(2,1)S(1)}, u32[]{:S(2)}, u32[]{:S(2)}) collective-permute-start(bf16[4,128,1024]{2,1,0:T(8,128)(2,1)} %get-tuple-element.134), channel_id=1, source_target_pairs={{0,4},{4,0},{8,12},{12,8},{16,20},{20,16},{24,28},{28,24},{1,5},{5... | collective-permute-start | bytes 3145736 | tf_op jit(solution)/shard_map/ppermute | solution.py:227
  427.5 60.3 %collective-permute-start.57 = (bf16[4,128,1024]{2,1,0:T(8,128)(2,1)}, bf16[4,128,1024]{2,1,0:T(8,128)(2,1)}, u32[]{:S(2)}, u32[]{:S(2)}) collective-permute-start(bf16[4,128,1024]{2,1,0:T(8,128)(2,1)} %get-tuple-element.135), channel_id=1, source_target_pairs={{0,8},{4,12},{8,0},{12,4},{16,24},{20,28},{24,16},{28,20},{1,9},{5... | collective-permute-start | bytes 3145736 | tf_op jit(solution)/shard_map/ppermute | solution.py:227
  433.1 61.6 %collective-permute-start.58 = (bf16[4,128,1024]{2,1,0:T(8,128)(2,1)}, bf16[4,128,1024]{2,1,0:T(8,128)(2,1)}, u32[]{:S(2)}, u32[]{:S(2)}) collective-permute-start(bf16[4,128,1024]{2,1,0:T(8,128)(2,1)} %get-tuple-element.122.refs_8_), channel_id=1, source_target_pairs={{0,12},{4,8},{8,4},{12,0},{16,28},{20,24},{24,20},{28,16},{1,13},{... | collective-permute-start | bytes 3145736 | tf_op jit(solution)/shard_map/ppermute | solution.py:227
  547.6 47.5 %collective-permute-start.72 = (bf16[4,272,256]{2,1,0:T(8,128)(2,1)S(1)}, bf16[4,272,256]{2,1,0:T(8,128)(2,1)S(1)}, u32[]{:S(2)}, u32[]{:S(2)}) collective-permute-start(bf16[4,272,256]{2,1,0:T(8,128)(2,1)S(1)} %copy-done.4), channel_id=1, source_target_pairs={{0,2},{1,3},{2,0},{3,1},{4,6},{5,7},{6,4},{7,5},{8,10},{9,11},{10,... | collective-permute-start | bytes 1671176 | tf_op jit(solution)/shard_map/ppermute | solution.py:230
  554.0 51.7 %collective-permute-start.73 = (bf16[4,272,256]{2,1,0:T(8,128)(2,1)S(1)}, bf16[4,272,256]{2,1,0:T(8,128)(2,1)S(1)}, u32[]{:S(2)}, u32[]{:S(2)}) collective-permute-start(bf16[4,272,256]{2,1,0:T(8,128)(2,1)S(1)} %copy-done.4), channel_id=1, source_target_pairs={{0,3},{1,2},{2,1},{3,0},{4,7},{5,6},{6,5},{7,4},{8,11},{9,10},{10,... | collective-permute-start | bytes 1671176 | tf_op jit(solution)/shard_map/ppermute | solution.py:230
  (116 other events, 2033.2 us)

commit v4 on v3

--- a/solution.py
+++ b/solution.py
@@ -13,6 +13,7 @@
 CAP = 34
 HALVES = 2
 GRAD_STEPS = 4
+KERNEL_VMEM = 51 << 20
 LANES = 128
 SUBLANES = 8
 NOWHERE = -1e6
@@ -178,6 +179,7 @@
         cost_estimate=pl.CostEstimate(
             flops=4 * E * CAP * tokens.size, bytes_accessed=2 * 10 * tokens.size, transcendentals=0
         ),
+        compiler_params=pltpu.CompilerParams(vmem_limit_bytes=KERNEL_VMEM),
         name="route",
     )(routes_t, weights_t, tokens, cotangent)
 
@@ -251,6 +253,7 @@
             out_shape=out_shape,
             input_output_aliases={i + 1: o for i, o in (aliases or {}).items()},
             cost_estimate=pl.CostEstimate(flops=cost[0], bytes_accessed=cost[1], transcendentals=0),
+            compiler_params=pltpu.CompilerParams(vmem_limit_bytes=KERNEL_VMEM),
         )(self.where, *args)
         self.last = outs[-1]
         return outs
@@ -592,9 +595,12 @@
             back = lax.all_to_all(total, "dp", split_axis=0, concat_axis=0, tiled=True)
 
     out = jax.ShapeDtypeStruct(tokens.shape, BF)
-    mixed, grad_tokens = pl.pallas_call(mix_kernel, out_shape=(out, out), name="mix")(
-        routes_t, route_weights, back
-    )
+    mixed, grad_tokens = pl.pallas_call(
+        mix_kernel,
+        out_shape=(out, out),
+        compiler_params=pltpu.CompilerParams(vmem_limit_bytes=KERNEL_VMEM),
+        name="mix",
+    )(routes_t, route_weights, back)
     return (mixed, grad_tokens, *grads)
 
 

time: 673 us -> 657 us (0.976)
  Pallas kernels: 227 us -> 170 us
  waiting for transfers between devices: 330 us -> 365 us
  local copies, waits for them, and re-layouts: 13.7 us -> 25.1 us
    pallas_call x49, Pallas kernels: 220 us -> 165 us  [call(): pl.pallas_call(placed, grid_spec=pltpu.PrefetchScalarGridSpec(num_scalar_...]
    ppermute x48, waiting for transfers between devices: 170 us -> 198 us  [pass_on(): lax.ppermute(value, 'member', [(i, i ^ k) for i in range(self.members)])]
    unnamed x117 -> x135, local copies, waits for them, and re-layouts: 10.6 us -> 22.4 us
  transfers between devices with their start and end apart: 82 -> 82, of which waited for: 25 -> 30; matrix products, arithmetic and copies ran while one was open for 1% -> 0% of each run, Pallas kernels for 31% -> 24%
where the time goes in v4:
time: 657 us; the launch traced here: 655 us
  waiting for transfers between devices  365 us (56%)
  Pallas kernels  170 us (26%)
  starting transfers between devices  93.4 us (14%)
  local copies, waits for them, and re-layouts  25.1 us (4%)
    ppermute x48, waiting for transfers between devices, pass_on(): lax.ppermute(value, 'member', [(i, i ^ k) for i in range(self.members)])  198 us
    pallas_call x49, Pallas kernels, call(): pl.pallas_call(placed, grid_spec=pltpu.PrefetchScalarGridSpec(num_scalar_...  165 us
    ppermute x32, waiting for transfers between devices, swap(): return lax.ppermute(value, 'dp', [(i, i ^ k) for i in range(self.dp_count)])  158 us
    ppermute x48, starting transfers between devices, pass_on(): lax.ppermute(value, 'member', [(i, i ^ k) for i in range(self.members)])  58.2 us
    ppermute x32, starting transfers between devices, swap(): return lax.ppermute(value, 'dp', [(i, i ^ k) for i in range(self.dp_count)])  25.2 us
    unnamed x135, local copies, waits for them, and re-layouts  22.4 us
  transfers between devices with their start and end apart: 82, of which 30 were waited for; matrix products, arithmetic and copies ran while one was open for 0% of the time, Pallas kernels for 24%

profile of v4, /device:TPU:0, one launch (start us, length us, event | category | flops | bytes accessed | tf_op | source)
XLA Modules:
  0.0 655.2 jit_solution(6560723777535806576)
XLA Ops:
  6.0 6.3 all-to-all-start
  23.4 30.2 %collective-permute-done.5.refs_4_.refs_8_ = bf16[4,128,512]{2,1,0:T(8,128)(2,1)S(1)} collective-permute-done((bf16[4,128,512]{2,1,0:T(8,128)(2,1)S(1)}, bf16[4,128,512]{2,1,0:T(8,128)(2,1)S(1)}, u32[]{:S(2)}, u32[]{:S(2)}) %collective-permute-start.5) | collective-permute-done | bytes 524320 | tf_op jit(solution)/shard_map/ppermute | solution.py:229
  89.0 21.5 %collective-permute-done.1.refs_4_.refs_7_ = bf16[4,128,1024]{2,1,0:T(8,128)(2,1)} collective-permute-done((bf16[4,128,1024]{2,1,0:T(8,128)(2,1)S(1)}, bf16[4,128,1024]{2,1,0:T(8,128)(2,1)}, u32[]{:S(2)}, u32[]{:S(2)}) %collective-permute-start.1) | collective-permute-done | bytes 1048608 | tf_op jit(solution)/shard_map/ppermute | solution.py:229
  120.3 47.6 %collective-permute-done.12.refs_1_ = bf16[4,272,128]{2,1,0:T(8,128)(2,1)S(1)} collective-permute-done((bf16[4,272,128]{2,1,0:T(8,128)(2,1)S(1)}, bf16[4,272,128]{2,1,0:T(8,128)(2,1)S(1)}, u32[]{:S(2)}, u32[]{:S(2)}) %collective-permute-start.12) | collective-permute-done | bytes 278560 | tf_op jit(solution)/shard_map/ppermute | solution.py:229
  170.7 13.7 %collective-permute-done.11.refs_3_ = bf16[4,272,256]{2,1,0:T(8,128)(2,1)S(1)} collective-permute-done((bf16[4,272,256]{2,1,0:T(8,128)(2,1)S(1)}, bf16[4,272,256]{2,1,0:T(8,128)(2,1)S(1)}, u32[]{:S(2)}, u32[]{:S(2)}) %collective-permute-start.11) | collective-permute-done | bytes 557088 | tf_op jit(solution)/shard_map/ppermute | solution.py:232
  184.4 9.7 %collective-permute-done.9.refs_1_ = bf16[4,272,256]{2,1,0:T(8,128)(2,1)S(1)} collective-permute-done((bf16[4,272,256]{2,1,0:T(8,128)(2,1)S(1)}, bf16[4,272,256]{2,1,0:T(8,128)(2,1)S(1)}, u32[]{:S(2)}, u32[]{:S(2)}) %collective-permute-start.9) | collective-permute-done | bytes 557088 | tf_op jit(solution)/shard_map/ppermute | solution.py:232
  210.9 14.7 %collective-permute-done.22.refs_1_ = bf16[4,272,256]{2,1,0:T(8,128)(2,1)S(1)} collective-permute-done((bf16[4,272,256]{2,1,0:T(8,128)(2,1)S(1)}, bf16[4,272,256]{2,1,0:T(8,128)(2,1)S(1)}, u32[]{:S(2)}, u32[]{:S(2)}) %collective-permute-start.22) | collective-permute-done | bytes 557088 | tf_op jit(solution)/shard_map/ppermute | solution.py:229
  228.5 21.7 %collective-permute-done.20.refs_2_ = bf16[4,272,256]{2,1,0:T(8,128)(2,1)S(1)} collective-permute-done((bf16[4,272,256]{2,1,0:T(8,128)(2,1)S(1)}, bf16[4,272,256]{2,1,0:T(8,128)(2,1)S(1)}, u32[]{:S(2)}, u32[]{:S(2)}) %collective-permute-start.20) | collective-permute-done | bytes 557088 | tf_op jit(solution)/shard_map/ppermute | solution.py:232
  259.9 8.1 %collective-permute-done.15.refs_5_.refs_8_ = bf16[4,128,1024]{2,1,0:T(8,128)(2,1)S(1)} collective-permute-done((bf16[4,128,1024]{2,1,0:T(8,128)(2,1)S(1)}, bf16[4,128,1024]{2,1,0:T(8,128)(2,1)S(1)}, u32[]{:S(2)}, u32[]{:S(2)}) %collective-permute-start.15) | collective-permute-done | bytes 1048608 | tf_op jit(solution)/shard_map/ppermute | solution.py:229
  278.1 18.7 %collective-permute-done.29.refs_3_.refs_5_ = bf16[4,272,128]{2,1,0:T(8,128)(2,1)S(1)} collective-permute-done((bf16[4,272,128]{2,1,0:T(8,128)(2,1)S(1)}, bf16[4,272,128]{2,1,0:T(8,128)(2,1)S(1)}, u32[]{:S(2)}, u32[]{:S(2)}) %collective-permute-start.29) | collective-permute-done | bytes 278560 | tf_op jit(solution)/shard_map/ppermute | solution.py:232
  303.6 21.2 %collective-permute-done.24.refs_2_ = bf16[4,272,256]{2,1,0:T(8,128)(2,1)} collective-permute-done((bf16[4,272,256]{2,1,0:T(8,128)(2,1)}, bf16[4,272,256]{2,1,0:T(8,128)(2,1)}, u32[]{:S(2)}, u32[]{:S(2)}) %collective-permute-start.24) | collective-permute-done | bytes 557088 | tf_op jit(solution)/shard_map/ppermute | solution.py:232
  367.8 23.3 %collective-permute-done.40.refs_2_ = bf16[4,272,256]{2,1,0:T(8,128)(2,1)S(1)} collective-permute-done((bf16[4,272,256]{2,1,0:T(8,128)(2,1)S(1)}, bf16[4,272,256]{2,1,0:T(8,128)(2,1)S(1)}, u32[]{:S(2)}, u32[]{:S(2)}) %collective-permute-start.40) | collective-permute-done | bytes 557088 | tf_op jit(solution)/shard_map/ppermute | solution.py:232
  419.2 11.3 %collective-permute-done.53.refs_1_.refs_3_ = bf16[4,272,256]{2,1,0:T(8,128)(2,1)S(1)} collective-permute-done((bf16[4,272,256]{2,1,0:T(8,128)(2,1)S(1)}, bf16[4,272,256]{2,1,0:T(8,128)(2,1)S(1)}, u32[]{:S(2)}, u32[]{:S(2)}) %collective-permute-start.53) | collective-permute-done | bytes 557088 | tf_op jit(solution)/shard_map/ppermute | solution.py:232
  430.5 8.2 %collective-permute-done.46.refs_1_ = bf16[4,272,256]{2,1,0:T(8,128)(2,1)S(1)} collective-permute-done((bf16[4,272,256]{2,1,0:T(8,128)(2,1)S(1)}, bf16[4,272,256]{2,1,0:T(8,128)(2,1)S(1)}, u32[]{:S(2)}, u32[]{:S(2)}) %collective-permute-start.46) | collective-permute-done | bytes 557088 | tf_op jit(solution)/shard_map/ppermute | solution.py:229
  442.0 23.1 %collective-permute-done.44.refs_2_ = bf16[4,272,256]{2,1,0:T(8,128)(2,1)S(1)} collective-permute-done((bf16[4,272,256]{2,1,0:T(8,128)(2,1)S(1)}, bf16[4,272,256]{2,1,0:T(8,128)(2,1)S(1)}, u32[]{:S(2)}, u32[]{:S(2)}) %collective-permute-start.44) | collective-permute-done | bytes 557088 | tf_op jit(solution)/shard_map/ppermute | solution.py:232
  477.3 6.2 shard_map.124
  494.7 16.8 %collective-permute-done.62.refs_1_ = bf16[4,272,256]{2,1,0:T(8,128)(2,1)S(1)} collective-permute-done((bf16[4,272,256]{2,1,0:T(8,128)(2,1)S(1)}, bf16[4,272,256]{2,1,0:T(8,128)(2,1)S(1)}, u32[]{:S(2)}, u32[]{:S(2)}) %collective-permute-start.62) | collective-permute-done | bytes 557088 | tf_op jit(solution)/shard_map/ppermute | solution.py:229
  524.8 6.1 shard_map.129
  534.6 6.7 %collective-permute-done.68.refs_2_.refs_4_ = bf16[4,272,256]{2,1,0:T(8,128)(2,1)S(1)} collective-permute-done((bf16[4,272,256]{2,1,0:T(8,128)(2,1)S(1)}, bf16[4,272,256]{2,1,0:T(8,128)(2,1)S(1)}, u32[]{:S(2)}, u32[]{:S(2)}) %collective-permute-start.68) | collective-permute-done | bytes 557088 | tf_op jit(solution)/shard_map/ppermute | solution.py:232
  543.2 10.7 %collective-permute-done.71.refs_1_.refs_3_ = bf16[4,272,256]{2,1,0:T(8,128)(2,1)S(1)} collective-permute-done((bf16[4,272,256]{2,1,0:T(8,128)(2,1)}, bf16[4,272,256]{2,1,0:T(8,128)(2,1)S(1)}, u32[]{:S(2)}, u32[]{:S(2)}) %collective-permute-start.71) | collective-permute-done | bytes 557088 | tf_op jit(solution)/shard_map/ppermute | solution.py:232
  564.2 15.3 %collective-permute-done.64.refs_2_ = bf16[4,272,128]{2,1,0:T(8,128)(2,1)S(1)} collective-permute-done((bf16[4,272,128]{2,1,0:T(8,128)(2,1)S(1)}, bf16[4,272,128]{2,1,0:T(8,128)(2,1)S(1)}, u32[]{:S(2)}, u32[]{:S(2)}) %collective-permute-start.64) | collective-permute-done | bytes 278560 | tf_op jit(solution)/shard_map/ppermute | solution.py:232
  584.7 6.1 shard_map.134
  626.7 6.1 shard_map.139
  642.6 9.8 %all-to-all-done.1.back_ref = bf16[8,136,512]{2,1,0:T(8,128)(2,1)S(1)} async-done(((bf16[8,136,512]{2,1,0:T(8,128)(2,1)}), bf16[8,136,512]{2,1,0:T(8,128)(2,1)S(1)}, u32[]{:S(2)}, u32[]{:S(2)}) %all-to-all-start.1) | async-done | bytes 1114144 | tf_op jit(solution)/shard_map/all_to_all | solution.py:595
  (329 shorter events, 290.8 us)
Async XLA Ops:
  6.0 48.4 %all-to-all-start = ((bf16[8,104,1024]{2,1,0:T(8,128)(2,1)}), bf16[8,104,1024]{2,1,0:T(8,128)(2,1)}, u32[]{:S(2)}, u32[]{:S(2)}) async-start(bf16[8,104,1024]{2,1,0:T(8,128)(2,1)} %route.1), calls=%async_computation | async-start | bytes 3407872 | tf_op jit(solution)/shard_map/all_to_all | solution.py:585
  17.0 43.4 %collective-permute-start.3 = (bf16[4,128,512]{2,1,0:T(8,128)(2,1)}, bf16[4,128,512]{2,1,0:T(8,128)(2,1)S(1)}, u32[]{:S(2)}, u32[]{:S(2)}) collective-permute-start(bf16[4,128,512]{2,1,0:T(8,128)(2,1)} %get-tuple-element.85), channel_id=1, source_target_pairs={{0,4},{4,0},{8,12},{12,8},{16,20},{20,16},{24,28},{28,24},{1,5},{5... | collective-permute-start | bytes 1572872 | tf_op jit(solution)/shard_map/ppermute | solution.py:229
  17.4 48.6 %collective-permute-start.4 = (bf16[4,128,512]{2,1,0:T(8,128)(2,1)S(1)}, bf16[4,128,512]{2,1,0:T(8,128)(2,1)S(1)}, u32[]{:S(2)}, u32[]{:S(2)}) collective-permute-start(bf16[4,128,512]{2,1,0:T(8,128)(2,1)S(1)} %get-tuple-element.86), channel_id=1, source_target_pairs={{0,8},{4,12},{8,0},{12,4},{16,24},{20,28},{24,16},{28,20},{1,9},{5... | collective-permute-start | bytes 1572872 | tf_op jit(solution)/shard_map/ppermute | solution.py:229
  21.2 67.8 %collective-permute-start.2 = (bf16[4,128,1024]{2,1,0:T(8,128)(2,1)}, bf16[4,128,1024]{2,1,0:T(8,128)(2,1)}, u32[]{:S(2)}, u32[]{:S(2)}) collective-permute-start(bf16[4,128,1024]{2,1,0:T(8,128)(2,1)} %get-tuple-element.81.refs_1_), channel_id=1, source_target_pairs={{0,12},{4,8},{8,4},{12,0},{16,28},{20,24},{24,20},{28,16},{1,13},{... | collective-permute-start | bytes 3145736 | tf_op jit(solution)/shard_map/ppermute | solution.py:229
  22.7 66.2 %collective-permute-start = (bf16[4,128,1024]{2,1,0:T(8,128)(2,1)}, bf16[4,128,1024]{2,1,0:T(8,128)(2,1)}, u32[]{:S(2)}, u32[]{:S(2)}) collective-permute-start(bf16[4,128,1024]{2,1,0:T(8,128)(2,1)} %get-tuple-element.83), channel_id=1, source_target_pairs={{0,4},{4,0},{8,12},{12,8},{16,20},{20,16},{24,28},{28,24},{1,5},{5... | collective-permute-start | bytes 3145736 | tf_op jit(solution)/shard_map/ppermute | solution.py:229
  53.6 56.9 %collective-permute-start.1 = (bf16[4,128,1024]{2,1,0:T(8,128)(2,1)S(1)}, bf16[4,128,1024]{2,1,0:T(8,128)(2,1)}, u32[]{:S(2)}, u32[]{:S(2)}) collective-permute-start(bf16[4,128,1024]{2,1,0:T(8,128)(2,1)S(1)} %get-tuple-element.84), channel_id=1, source_target_pairs={{0,8},{4,12},{8,0},{12,4},{16,24},{20,28},{24,16},{28,20},{1,9},{5... | collective-permute-start | bytes 3145736 | tf_op jit(solution)/shard_map/ppermute | solution.py:229
  114.4 55.0 %collective-permute-start.10 = (bf16[4,272,256]{2,1,0:T(8,128)(2,1)S(1)}, bf16[4,272,256]{2,1,0:T(8,128)(2,1)S(1)}, u32[]{:S(2)}, u32[]{:S(2)}) collective-permute-start(bf16[4,272,256]{2,1,0:T(8,128)(2,1)S(1)} %get-tuple-element.94), channel_id=1, source_target_pairs={{0,2},{1,3},{2,0},{3,1},{4,6},{5,7},{6,4},{7,5},{8,10},{9,11},{10,... | collective-permute-start | bytes 1671176 | tf_op jit(solution)/shard_map/ppermute | solution.py:232
  116.0 86.0 %collective-permute-start.16 = (bf16[4,128,1024]{2,1,0:T(8,128)(2,1)S(1)}, bf16[4,128,1024]{2,1,0:T(8,128)(2,1)S(1)}, u32[]{:S(2)}, u32[]{:S(2)}) collective-permute-start(bf16[4,128,1024]{2,1,0:T(8,128)(2,1)S(1)} %get-tuple-element.99), channel_id=1, source_target_pairs={{0,4},{4,0},{8,12},{12,8},{16,20},{20,16},{24,28},{28,24},{1,5},{5... | collective-permute-start | bytes 3145736 | tf_op jit(solution)/shard_map/ppermute | solution.py:229
  116.0 86.0 %collective-permute-start.17 = (bf16[4,128,1024]{2,1,0:T(8,128)(2,1)S(1)}, bf16[4,128,1024]{2,1,0:T(8,128)(2,1)S(1)}, u32[]{:S(2)}, u32[]{:S(2)}) collective-permute-start(bf16[4,128,1024]{2,1,0:T(8,128)(2,1)S(1)} %get-tuple-element.100), channel_id=1, source_target_pairs={{0,8},{4,12},{8,0},{12,4},{16,24},{20,28},{24,16},{28,20},{1,9},{5... | collective-permute-start | bytes 3145736 | tf_op jit(solution)/shard_map/ppermute | solution.py:229
  116.4 85.5 %collective-permute-start.18 = (bf16[4,128,1024]{2,1,0:T(8,128)(2,1)S(1)}, bf16[4,128,1024]{2,1,0:T(8,128)(2,1)S(1)}, u32[]{:S(2)}, u32[]{:S(2)}) collective-permute-start(bf16[4,128,1024]{2,1,0:T(8,128)(2,1)S(1)} %copy-done.66), channel_id=1, source_target_pairs={{0,12},{4,8},{8,4},{12,0},{16,28},{20,24},{24,20},{28,16},{1,13},{... | collective-permute-start | bytes 3145736 | tf_op jit(solution)/shard_map/ppermute | solution.py:229
  117.9 50.1 %collective-permute-start.12 = (bf16[4,272,128]{2,1,0:T(8,128)(2,1)S(1)}, bf16[4,272,128]{2,1,0:T(8,128)(2,1)S(1)}, u32[]{:S(2)}, u32[]{:S(2)}) collective-permute-start(bf16[4,272,128]{2,1,0:T(8,128)(2,1)S(1)} %shard_map.97.refs_12_.refs_0_), channel_id=1, source_target_pairs={{0,16},{4,20},{8,24},{12,28},{16,0},{20,4},{24,8},{28,12},{1,17},{... | collective-permute-start | bytes 835592 | tf_op jit(solution)/shard_map/ppermute | solution.py:229
  209.0 50.8 %collective-permute-start.13 = (bf16[4,128,1024]{2,1,0:T(8,128)(2,1)S(1)}, bf16[4,128,1024]{2,1,0:T(8,128)(2,1)S(1)}, u32[]{:S(2)}, u32[]{:S(2)}) collective-permute-start(bf16[4,128,1024]{2,1,0:T(8,128)(2,1)S(1)} %get-tuple-element.96), channel_id=1, source_target_pairs={{0,4},{4,0},{8,12},{12,8},{16,20},{20,16},{24,28},{28,24},{1,5},{5... | collective-permute-start | bytes 3145736 | tf_op jit(solution)/shard_map/ppermute | solution.py:229
  209.0 50.9 %collective-permute-start.14 = (bf16[4,128,1024]{2,1,0:T(8,128)(2,1)S(1)}, bf16[4,128,1024]{2,1,0:T(8,128)(2,1)S(1)}, u32[]{:S(2)}, u32[]{:S(2)}) collective-permute-start(bf16[4,128,1024]{2,1,0:T(8,128)(2,1)S(1)} %get-tuple-element.97), channel_id=1, source_target_pairs={{0,8},{4,12},{8,0},{12,4},{16,24},{20,28},{24,16},{28,20},{1,9},{5... | collective-permute-start | bytes 3145736 | tf_op jit(solution)/shard_map/ppermute | solution.py:229
  210.2 57.9 %collective-permute-start.15 = (bf16[4,128,1024]{2,1,0:T(8,128)(2,1)S(1)}, bf16[4,128,1024]{2,1,0:T(8,128)(2,1)S(1)}, u32[]{:S(2)}, u32[]{:S(2)}) collective-permute-start(bf16[4,128,1024]{2,1,0:T(8,128)(2,1)S(1)} %copy-done.65), channel_id=1, source_target_pairs={{0,12},{4,8},{8,4},{12,0},{16,28},{20,24},{24,20},{28,16},{1,13},{... | collective-permute-start | bytes 3145736 | tf_op jit(solution)/shard_map/ppermute | solution.py:229
  275.0 59.8 %collective-permute-start.36 = (bf16[4,128,1024]{2,1,0:T(8,128)(2,1)}, bf16[4,128,1024]{2,1,0:T(8,128)(2,1)}, u32[]{:S(2)}, u32[]{:S(2)}) collective-permute-start(bf16[4,128,1024]{2,1,0:T(8,128)(2,1)} %get-tuple-element.116), channel_id=1, source_target_pairs={{0,4},{4,0},{8,12},{12,8},{16,20},{20,16},{24,28},{28,24},{1,5},{5... | collective-permute-start | bytes 3145736 | tf_op jit(solution)/shard_map/ppermute | solution.py:229
  275.3 62.2 %collective-permute-start.37 = (bf16[4,128,1024]{2,1,0:T(8,128)(2,1)}, bf16[4,128,1024]{2,1,0:T(8,128)(2,1)}, u32[]{:S(2)}, u32[]{:S(2)}) collective-permute-start(bf16[4,128,1024]{2,1,0:T(8,128)(2,1)} %get-tuple-element.117), channel_id=1, source_target_pairs={{0,8},{4,12},{8,0},{12,4},{16,24},{20,28},{24,16},{28,20},{1,9},{5... | collective-permute-start | bytes 3145736 | tf_op jit(solution)/shard_map/ppermute | solution.py:229
  297.5 51.5 %collective-permute-start.38 = (bf16[4,128,1024]{2,1,0:T(8,128)(2,1)}, bf16[4,128,1024]{2,1,0:T(8,128)(2,1)}, u32[]{:S(2)}, u32[]{:S(2)}) collective-permute-start(bf16[4,128,1024]{2,1,0:T(8,128)(2,1)} %get-tuple-element.105.refs_6_), channel_id=1, source_target_pairs={{0,12},{4,8},{8,4},{12,0},{16,28},{20,24},{24,20},{28,16},{1,13},{... | collective-permute-start | bytes 3145736 | tf_op jit(solution)/shard_map/ppermute | solution.py:229
  357.6 48.9 %collective-permute-start.31 = (bf16[4,128,1024]{2,1,0:T(8,128)(2,1)}, bf16[4,128,1024]{2,1,0:T(8,128)(2,1)}, u32[]{:S(2)}, u32[]{:S(2)}) collective-permute-start(bf16[4,128,1024]{2,1,0:T(8,128)(2,1)} %get-tuple-element.111), channel_id=1, source_target_pairs={{0,8},{4,12},{8,0},{12,4},{16,24},{20,28},{24,16},{28,20},{1,9},{5... | collective-permute-start | bytes 3145736 | tf_op jit(solution)/shard_map/ppermute | solution.py:229
  361.1 52.9 %collective-permute-start.32 = (bf16[4,128,1024]{2,1,0:T(8,128)(2,1)}, bf16[4,128,1024]{2,1,0:T(8,128)(2,1)}, u32[]{:S(2)}, u32[]{:S(2)}) collective-permute-start(bf16[4,128,1024]{2,1,0:T(8,128)(2,1)} %get-tuple-element.112.refs_6_), channel_id=1, source_target_pairs={{0,12},{4,8},{8,4},{12,0},{16,28},{20,24},{24,20},{28,16},{1,13},{... | collective-permute-start | bytes 3145736 | tf_op jit(solution)/shard_map/ppermute | solution.py:229
  419.1 58.0 %collective-permute-start.56 = (bf16[4,128,1024]{2,1,0:T(8,128)(2,1)}, bf16[4,128,1024]{2,1,0:T(8,128)(2,1)S(1)}, u32[]{:S(2)}, u32[]{:S(2)}) collective-permute-start(bf16[4,128,1024]{2,1,0:T(8,128)(2,1)} %get-tuple-element.134), channel_id=1, source_target_pairs={{0,4},{4,0},{8,12},{12,8},{16,20},{20,16},{24,28},{28,24},{1,5},{5... | collective-permute-start | bytes 3145736 | tf_op jit(solution)/shard_map/ppermute | solution.py:229
  419.1 58.1 %collective-permute-start.57 = (bf16[4,128,1024]{2,1,0:T(8,128)(2,1)S(1)}, bf16[4,128,1024]{2,1,0:T(8,128)(2,1)S(1)}, u32[]{:S(2)}, u32[]{:S(2)}) collective-permute-start(bf16[4,128,1024]{2,1,0:T(8,128)(2,1)S(1)} %get-tuple-element.135), channel_id=1, source_target_pairs={{0,8},{4,12},{8,0},{12,4},{16,24},{20,28},{24,16},{28,20},{1,9},{5... | collective-permute-start | bytes 3145736 | tf_op jit(solution)/shard_map/ppermute | solution.py:229
  430.5 53.0 %collective-permute-start.58 = (bf16[4,128,1024]{2,1,0:T(8,128)(2,1)}, bf16[4,128,1024]{2,1,0:T(8,128)(2,1)S(1)}, u32[]{:S(2)}, u32[]{:S(2)}) collective-permute-start(bf16[4,128,1024]{2,1,0:T(8,128)(2,1)} %get-tuple-element.122.refs_8_), channel_id=1, source_target_pairs={{0,12},{4,8},{8,4},{12,0},{16,28},{20,24},{24,20},{28,16},{1,13},{... | collective-permute-start | bytes 3145736 | tf_op jit(solution)/shard_map/ppermute | solution.py:229
  530.9 51.3 %collective-permute-start.72 = (bf16[4,272,256]{2,1,0:T(8,128)(2,1)}, bf16[4,272,256]{2,1,0:T(8,128)(2,1)S(1)}, u32[]{:S(2)}, u32[]{:S(2)}) collective-permute-start(bf16[4,272,256]{2,1,0:T(8,128)(2,1)} %shard_map.127.refs_4_.refs_0_.refs_2_), channel_id=1, source_target_pairs={{0,2},{1,3},{2,0},{3,1},{4,6},{5,7},{6,4},{7,5},{8,10},{9,11},{10,... | collective-permute-start | bytes 1671176 | tf_op jit(solution)/shard_map/ppermute | solution.py:232
  542.8 48.0 %collective-permute-start.73 = (bf16[4,272,256]{2,1,0:T(8,128)(2,1)}, bf16[4,272,256]{2,1,0:T(8,128)(2,1)S(1)}, u32[]{:S(2)}, u32[]{:S(2)}) collective-permute-start(bf16[4,272,256]{2,1,0:T(8,128)(2,1)} %shard_map.127.refs_4_.refs_0_.refs_2_), channel_id=1, source_target_pairs={{0,3},{1,2},{2,1},{3,0},{4,7},{5,6},{6,5},{7,4},{8,11},{9,10},{10,... | collective-permute-start | bytes 1671176 | tf_op jit(solution)/shard_map/ppermute | solution.py:232
  (125 other events, 2050.8 us)

commit v5 on v4

--- a/solution.py
+++ b/solution.py
@@ -12,7 +12,7 @@
 E = 8
 CAP = 34
 HALVES = 2
-GRAD_STEPS = 4
+GRAD_STEPS = 8
 KERNEL_VMEM = 51 << 20
 LANES = 128
 SUBLANES = 8
@@ -342,6 +342,11 @@
     return pl.ds(pl.multiple_of((where[1] ^ m) * sub, LANES), sub)
 
 
+def member_groups(plan, sub):
+    take = max(1, min(plan.members, 2 * LANES // sub))
+    return [range(m, m + take) for m in range(0, plan.members, take)]
+
+
 def stacked_rows(refs, i, lanes):
     return jnp.concatenate([refs[i][0, :, lanes]] + [ref[i, :, lanes] for ref in refs[2:]], axis=0)
 
@@ -352,12 +357,14 @@
 
     def kernel(where, rows_ref, *refs):
         w_refs, outs = refs[: 2 + plan.peers], refs[-plan.members :]
-        for m in range(plan.members):
-            lanes = member_lanes(where, m, sub)
+        for ms in member_groups(plan, sub):
             for i in range(2):
-                outs[m][i] = jnp.dot(
-                    rows_ref[i], stacked_rows(w_refs, i, lanes), preferred_element_type=F32
+                weights = [stacked_rows(w_refs, i, member_lanes(where, m, sub)) for m in ms]
+                value = jnp.dot(
+                    rows_ref[i], jnp.concatenate(weights, axis=1), preferred_element_type=F32
                 ).astype(BF)
+                for j, m in enumerate(ms):
+                    outs[m][i] = value[:, j * sub : (j + 1) * sub]
 
     return plan.call(
         kernel,
@@ -428,9 +435,10 @@
         out, acc, wide = refs[-3:] if final else (refs[-1], None, None)
         for i in range(2):
             value = None
-            for m in range(plan.members):
-                weights = stacked_rows(w_refs, 1 - i, member_lanes(where, m, sub))
-                term = contract(p_refs[m][i], weights, 1, 1)
+            for ms in member_groups(plan, sub):
+                weights = [stacked_rows(w_refs, 1 - i, member_lanes(where, m, sub)) for m in ms]
+                hidden = jnp.concatenate([p_refs[m][i] for m in ms], axis=1)
+                term = contract(hidden, jnp.concatenate(weights, axis=1), 1, 1)
                 value = term if value is None else value + term
             for k in range(plan.size):
                 at = pl.ds(pl.multiple_of((place ^ k) * share, LANES), share)
@@ -491,14 +499,12 @@
 
     def kernel(where, x_ref, d_ref, *refs):
         up_out, down_out = refs[-2:]
-        for m in range(plan.members):
-            lanes = member_lanes(where, m, sub)
-            down_out[0, :, lanes] = jnp.dot(
-                d_ref[...], refs[m][0], preferred_element_type=F32
-            ).astype(BF)
-            up_out[0, :, lanes] = jnp.dot(
-                x_ref[...], refs[m][1], preferred_element_type=F32
-            ).astype(BF)
+        for ms in member_groups(plan, sub):
+            for i, (rows_ref, out) in enumerate(((d_ref, down_out), (x_ref, up_out))):
+                hidden = jnp.concatenate([refs[m][i] for m in ms], axis=1)
+                value = jnp.dot(rows_ref[...], hidden, preferred_element_type=F32).astype(BF)
+                for j, m in enumerate(ms):
+                    out[0, :, member_lanes(where, m, sub)] = value[:, j * sub : (j + 1) * sub]
 
     in_specs = [pl.BlockSpec((block, slots), lambda q, where: (q, 0))] * 2
     in_specs += [full_spec((2, slots, sub))] * plan.members
@@ -522,19 +528,19 @@
 
 def chunk_list(hidden, unit):
     units = hidden // unit
-    wide = max(0, (units - 1) // 2)
+    wide = max(0, (units - 6) // 2)
     narrow = [(2 * wide + i, 1) for i in range(units - 2 * wide)]
-    chunks = narrow[:-1] + [(2 * i, 2) for i in range(wide)] + narrow[-1:]
+    chunks = narrow[:1] + [(2 * i, 2) for i in range(wide)] + narrow[1:]
     return [(unit * start, unit * width) for start, width in chunks]
 
 
 LAGS = (
     ("hidden", 0),
+    ("sums", 1),
+    ("grads", 4),
+    ("fetch", -2),
+    ("activate", 2),
     ("features", 3),
-    ("activate", 1),
-    ("sums", 0),
-    ("fetch", -2),
-    ("grads", 3),
 )
 
 

time: 657 us -> 669 us (1.018)
  waiting for transfers between devices: 365 us -> 310 us
  Pallas kernels: 170 us -> 204 us
  starting transfers between devices: 93.4 us -> 122 us
    ppermute x48 -> x60, waiting for transfers between devices: 198 us -> 89.7 us  [pass_on(): lax.ppermute(value, 'member', [(i, i ^ k) for i in range(self.members)])]
    ppermute x32 -> x40, waiting for transfers between devices: 158 us -> 216 us  [swap(): return lax.ppermute(value, 'dp', [(i, i ^ k) for i in range(self.dp_count)])]
    pallas_call x49 -> x61, Pallas kernels: 165 us -> 199 us  [call(): pl.pallas_call(placed, grid_spec=pltpu.PrefetchScalarGridSpec(num_scalar_...]
    ppermute x48 -> x60, starting transfers between devices: 58.2 us -> 74.9 us  [pass_on(): lax.ppermute(value, 'member', [(i, i ^ k) for i in range(self.members)])]
    ppermute x32 -> x40, starting transfers between devices: 25.2 us -> 37.2 us  [swap(): return lax.ppermute(value, 'dp', [(i, i ^ k) for i in range(self.dp_count)])]
    unnamed x135 -> x159, local copies, waits for them, and re-layouts: 22.4 us -> 23.9 us
  transfers between devices with their start and end apart: 82 -> 102, of which waited for: 30 -> 29; matrix products, arithmetic and copies ran while one was open for 0% -> 1% of each run, Pallas kernels for 24% -> 29%
where the time goes in v5:
time: 669 us; the launch traced here: 667 us
  waiting for transfers between devices  310 us (46%)
  Pallas kernels  204 us (30%)
  starting transfers between devices  122 us (18%)
  local copies, waits for them, and re-layouts  28.8 us (4%)
    ppermute x40, waiting for transfers between devices, swap(): return lax.ppermute(value, 'dp', [(i, i ^ k) for i in range(self.dp_count)])  216 us
    pallas_call x61, Pallas kernels, call(): pl.pallas_call(placed, grid_spec=pltpu.PrefetchScalarGridSpec(num_scalar_...  199 us
    ppermute x60, waiting for transfers between devices, pass_on(): lax.ppermute(value, 'member', [(i, i ^ k) for i in range(self.members)])  89.7 us
    ppermute x60, starting transfers between devices, pass_on(): lax.ppermute(value, 'member', [(i, i ^ k) for i in range(self.members)])  74.9 us
    ppermute x40, starting transfers between devices, swap(): return lax.ppermute(value, 'dp', [(i, i ^ k) for i in range(self.dp_count)])  37.2 us
    unnamed x159, local copies, waits for them, and re-layouts  23.9 us
  transfers between devices with their start and end apart: 102, of which 29 were waited for; matrix products, arithmetic and copies ran while one was open for 1% of the time, Pallas kernels for 29%

profile of v5, /device:TPU:0, one launch (start us, length us, event | category | flops | bytes accessed | tf_op | source)
XLA Modules:
  0.0 666.6 jit_solution(7592647043238926559)
XLA Ops:
  6.0 6.3 all-to-all-start
  23.2 30.5 %collective-permute-done.2.refs_4_.refs_8_ = bf16[4,128,512]{2,1,0:T(8,128)(2,1)S(1)} collective-permute-done((bf16[4,128,512]{2,1,0:T(8,128)(2,1)S(1)}, bf16[4,128,512]{2,1,0:T(8,128)(2,1)S(1)}, u32[]{:S(2)}, u32[]{:S(2)}) %collective-permute-start.2) | collective-permute-done | bytes 524320 | tf_op jit(solution)/shard_map/ppermute | solution.py:229
  60.4 50.0 %collective-permute-done.1.refs_3_.refs_7_ = bf16[4,128,512]{2,1,0:T(8,128)(2,1)S(1)} collective-permute-done((bf16[4,128,512]{2,1,0:T(8,128)(2,1)S(1)}, bf16[4,128,512]{2,1,0:T(8,128)(2,1)S(1)}, u32[]{:S(2)}, u32[]{:S(2)}) %collective-permute-start.1) | collective-permute-done | bytes 524320 | tf_op jit(solution)/shard_map/ppermute | solution.py:229
  120.9 6.0 collective-permute-done.3.refs_1_
  139.7 7.4 %collective-permute-done.13.refs_1_ = bf16[4,272,256]{2,1,0:T(8,128)(2,1)S(1)} collective-permute-done((bf16[4,272,256]{2,1,0:T(8,128)(2,1)S(1)}, bf16[4,272,256]{2,1,0:T(8,128)(2,1)S(1)}, u32[]{:S(2)}, u32[]{:S(2)}) %collective-permute-start.13) | collective-permute-done | bytes 557088 | tf_op jit(solution)/shard_map/ppermute | solution.py:232
  151.7 12.7 %collective-permute-done.18.refs_5_.refs_8_ = bf16[4,128,1024]{2,1,0:T(8,128)(2,1)S(1)} collective-permute-done((bf16[4,128,1024]{2,1,0:T(8,128)(2,1)}, bf16[4,128,1024]{2,1,0:T(8,128)(2,1)S(1)}, u32[]{:S(2)}, u32[]{:S(2)}) %collective-permute-start.18) | collective-permute-done | bytes 1048608 | tf_op jit(solution)/shard_map/ppermute | solution.py:229
  176.4 37.3 %collective-permute-done.12.refs_1_ = bf16[4,272,128]{2,1,0:T(8,128)(2,1)S(1)} collective-permute-done((bf16[4,272,128]{2,1,0:T(8,128)(2,1)S(1)}, bf16[4,272,128]{2,1,0:T(8,128)(2,1)S(1)}, u32[]{:S(2)}, u32[]{:S(2)}) %collective-permute-start.12) | collective-permute-done | bytes 278560 | tf_op jit(solution)/shard_map/ppermute | solution.py:229
  237.7 19.4 %collective-permute-done.29.refs_1_ = bf16[4,272,256]{2,1,0:T(8,128)(2,1)S(1)} collective-permute-done((bf16[4,272,256]{2,1,0:T(8,128)(2,1)}, bf16[4,272,256]{2,1,0:T(8,128)(2,1)S(1)}, u32[]{:S(2)}, u32[]{:S(2)}) %collective-permute-start.29) | collective-permute-done | bytes 557088 | tf_op jit(solution)/shard_map/ppermute | solution.py:232
  273.9 10.1 %collective-permute-done.20.refs_2_ = bf16[4,272,256]{2,1,0:T(8,128)(2,1)S(1)} collective-permute-done((bf16[4,272,256]{2,1,0:T(8,128)(2,1)S(1)}, bf16[4,272,256]{2,1,0:T(8,128)(2,1)S(1)}, u32[]{:S(2)}, u32[]{:S(2)}) %collective-permute-start.20) | collective-permute-done | bytes 557088 | tf_op jit(solution)/shard_map/ppermute | solution.py:232
  296.4 26.0 %collective-permute-done.24.refs_5_.refs_8_ = bf16[4,128,1024]{2,1,0:T(8,128)(2,1)} collective-permute-done((bf16[4,128,1024]{2,1,0:T(8,128)(2,1)}, bf16[4,128,1024]{2,1,0:T(8,128)(2,1)}, u32[]{:S(2)}, u32[]{:S(2)}) %collective-permute-start.24) | collective-permute-done | bytes 1048608 | tf_op jit(solution)/shard_map/ppermute | solution.py:229
  323.5 11.5 %collective-permute-done.40.refs_4_.refs_7_ = bf16[4,128,512]{2,1,0:T(8,128)(2,1)S(1)} collective-permute-done((bf16[4,128,512]{2,1,0:T(8,128)(2,1)}, bf16[4,128,512]{2,1,0:T(8,128)(2,1)S(1)}, u32[]{:S(2)}, u32[]{:S(2)}) %collective-permute-start.40) | collective-permute-done | bytes 524320 | tf_op jit(solution)/shard_map/ppermute | solution.py:229
  351.3 7.0 %shard_map.112 = (bf16[1,1024,7168]{2,1,0:T(8,128)(2,1)}, bf16[1,1024,7168]{2,1,0:T(8,128)(2,1)}) custom-call(s32[2]{0:T(128)S(1)} %pad_add_fusion.where, bf16[1024,272]{1,0:T(8,128)(2,1)S(1)} %get-tuple-element.193.refs_0_.x_ref, bf16[1024,272]{1,0:T(8,128)(2,1)} %get-tuple-element.192.refs_1_.d_ref, ...), custom_call_target="tpu_custom_call" | custom-call | flops 570425344 | bytes 2654208 | tf_op jit(solution)/shard_map/pallas_call | solution.py:244
  367.6 14.2 %collective-permute-done.53.refs_4_.refs_7_ = bf16[4,128,512]{2,1,0:T(8,128)(2,1)S(1)} collective-permute-done((bf16[4,128,512]{2,1,0:T(8,128)(2,1)S(1)}, bf16[4,128,512]{2,1,0:T(8,128)(2,1)S(1)}, u32[]{:S(2)}, u32[]{:S(2)}) %collective-permute-start.53) | collective-permute-done | bytes 524320 | tf_op jit(solution)/shard_map/ppermute | solution.py:229
  390.5 5.6 shard_map.115.refs_6_.refs_9_
  402.6 8.2 %shard_map.118 = (bf16[1,1024,7168]{2,1,0:T(8,128)(2,1)}, bf16[1,1024,7168]{2,1,0:T(8,128)(2,1)}) custom-call(s32[2]{0:T(128)S(1)} %pad_add_fusion.where, bf16[1024,272]{1,0:T(8,128)(2,1)} %copy-done.1, bf16[1024,272]{1,0:T(8,128)(2,1)} %get-tuple-element.192.refs_1_.d_ref, ...), custom_call_target="tpu_custom_call", output_to_operand_aliasing={{0}: (7, {}), {1}: (8, {})} | custom-call | flops 1140850688 | bytes 5308416 | tf_op jit(solution)/shard_map/pallas_call | solution.py:244
  416.6 5.6 shard_map.121.refs_6_.refs_9_
  432.7 5.8 collective-permute-done.55.refs_1_
  443.3 8.1 %shard_map.124 = (bf16[1,1024,7168]{2,1,0:T(8,128)(2,1)}, bf16[1,1024,7168]{2,1,0:T(8,128)(2,1)}) custom-call(s32[2]{0:T(128)S(1)} %pad_add_fusion.where, bf16[1024,272]{1,0:T(8,128)(2,1)} %copy-done.1, bf16[1024,272]{1,0:T(8,128)(2,1)} %get-tuple-element.192.refs_1_.d_ref, ...), custom_call_target="tpu_custom_call", output_to_operand_aliasing={{0}: (7, {}), {1}: (8, {})} | custom-call | flops 1140850688 | bytes 5308416 | tf_op jit(solution)/shard_map/pallas_call | solution.py:244
  453.6 11.6 %collective-permute-done.61.refs_1_ = bf16[4,272,256]{2,1,0:T(8,128)(2,1)S(1)} collective-permute-done((bf16[4,272,256]{2,1,0:T(8,128)(2,1)S(1)}, bf16[4,272,256]{2,1,0:T(8,128)(2,1)S(1)}, u32[]{:S(2)}, u32[]{:S(2)}) %collective-permute-start.61) | collective-permute-done | bytes 557088 | tf_op jit(solution)/shard_map/ppermute | solution.py:229
  478.0 14.7 %collective-permute-done.65.refs_1_ = bf16[4,272,128]{2,1,0:T(8,128)(2,1)S(1)} collective-permute-done((bf16[4,272,128]{2,1,0:T(8,128)(2,1)S(1)}, bf16[4,272,128]{2,1,0:T(8,128)(2,1)S(1)}, u32[]{:S(2)}, u32[]{:S(2)}) %collective-permute-start.65) | collective-permute-done | bytes 278560 | tf_op jit(solution)/shard_map/ppermute | solution.py:229
  498.5 8.1 %shard_map.130 = (bf16[1,1024,7168]{2,1,0:T(8,128)(2,1)}, bf16[1,1024,7168]{2,1,0:T(8,128)(2,1)}) custom-call(s32[2]{0:T(128)S(1)} %pad_add_fusion.where, bf16[1024,272]{1,0:T(8,128)(2,1)} %copy-done.1, bf16[1024,272]{1,0:T(8,128)(2,1)} %get-tuple-element.192.refs_1_.d_ref, ...), custom_call_target="tpu_custom_call", output_to_operand_aliasing={{0}: (7, {}), {1}: (8, {})} | custom-call | flops 1140850688 | bytes 5308416 | tf_op jit(solution)/shard_map/pallas_call | solution.py:244
  515.6 7.2 %collective-permute-done.72.refs_1_ = bf16[4,272,128]{2,1,0:T(8,128)(2,1)S(1)} collective-permute-done((bf16[4,272,128]{2,1,0:T(8,128)(2,1)S(1)}, bf16[4,272,128]{2,1,0:T(8,128)(2,1)S(1)}, u32[]{:S(2)}, u32[]{:S(2)}) %collective-permute-start.72) | collective-permute-done | bytes 278560 | tf_op jit(solution)/shard_map/ppermute | solution.py:229
  522.8 7.5 %collective-permute-done.66.refs_1_.refs_3_ = bf16[4,272,128]{2,1,0:T(8,128)(2,1)S(1)} collective-permute-done((bf16[4,272,128]{2,1,0:T(8,128)(2,1)S(1)}, bf16[4,272,128]{2,1,0:T(8,128)(2,1)S(1)}, u32[]{:S(2)}, u32[]{:S(2)}) %collective-permute-start.66) | collective-permute-done | bytes 278560 | tf_op jit(solution)/shard_map/ppermute | solution.py:232
  550.5 8.1 %shard_map.136 = (bf16[1,1024,7168]{2,1,0:T(8,128)(2,1)}, bf16[1,1024,7168]{2,1,0:T(8,128)(2,1)}) custom-call(s32[2]{0:T(128)S(1)} %pad_add_fusion.where, bf16[1024,272]{1,0:T(8,128)(2,1)} %copy-done.1, bf16[1024,272]{1,0:T(8,128)(2,1)} %get-tuple-element.192.refs_1_.d_ref, ...), custom_call_target="tpu_custom_call", output_to_operand_aliasing={{0}: (7, {}), {1}: (8, {})} | custom-call | flops 1140850688 | bytes 5308416 | tf_op jit(solution)/shard_map/pallas_call | solution.py:244
  (405 shorter events, 336.1 us)
Async XLA Ops:
  6.0 48.4 %all-to-all-start = ((bf16[8,104,1024]{2,1,0:T(8,128)(2,1)}), bf16[8,104,1024]{2,1,0:T(8,128)(2,1)}, u32[]{:S(2)}, u32[]{:S(2)}) async-start(bf16[8,104,1024]{2,1,0:T(8,128)(2,1)} %route.1), calls=%async_computation | async-start | bytes 3407872 | tf_op jit(solution)/shard_map/all_to_all | solution.py:591
  15.3 38.3 %collective-permute-start.2 = (bf16[4,128,512]{2,1,0:T(8,128)(2,1)S(1)}, bf16[4,128,512]{2,1,0:T(8,128)(2,1)S(1)}, u32[]{:S(2)}, u32[]{:S(2)}) collective-permute-start(bf16[4,128,512]{2,1,0:T(8,128)(2,1)S(1)} %get-tuple-element.98.refs_12_), channel_id=1, source_target_pairs={{0,12},{4,8},{8,4},{12,0},{16,28},{20,24},{24,20},{28,16},{1,13},{... | collective-permute-start | bytes 1572872 | tf_op jit(solution)/shard_map/ppermute | solution.py:229
  20.8 96.5 %collective-permute-start.8 = (bf16[4,128,1024]{2,1,0:T(8,128)(2,1)}, bf16[4,128,1024]{2,1,0:T(8,128)(2,1)}, u32[]{:S(2)}, u32[]{:S(2)}) collective-permute-start(bf16[4,128,1024]{2,1,0:T(8,128)(2,1)} %get-tuple-element.99.refs_1_), channel_id=1, source_target_pairs={{0,12},{4,8},{8,4},{12,0},{16,28},{20,24},{24,20},{28,16},{1,13},{... | collective-permute-start | bytes 3145736 | tf_op jit(solution)/shard_map/ppermute | solution.py:229
  20.9 97.9 %collective-permute-start.6 = (bf16[4,128,1024]{2,1,0:T(8,128)(2,1)}, bf16[4,128,1024]{2,1,0:T(8,128)(2,1)}, u32[]{:S(2)}, u32[]{:S(2)}) collective-permute-start(bf16[4,128,1024]{2,1,0:T(8,128)(2,1)} %get-tuple-element.108), channel_id=1, source_target_pairs={{0,4},{4,0},{8,12},{12,8},{16,20},{20,16},{24,28},{28,24},{1,5},{5... | collective-permute-start | bytes 3145736 | tf_op jit(solution)/shard_map/ppermute | solution.py:229
  21.4 98.9 %collective-permute-start.7 = (bf16[4,128,1024]{2,1,0:T(8,128)(2,1)S(1)}, bf16[4,128,1024]{2,1,0:T(8,128)(2,1)}, u32[]{:S(2)}, u32[]{:S(2)}) collective-permute-start(bf16[4,128,1024]{2,1,0:T(8,128)(2,1)S(1)} %get-tuple-element.109), channel_id=1, source_target_pairs={{0,8},{4,12},{8,0},{12,4},{16,24},{20,28},{24,16},{28,20},{1,9},{5... | collective-permute-start | bytes 3145736 | tf_op jit(solution)/shard_map/ppermute | solution.py:229
  23.0 37.3 %collective-permute-start = (bf16[4,128,512]{2,1,0:T(8,128)(2,1)}, bf16[4,128,512]{2,1,0:T(8,128)(2,1)S(1)}, u32[]{:S(2)}, u32[]{:S(2)}) collective-permute-start(bf16[4,128,512]{2,1,0:T(8,128)(2,1)} %get-tuple-element.102), channel_id=1, source_target_pairs={{0,4},{4,0},{8,12},{12,8},{16,20},{20,16},{24,28},{28,24},{1,5},{5... | collective-permute-start | bytes 1572872 | tf_op jit(solution)/shard_map/ppermute | solution.py:229
  53.6 56.8 %collective-permute-start.1 = (bf16[4,128,512]{2,1,0:T(8,128)(2,1)S(1)}, bf16[4,128,512]{2,1,0:T(8,128)(2,1)S(1)}, u32[]{:S(2)}, u32[]{:S(2)}) collective-permute-start(bf16[4,128,512]{2,1,0:T(8,128)(2,1)S(1)} %get-tuple-element.103), channel_id=1, source_target_pairs={{0,8},{4,12},{8,0},{12,4},{16,24},{20,28},{24,16},{28,20},{1,9},{5... | collective-permute-start | bytes 1572872 | tf_op jit(solution)/shard_map/ppermute | solution.py:229
  126.9 37.4 %collective-permute-start.18 = (bf16[4,128,1024]{2,1,0:T(8,128)(2,1)}, bf16[4,128,1024]{2,1,0:T(8,128)(2,1)S(1)}, u32[]{:S(2)}, u32[]{:S(2)}) collective-permute-start(bf16[4,128,1024]{2,1,0:T(8,128)(2,1)} %get-tuple-element.110.refs_6_), channel_id=1, source_target_pairs={{0,12},{4,8},{8,4},{12,0},{16,28},{20,24},{24,20},{28,16},{1,13},{... | collective-permute-start | bytes 3145736 | tf_op jit(solution)/shard_map/ppermute | solution.py:229
  147.1 78.6 %collective-permute-start.10 = (bf16[4,128,1024]{2,1,0:T(8,128)(2,1)S(1)}, bf16[4,128,1024]{2,1,0:T(8,128)(2,1)}, u32[]{:S(2)}, u32[]{:S(2)}) collective-permute-start(bf16[4,128,1024]{2,1,0:T(8,128)(2,1)S(1)} %get-tuple-element.113), channel_id=1, source_target_pairs={{0,8},{4,12},{8,0},{12,4},{16,24},{20,28},{24,16},{28,20},{1,9},{5... | collective-permute-start | bytes 3145736 | tf_op jit(solution)/shard_map/ppermute | solution.py:229
  148.3 80.7 %collective-permute-start.11 = (bf16[4,128,1024]{2,1,0:T(8,128)(2,1)}, bf16[4,128,1024]{2,1,0:T(8,128)(2,1)S(1)}, u32[]{:S(2)}, u32[]{:S(2)}) collective-permute-start(bf16[4,128,1024]{2,1,0:T(8,128)(2,1)} %get-tuple-element.114.refs_6_), channel_id=1, source_target_pairs={{0,12},{4,8},{8,4},{12,0},{16,28},{20,24},{24,20},{28,16},{1,13},{... | collective-permute-start | bytes 3145736 | tf_op jit(solution)/shard_map/ppermute | solution.py:229
  148.3 82.2 %collective-permute-start.9 = (bf16[4,128,1024]{2,1,0:T(8,128)(2,1)S(1)}, bf16[4,128,1024]{2,1,0:T(8,128)(2,1)}, u32[]{:S(2)}, u32[]{:S(2)}) collective-permute-start(bf16[4,128,1024]{2,1,0:T(8,128)(2,1)S(1)} %get-tuple-element.112), channel_id=1, source_target_pairs={{0,4},{4,0},{8,12},{12,8},{16,20},{20,16},{24,28},{28,24},{1,5},{5... | collective-permute-start | bytes 3145736 | tf_op jit(solution)/shard_map/ppermute | solution.py:229
  164.3 49.4 %collective-permute-start.12 = (bf16[4,272,128]{2,1,0:T(8,128)(2,1)S(1)}, bf16[4,272,128]{2,1,0:T(8,128)(2,1)S(1)}, u32[]{:S(2)}, u32[]{:S(2)}) collective-permute-start(bf16[4,272,128]{2,1,0:T(8,128)(2,1)S(1)} %shard_map.99.refs_12_.refs_0_), channel_id=1, source_target_pairs={{0,16},{4,20},{8,24},{12,28},{16,0},{20,4},{24,8},{28,12},{1,17},{... | collective-permute-start | bytes 835592 | tf_op jit(solution)/shard_map/ppermute | solution.py:229
  269.8 52.6 %collective-permute-start.24 = (bf16[4,128,1024]{2,1,0:T(8,128)(2,1)}, bf16[4,128,1024]{2,1,0:T(8,128)(2,1)}, u32[]{:S(2)}, u32[]{:S(2)}) collective-permute-start(bf16[4,128,1024]{2,1,0:T(8,128)(2,1)} %get-tuple-element.121.refs_2_), channel_id=1, source_target_pairs={{0,12},{4,8},{8,4},{12,0},{16,28},{20,24},{24,20},{28,16},{1,13},{... | collective-permute-start | bytes 3145736 | tf_op jit(solution)/shard_map/ppermute | solution.py:229
  284.8 38.1 %collective-permute-start.39 = (bf16[4,128,512]{2,1,0:T(8,128)(2,1)}, bf16[4,128,512]{2,1,0:T(8,128)(2,1)S(1)}, u32[]{:S(2)}, u32[]{:S(2)}) collective-permute-start(bf16[4,128,512]{2,1,0:T(8,128)(2,1)} %get-tuple-element.138), channel_id=1, source_target_pairs={{0,4},{4,0},{8,12},{12,8},{16,20},{20,16},{24,28},{28,24},{1,5},{5... | collective-permute-start | bytes 1572872 | tf_op jit(solution)/shard_map/ppermute | solution.py:229
  285.7 49.3 %collective-permute-start.40 = (bf16[4,128,512]{2,1,0:T(8,128)(2,1)}, bf16[4,128,512]{2,1,0:T(8,128)(2,1)S(1)}, u32[]{:S(2)}, u32[]{:S(2)}) collective-permute-start(bf16[4,128,512]{2,1,0:T(8,128)(2,1)} %get-tuple-element.139), channel_id=1, source_target_pairs={{0,8},{4,12},{8,0},{12,4},{16,24},{20,28},{24,16},{28,20},{1,9},{5... | collective-permute-start | bytes 1572872 | tf_op jit(solution)/shard_map/ppermute | solution.py:229
  290.2 70.4 %collective-permute-start.42 = (bf16[4,272,256]{2,1,0:T(8,128)(2,1)S(1)}, bf16[4,272,256]{2,1,0:T(8,128)(2,1)}, u32[]{:S(2)}, u32[]{:S(2)}) collective-permute-start(bf16[4,272,256]{2,1,0:T(8,128)(2,1)S(1)} %shard_map.106.refs_12_.refs_0_), channel_id=1, source_target_pairs={{0,16},{4,20},{8,24},{12,28},{16,0},{20,4},{24,8},{28,12},{1,17},{... | collective-permute-start | bytes 1671176 | tf_op jit(solution)/shard_map/ppermute | solution.py:229
  291.1 69.3 %collective-permute-start.41 = (bf16[4,128,512]{2,1,0:T(8,128)(2,1)}, bf16[4,128,512]{2,1,0:T(8,128)(2,1)}, u32[]{:S(2)}, u32[]{:S(2)}) collective-permute-start(bf16[4,128,512]{2,1,0:T(8,128)(2,1)} %get-tuple-element.131.refs_2_), channel_id=1, source_target_pairs={{0,12},{4,8},{8,4},{12,0},{16,28},{20,24},{24,20},{28,16},{1,13},{... | collective-permute-start | bytes 1572872 | tf_op jit(solution)/shard_map/ppermute | solution.py:229
  322.4 38.3 %collective-permute-start.33 = (bf16[4,272,256]{2,1,0:T(8,128)(2,1)}, bf16[4,272,256]{2,1,0:T(8,128)(2,1)S(1)}, u32[]{:S(2)}, u32[]{:S(2)}) collective-permute-start(bf16[4,272,256]{2,1,0:T(8,128)(2,1)} %shard_map.108.refs_9_.refs_0_.refs_2_), channel_id=1, source_target_pairs={{0,1},{1,0},{2,3},{3,2},{4,5},{5,4},{6,7},{7,6},{8,9},{9,8},{10,11... | collective-permute-start | bytes 1671176 | tf_op jit(solution)/shard_map/ppermute | solution.py:232
  322.9 39.2 %collective-permute-start.34 = (bf16[4,272,256]{2,1,0:T(8,128)(2,1)}, bf16[4,272,256]{2,1,0:T(8,128)(2,1)S(1)}, u32[]{:S(2)}, u32[]{:S(2)}) collective-permute-start(bf16[4,272,256]{2,1,0:T(8,128)(2,1)} %shard_map.108.refs_9_.refs_0_.refs_2_), channel_id=1, source_target_pairs={{0,2},{1,3},{2,0},{3,1},{4,6},{5,7},{6,4},{7,5},{8,10},{9,11},{10,... | collective-permute-start | bytes 1671176 | tf_op jit(solution)/shard_map/ppermute | solution.py:232
  364.2 36.1 %collective-permute-start.32 = (bf16[4,272,256]{2,1,0:T(8,128)(2,1)S(1)}, bf16[4,272,256]{2,1,0:T(8,128)(2,1)S(1)}, u32[]{:S(2)}, u32[]{:S(2)}) collective-permute-start(bf16[4,272,256]{2,1,0:T(8,128)(2,1)S(1)} %shard_map.111.refs_6_.refs_0_), channel_id=1, source_target_pairs={{0,16},{4,20},{8,24},{12,28},{16,0},{20,4},{24,8},{28,12},{1,17},{... | collective-permute-start | bytes 1671176 | tf_op jit(solution)/shard_map/ppermute | solution.py:229
  453.5 39.1 %collective-permute-start.76 = (bf16[4,128,512]{2,1,0:T(8,128)(2,1)S(1)}, bf16[4,128,512]{2,1,0:T(8,128)(2,1)S(1)}, u32[]{:S(2)}, u32[]{:S(2)}) collective-permute-start(bf16[4,128,512]{2,1,0:T(8,128)(2,1)S(1)} %get-tuple-element.168), channel_id=1, source_target_pairs={{0,4},{4,0},{8,12},{12,8},{16,20},{20,16},{24,28},{28,24},{1,5},{5... | collective-permute-start | bytes 1572872 | tf_op jit(solution)/shard_map/ppermute | solution.py:229
  494.2 38.1 %collective-permute-start.69 = (bf16[4,272,256]{2,1,0:T(8,128)(2,1)S(1)}, bf16[4,272,256]{2,1,0:T(8,128)(2,1)S(1)}, u32[]{:S(2)}, u32[]{:S(2)}) collective-permute-start(bf16[4,272,256]{2,1,0:T(8,128)(2,1)S(1)} %shard_map.126.refs_10_.refs_0_.refs_2_), channel_id=1, source_target_pairs={{0,1},{1,0},{2,3},{3,2},{4,5},{5,4},{6,7},{7,6},{8,9},{9,8},{10,11... | collective-permute-start | bytes 1671176 | tf_op jit(solution)/shard_map/ppermute | solution.py:232
  496.2 36.5 %collective-permute-start.70 = (bf16[4,272,256]{2,1,0:T(8,128)(2,1)S(1)}, bf16[4,272,256]{2,1,0:T(8,128)(2,1)S(1)}, u32[]{:S(2)}, u32[]{:S(2)}) collective-permute-start(bf16[4,272,256]{2,1,0:T(8,128)(2,1)S(1)} %shard_map.126.refs_10_.refs_0_.refs_2_), channel_id=1, source_target_pairs={{0,2},{1,3},{2,0},{3,1},{4,6},{5,7},{6,4},{7,5},{8,10},{9,11},{10,... | collective-permute-start | bytes 1671176 | tf_op jit(solution)/shard_map/ppermute | solution.py:232
  496.9 35.7 %collective-permute-start.71 = (bf16[4,272,256]{2,1,0:T(8,128)(2,1)S(1)}, bf16[4,272,256]{2,1,0:T(8,128)(2,1)S(1)}, u32[]{:S(2)}, u32[]{:S(2)}) collective-permute-start(bf16[4,272,256]{2,1,0:T(8,128)(2,1)S(1)} %shard_map.126.refs_10_.refs_0_.refs_2_), channel_id=1, source_target_pairs={{0,3},{1,2},{2,1},{3,0},{4,7},{5,6},{6,5},{7,4},{8,11},{9,10},{10,... | collective-permute-start | bytes 1671176 | tf_op jit(solution)/shard_map/ppermute | solution.py:232
  (157 other events, 2518.4 us)
